TPU v7x, 512 devices: a whole 4x4x16 slice. The times are simulated.
512 devices in a mesh: blk: 8 (over y_lo, x), rows: 64 (over z, y_hi, core).
Axes of the slice: x: 4, y: 4 (y_hi: 2, y_lo: 2; y = y_hi * 2 + y_lo), z: 16, core: 2. Of those that a mesh axis runs over, the one named last changes fastest.
Arguments:
- queries: bfloat16 [128, 4, 8192], P('rows', None, 'blk'), may hold values from -36 to 36
- new_entries: bfloat16 [128, 4, 2, 1024], P('rows', None, None, 'blk'), may hold values from -9 to 9
- resident: bfloat16 [4096, 2, 16, 1024], P('rows', None, None, 'blk'), may hold values from -9 to 9
- swap_area: bfloat16 [4096, 2, 16, 1024], P('rows', None, None, 'blk'), may hold values from -9 to 9
- swap_dest: int32 [4096], P('rows'), may hold values from 0 to 63, as said below
- page_table: int32 [128, 64], P('rows'), may hold values from 0 to 191, as said below
- lengths: int32 [128], P('rows'), may hold values from 256 to 1024, as said below
- norm_gain: bfloat16 [8192], P('blk'), may hold values from 0.099609375 to 1.8984375
- gate_weight: bfloat16 [8192, 28672], P('blk', 'rows'), may hold values from -0.0625 to 0.0625
- up_weight: bfloat16 [8192, 28672], P('blk', 'rows'), may hold values from -0.0625 to 0.0625
- down_weight: bfloat16 [28672, 8192], P('rows', 'blk'), may hold values from -0.03125 to 0.03125
Outputs:
- attended: bfloat16 [128, 4, 8192], P('rows', None, 'blk')
- layer_out: bfloat16 [128, 4, 8192], P('rows', None, 'blk')
Inputs may be any that keep to these rules, and one draw needn't show every extreme that they name: `swap_dest`: every owner sends exactly 2 of its pages to each of 32 different owners (possibly itself), and every owner receives exactly 64 pages. `page_table`: the entries of the 2 rows of one owner name each of its 64 resident pages and each of the 64 pages that land there exactly once; an entry at or above 64 is 64 + s * 2 + k for the k-th page, in the order of the sender's pages, that owner s sends to the row's owner. `lengths`: some row has exactly 1024 cached positions.
All inputs are finite; a program needn't handle non-finite values.
Results may differ from a plain program's by a relative error of at most 0.0086.
Values may be sent and summed in bfloat16 or wider, within the bound.
No kernel may reach another device: no remote copies, remote signals or barrier semaphores. Data moves between devices by JAX's collectives and lax.ppermute only.
A program may use at most 64 MiB of HBM per device.

v0:
```python
import math

import jax
import jax.numpy as jnp
from jax import lax
from jax.sharding import PartitionSpec as P

GQ = 8
HD = 128
PAGE = 16
CAP = 2


epsilon = 1e-05


def on_device(
    queries,
    new_entries,
    resident,
    swap_area,
    swap_dest,
    page_table,
    lengths,
    norm_gain,
    gate_weight,
    up_weight,
    down_weight,
):
    owners = lax.axis_size("rows")
    swap_count = swap_area.shape[0]
    page_width = swap_area.shape[1] * swap_area.shape[2] * swap_area.shape[3]
    flat_swap = swap_area.reshape(swap_count, page_width)
    target = swap_dest[:, None] == jnp.arange(owners, dtype=jnp.int32)[None, :]
    before = jnp.cumsum(target.astype(jnp.int32), axis=0) - 1
    page_rank = jnp.sum(jnp.where(target, before, 0), axis=1)
    send_slot = swap_dest * CAP + page_rank
    placement = (jnp.arange(owners * CAP, dtype=jnp.int32)[:, None] == send_slot[None, :]).astype(
        jnp.bfloat16
    )
    outgoing = jnp.dot(placement, flat_swap, preferred_element_type=jnp.float32).astype(
        jnp.bfloat16
    )
    outgoing = outgoing.reshape(owners, CAP, page_width)
    arrived = lax.all_to_all(outgoing, "rows", split_axis=0, concat_axis=0, tiled=True)
    page_store = jnp.concatenate(
        [resident.reshape(-1, page_width), arrived.reshape(owners * CAP, page_width)], axis=0
    )
    fetched = page_store[page_table]
    rows_here, pages_row = page_table.shape
    step_count = queries.shape[1]
    kv_heads = new_entries.shape[-1] // HD
    fetched = fetched.reshape(rows_here, pages_row, 2, PAGE, kv_heads, HD)
    cached_keys = fetched[:, :, 0].reshape(rows_here, pages_row * PAGE, kv_heads, HD)
    cached_values = fetched[:, :, 1].reshape(rows_here, pages_row * PAGE, kv_heads, HD)
    head_queries = queries.reshape(rows_here, step_count, kv_heads, GQ, HD)
    step_entries = new_entries.reshape(rows_here, step_count, 2, kv_heads, HD)
    score_scale = 1.0 / math.sqrt(HD)
    cached_scores = (
        jnp.einsum(
            "rskgd,rlkd->rkgsl", head_queries, cached_keys, preferred_element_type=jnp.float32
        )
        * score_scale
    )
    new_scores = (
        jnp.einsum(
            "rskgd,rtkd->rkgst",
            head_queries,
            step_entries[:, :, 0],
            preferred_element_type=jnp.float32,
        )
        * score_scale
    )
    visible = jnp.arange(pages_row * PAGE, dtype=jnp.int32)[None, :] < lengths[:, None]
    causal = jnp.arange(step_count)[None, :] <= jnp.arange(step_count)[:, None]
    cached_scores = jnp.where(visible[:, None, None, None, :], cached_scores, -1e30)
    new_scores = jnp.where(causal[None, None, None], new_scores, -1e30)
    row_peak = jnp.maximum(jnp.max(cached_scores, axis=-1), jnp.max(new_scores, axis=-1))[..., None]
    cached_exp = jnp.exp(cached_scores - row_peak)
    new_exp = jnp.exp(new_scores - row_peak)
    row_total = (jnp.sum(cached_exp, axis=-1) + jnp.sum(new_exp, axis=-1))[..., None]
    cached_weights = (cached_exp / row_total).astype(jnp.bfloat16)
    new_weights = (new_exp / row_total).astype(jnp.bfloat16)
    mixed_heads = jnp.einsum(
        "rkgsl,rlkd->rskgd", cached_weights, cached_values, preferred_element_type=jnp.float32
    )
    mixed_heads = mixed_heads + jnp.einsum(
        "rkgst,rtkd->rskgd", new_weights, step_entries[:, :, 1], preferred_element_type=jnp.float32
    )
    attended = mixed_heads.reshape(rows_here, step_count, -1).astype(jnp.bfloat16)
    local_tokens = attended.reshape(rows_here * step_count, -1)
    gathered = lax.all_gather(local_tokens, "rows", axis=0, tiled=True)
    gathered_wide = gathered.astype(jnp.float32)
    squares = jnp.sum(gathered_wide * gathered_wide, axis=1)
    normed = (gathered_wide * norm_gain.astype(jnp.float32)[None, :]).astype(jnp.bfloat16)
    gate_part = jnp.dot(normed, gate_weight, preferred_element_type=jnp.float32)
    up_part = jnp.dot(normed, up_weight, preferred_element_type=jnp.float32)
    width_total = gathered.shape[1] * lax.axis_size("blk")
    gate_sum, up_sum, square_sum = lax.psum((gate_part, up_part, squares), "blk")
    factor = lax.rsqrt(square_sum / width_total + epsilon)[:, None]
    hidden = (jax.nn.silu(factor * gate_sum) * (factor * up_sum)).astype(jnp.bfloat16)
    down_sum = lax.psum_scatter(
        jnp.dot(hidden, down_weight, preferred_element_type=jnp.float32),
        "rows",
        scatter_dimension=0,
        tiled=True,
    )
    layer_out = (local_tokens.astype(jnp.float32) + down_sum).astype(jnp.bfloat16)
    return (attended, layer_out.reshape(rows_here, step_count, -1))


def solution(mesh):
    placed = (
        P("rows", None, "blk"),
        P("rows", None, None, "blk"),
        P("rows", None, None, "blk"),
        P("rows", None, None, "blk"),
        P("rows"),
        P("rows", None),
        P("rows"),
        P("blk"),
        P("blk", "rows"),
        P("blk", "rows"),
        P("rows", "blk"),
    )
    return jax.shard_map(
        on_device,
        mesh=mesh,
        in_specs=placed,
        out_specs=(P("rows", None, "blk"), P("rows", None, "blk")),
        check_vma=False,
    )
```

profile of v0, /device:TPU:2, one launch (start us, length us, event | category | flops | bytes accessed | tf_op | source)
XLA Modules:
  0.0 548.7 jit_solution(16742943073197080970)
XLA Ops:
  7.2 0.0 copy-start
  7.2 0.8 fusion.23
  8.0 0.1 reduce_window_sum.11
  8.1 0.8 select_reduce_fusion
  8.9 0.7 multiply_add_fusion
  9.6 1.5 convolution_convert_fusion
  11.1 0.0 copy-start.11
  11.1 0.0 copy-start.7
  11.1 0.0 copy-start.5
  11.1 0.0 copy-start.2
  11.1 1.5 reshape.143
  12.6 18.9 %all-to-all-start = ((bf16[64,2,4096]{2,1,0:T(2,128)(2,1)}), bf16[64,2,4096]{2,1,0:T(2,128)(2,1)S(1)}, u32[]{:S(2)}, u32[]{:S(2)}) async-start(bf16[64,2,4096]{2,1,0:T(2,128)(2,1)} %reshape.143), calls=%async_computation | async-start | bytes 2097152 | tf_op jit(solution)/shard_map/all_to_all | solution.py:45
  31.5 0.0 all-gather.2.cloned.1.call-start
  31.6 0.1 reshape.157
  31.7 1.0 copy.35
  32.7 0.6 pad_clamp_fusion
  33.3 0.7 iota_compare_fusion.3
  34.0 1.4 fusion.30
  35.4 52.2 %all-to-all-done = bf16[64,2,4096]{2,1,0:T(2,128)(2,1)S(1)} async-done(((bf16[64,2,4096]{2,1,0:T(2,128)(2,1)}), bf16[64,2,4096]{2,1,0:T(2,128)(2,1)S(1)}, u32[]{:S(2)}, u32[]{:S(2)}) %all-to-all-start) | async-done | bytes 1048608 | tf_op jit(solution)/shard_map/all_to_all | solution.py:45
  87.6 0.4 reshape.144
  88.1 1.2 pad_maximum_fusion
  89.3 1.3 gather_fusion
  90.6 0.0 copy-start.4
  90.6 0.2 copy.24
  90.9 0.0 copy-start.13
  90.9 0.2 fusion.28
  91.1 0.2 copy-done.3
  91.3 0.4 fusion.29
  91.7 0.2 fusion.18
  91.9 0.3 fusion.19
  92.2 0.2 fusion.6
  92.4 0.6 copy.36
  93.0 0.0 all-gather.2.cloned.1.call-update
  93.0 0.0 all-reduce.3.cloned.1.call-start
  93.1 130.8 %all-gather.2.cloned.1.call-done = bf16[512,1024]{1,0:T(8,128)(2,1)} async-done(((bf16[8,1024]{1,0:T(8,128)(2,1)}), bf16[512,1024]{1,0:T(8,128)(2,1)}) %all-gather.2.cloned.1.call-update) | async-done | bytes 1048592 | tf_op jit(solution)/shard_map/all_gather | solution.py:92
  223.9 3.0 fusion.9
  226.9 2.8 fusion.11
  229.7 0.0 all-reduce.3.cloned.1.call-update
  229.7 0.0 reduce-scatter.2.cloned.1.call-start
  229.7 0.3 fusion
  230.0 16.5 %psum.21 = f32[512]{0:T(512)S(1)} all-reduce(f32[512]{0:T(512)S(1)} %fusion), channel_id=1, replica_groups=mesh['blk'=8,'rows'=64] {'blk'}, use_global_device_ids=true, to_apply=%region_7.8 | all-reduce | flops 512 | bytes 4096 | tf_op jit(solution)/shard_map/psum | solution.py:99
  246.5 74.4 %all-reduce.3.cloned.1.call-done = (f32[512,448]{0,1:T(8,128)}, f32[512,448]{0,1:T(8,128)}) async-done(((f32[512,448]{0,1:T(8,128)}, f32[512,448]{0,1:T(8,128)}), (f32[512,448]{0,1:T(8,128)}, f32[512,448]{0,1:T(8,128)})) %all-reduce.3.cloned.1.call-update) | async-done | bytes 1835024 | tf_op jit(solution)/shard_map/psum | solution.py:99
  321.0 3.6 fusion.15
  324.6 0.0 reduce-scatter.2.cloned.1.call-update
  324.6 0.6 convert_element_type.56
  325.2 215.6 %reduce-scatter.2.cloned.1.call-done = f32[8,1024]{1,0:T(8,128)} async-done(((f32[512,1024]{1,0:T(8,128)}), f32[8,1024]{1,0:T(8,128)}) %reduce-scatter.2.cloned.1.call-update) | async-done | bytes 32784 | tf_op jit(solution)/shard_map/reduce_scatter | solution.py:102
  540.8 0.8 add_convert_fusion
  541.6 0.6 reshape.154
  (29 shorter events, 0.1 us)
Async XLA Ops:
  7.2 313.8 %copy-start = (bf16[448,1024]{1,0:T(8,128)(2,1)S(1)}, bf16[448,1024]{1,0:T(8,128)(2,1)}, u32[]{:S(2)}) copy-start(bf16[448,1024]{1,0:T(8,128)(2,1)} %param.21) | copy-start | bytes 2752516
  11.1 20.5 %copy-start.11 = (s32[2,64]{1,0:T(2,128)S(1)}, s32[2,64]{1,0:T(2,128)}, u32[]{:S(2)}) copy-start(s32[2,64]{1,0:T(2,128)} %param.16) | copy-start | bytes 1540
  11.1 20.6 %copy-start.7 = (bf16[2,4,2,128]{3,2,1,0:T(2,128)(2,1)S(1)}, bf16[2,4,2,128]{3,2,1,0:T(2,128)(2,1)}, u32[]{:S(2)}) copy-start(bf16[2,4,2,128]{3,2,1,0:T(2,128)(2,1)} %param.12) | copy-start | bytes 12292
  11.1 20.6 %copy-start.5 = (bf16[2,4,1024]{2,1,0:T(4,128)(2,1)S(1)}, bf16[2,4,1024]{2,1,0:T(4,128)(2,1)}, u32[]{:S(2)}) copy-start(bf16[2,4,1024]{2,1,0:T(4,128)(2,1)} %param.11) | copy-start | bytes 49156
  11.1 20.6 %copy-start.2 = (bf16[64,2,16,128]{3,2,1,0:T(8,128)(2,1)S(1)}, bf16[64,2,16,128]{3,2,1,0:T(8,128)(2,1)}, u32[]{:S(2)}) copy-start(bf16[64,2,16,128]{3,2,1,0:T(8,128)(2,1)} %param.13) | copy-start | bytes 1572868
  12.6 20.7 %copy-start.12 = (s32[2]{0:T(128)S(1)}, s32[2]{0:T(128)}, u32[]{:S(2)}) copy-start(s32[2]{0:T(128)} %param.17) | copy-start | bytes 28
  12.6 75.0 %all-to-all-start = ((bf16[64,2,4096]{2,1,0:T(2,128)(2,1)}), bf16[64,2,4096]{2,1,0:T(2,128)(2,1)S(1)}, u32[]{:S(2)}, u32[]{:S(2)}) async-start(bf16[64,2,4096]{2,1,0:T(2,128)(2,1)} %reshape.143), calls=%async_computation | async-start | bytes 2097152 | tf_op jit(solution)/shard_map/all_to_all | solution.py:45
  31.5 192.4 %all-gather.2.cloned.1.call-start = ((), (), s32[]{:S(2)}) async-start(), calls=%async_computation.2 | async-start | bytes 1064960 | tf_op jit(solution)/shard_map/all_gather | solution.py:92
  31.7 3.7 copy-start.8
  90.6 0.7 copy-start.3
  90.6 1.0 copy-start.6
  90.6 1.0 copy-start.4
  90.9 1.3 copy-start.9
  90.9 2.2 copy-start.10
  90.9 133.0 %copy-start.13 = (bf16[1024,448]{0,1:T(8,128)(2,1)S(1)}, bf16[1024,448]{0,1:T(8,128)(2,1)}, u32[]{:S(2)}) copy-start(bf16[1024,448]{0,1:T(8,128)(2,1)} %param.20) | copy-start | bytes 2752516
  93.0 228.0 %all-reduce.3.cloned.1.call-start = ((), (), s32[]{:S(2)}) async-start(), calls=%async_computation.4 | async-start | bytes 3670016 | tf_op jit(solution)/shard_map/psum | solution.py:99
  223.9 3.0 copy-start.1
  229.7 311.1 %reduce-scatter.2.cloned.1.call-start = ((), (), s32[]{:S(2)}) async-start(), calls=%async_computation.3 | async-start | bytes 2129920 | tf_op jit(solution)/shard_map/reduce_scatter | solution.py:102
Sparse Core Ops, SparseCore 0:
  93.1 130.7 all-gather.1
  229.8 91.1 all-reduce.2
  325.6 215.1 reduce-scatter.1
where the time goes:
time: 549 us
  waiting for transfers between devices  473 us (86%)
  starting transfers between devices  19 us (3%)
  blocking collectives  16.5 us (3%)
  between operations  14 us (3%)
  matrix products  13.1 us (2%)
  local copies, waits for them, and re-layouts  6.88 us (1%)
  other arithmetic  6.15 us (1%)
    reduce_scatter x1, waiting for transfers between devices, on_device(): lax.psum_scatter(jnp.dot(hidden, down_weight, preferred_element_type=jnp....  216 us
    all_gather x1, waiting for transfers between devices, on_device(): gathered = lax.all_gather(local_tokens, 'rows', axis=0, tiled=True)  131 us
    psum x1, waiting for transfers between devices, on_device(): lax.psum((gate_part, up_part, squares), 'blk')  74.4 us
    all_to_all x1, waiting for transfers between devices, on_device(): lax.all_to_all(outgoing, 'rows', split_axis=0, concat_axis=0, tiled=True)  52.2 us
    all_to_all x1, starting transfers between devices, on_device(): lax.all_to_all(outgoing, 'rows', split_axis=0, concat_axis=0, tiled=True)  18.9 us
    psum x1, blocking collectives, on_device(): lax.psum((gate_part, up_part, squares), 'blk')  16.5 us
  transfers between devices with their start and end apart: 4, of which 4 were waited for; matrix products, arithmetic and copies ran while one was open for 1% of the time, Pallas kernels for 0%

commit v1 on v0

--- a/solution.py
+++ b/solution.py
@@ -3,6 +3,7 @@
 import jax
 import jax.numpy as jnp
 from jax import lax
+from jax.sharding import Mesh
 from jax.sharding import PartitionSpec as P
 
 GQ = 8
@@ -10,24 +11,30 @@
 PAGE = 16
 CAP = 2
 
+AXES = ("ylo", "x", "zhi", "zlo", "yhi", "core")
+SIZES = (2, 4, 4, 4, 2, 2)
+BLK = ("ylo", "x")
+ROWS = ("zhi", "zlo", "yhi", "core")
+FAR = ("zhi", "yhi")
+SWAP = [(0, 1), (1, 0)]
 
 epsilon = 1e-05
 
 
-def on_device(
-    queries,
-    new_entries,
-    resident,
-    swap_area,
-    swap_dest,
-    page_table,
-    lengths,
-    norm_gain,
-    gate_weight,
-    up_weight,
-    down_weight,
-):
-    owners = lax.axis_size("rows")
+def spread(part, axes):
+    count = lax.axis_size(axes)
+    copies = jnp.broadcast_to(part[None], (count,) + part.shape)
+    arrived = lax.all_to_all(copies, axes, split_axis=0, concat_axis=0, tiled=True)
+    return arrived.reshape((count * part.shape[0],) + part.shape[1:])
+
+
+def collect(parts, axes):
+    arrived = lax.all_to_all(parts, axes, split_axis=0, concat_axis=0, tiled=True)
+    return jnp.sum(arrived.astype(jnp.float32), axis=0)
+
+
+def attention(queries, new_entries, resident, swap_area, swap_dest, page_table, lengths):
+    owners = lax.axis_size(ROWS)
     swap_count = swap_area.shape[0]
     page_width = swap_area.shape[1] * swap_area.shape[2] * swap_area.shape[3]
     flat_swap = swap_area.reshape(swap_count, page_width)
@@ -42,7 +49,7 @@
         jnp.bfloat16
     )
     outgoing = outgoing.reshape(owners, CAP, page_width)
-    arrived = lax.all_to_all(outgoing, "rows", split_axis=0, concat_axis=0, tiled=True)
+    arrived = lax.all_to_all(outgoing, ROWS, split_axis=0, concat_axis=0, tiled=True)
     page_store = jnp.concatenate(
         [resident.reshape(-1, page_width), arrived.reshape(owners * CAP, page_width)], axis=0
     )
@@ -87,46 +94,105 @@
     mixed_heads = mixed_heads + jnp.einsum(
         "rkgst,rtkd->rskgd", new_weights, step_entries[:, :, 1], preferred_element_type=jnp.float32
     )
-    attended = mixed_heads.reshape(rows_here, step_count, -1).astype(jnp.bfloat16)
-    local_tokens = attended.reshape(rows_here * step_count, -1)
-    gathered = lax.all_gather(local_tokens, "rows", axis=0, tiled=True)
-    gathered_wide = gathered.astype(jnp.float32)
-    squares = jnp.sum(gathered_wide * gathered_wide, axis=1)
-    normed = (gathered_wide * norm_gain.astype(jnp.float32)[None, :]).astype(jnp.bfloat16)
+    return mixed_heads.reshape(rows_here, step_count, -1).astype(jnp.bfloat16)
+
+
+def gated_parts(tokens, norm_gain, gate_weight, up_weight):
+    wide = tokens.astype(jnp.float32)
+    squares = jnp.sum(wide * wide, axis=1, keepdims=True)
+    squares_high = squares.astype(jnp.bfloat16)
+    squares_low = (squares - squares_high.astype(jnp.float32)).astype(jnp.bfloat16)
+    normed = (wide * norm_gain.astype(jnp.float32)[None, :]).astype(jnp.bfloat16)
     gate_part = jnp.dot(normed, gate_weight, preferred_element_type=jnp.float32)
     up_part = jnp.dot(normed, up_weight, preferred_element_type=jnp.float32)
-    width_total = gathered.shape[1] * lax.axis_size("blk")
-    gate_sum, up_sum, square_sum = lax.psum((gate_part, up_part, squares), "blk")
-    factor = lax.rsqrt(square_sum / width_total + epsilon)[:, None]
+    count, units = gate_part.shape
+    gap = jnp.zeros((count, 512 - units - 2), jnp.bfloat16)
+    tail = jnp.zeros((count, 512 - units), jnp.bfloat16)
+    return jnp.concatenate(
+        [
+            gate_part.astype(jnp.bfloat16),
+            squares_high,
+            squares_low,
+            gap,
+            up_part.astype(jnp.bfloat16),
+            tail,
+        ],
+        axis=1,
+    )
+
+
+def mlp(attended, norm_gain, gate_weight, up_weight, down_weight):
+    rows_here, step_count, width = attended.shape
+    local_tokens = attended.reshape(rows_here * step_count, width)
+    far = lax.axis_size(FAR)
+    near = lax.axis_size("zlo")
+    blk = lax.axis_size(BLK)
+    units = gate_weight.shape[1]
+    own = spread(spread(local_tokens, FAR), "zlo")
+    other = lax.ppermute(own, "core", SWAP)
+    half = own.shape[0]
+    parts = jnp.concatenate(
+        [
+            gated_parts(own, norm_gain, gate_weight, up_weight),
+            gated_parts(other, norm_gain, gate_weight, up_weight),
+        ],
+        axis=0,
+    )
+    summed = collect(parts.reshape(blk, 2 * half // blk, 1024), BLK)
+    gate_sum = summed[:, :units]
+    up_sum = summed[:, 512 : 512 + units]
+    square_sum = summed[:, units : units + 1] + summed[:, units + 1 : units + 2]
+    factor = lax.rsqrt(square_sum / (width * blk) + epsilon)
     hidden = (jax.nn.silu(factor * gate_sum) * (factor * up_sum)).astype(jnp.bfloat16)
-    down_sum = lax.psum_scatter(
-        jnp.dot(hidden, down_weight, preferred_element_type=jnp.float32),
-        "rows",
-        scatter_dimension=0,
-        tiled=True,
+    hidden = spread(hidden, BLK)
+    away = jnp.dot(hidden[half:], down_weight, preferred_element_type=jnp.float32)
+    received = lax.ppermute(away.astype(jnp.bfloat16), "core", SWAP)
+    kept = jnp.dot(hidden[:half], down_weight, preferred_element_type=jnp.float32)
+    kept = (kept + received.astype(jnp.float32)).astype(jnp.bfloat16)
+    kept = collect(kept.reshape(near, half // near, width), "zlo").astype(jnp.bfloat16)
+    down_sum = collect(kept.reshape(far, half // near // far, width), FAR)
+    layer_out = (local_tokens.astype(jnp.float32) + down_sum).astype(jnp.bfloat16)
+    return layer_out.reshape(rows_here, step_count, width)
+
+
+def on_device(
+    queries,
+    new_entries,
+    resident,
+    swap_area,
+    swap_dest,
+    page_table,
+    lengths,
+    norm_gain,
+    gate_weight,
+    up_weight,
+    down_weight,
+):
+    attended = attention(
+        queries, new_entries, resident, swap_area, swap_dest, page_table, lengths
     )
-    layer_out = (local_tokens.astype(jnp.float32) + down_sum).astype(jnp.bfloat16)
-    return (attended, layer_out.reshape(rows_here, step_count, -1))
+    return attended, mlp(attended, norm_gain, gate_weight, up_weight, down_weight)
 
 
 def solution(mesh):
+    fine = Mesh(mesh.devices.reshape(SIZES), AXES)
     placed = (
-        P("rows", None, "blk"),
-        P("rows", None, None, "blk"),
-        P("rows", None, None, "blk"),
-        P("rows", None, None, "blk"),
-        P("rows"),
-        P("rows", None),
-        P("rows"),
-        P("blk"),
-        P("blk", "rows"),
-        P("blk", "rows"),
-        P("rows", "blk"),
+        P(ROWS, None, BLK),
+        P(ROWS, None, None, BLK),
+        P(ROWS, None, None, BLK),
+        P(ROWS, None, None, BLK),
+        P(ROWS),
+        P(ROWS, None),
+        P(ROWS),
+        P(BLK),
+        P(BLK, ROWS),
+        P(BLK, ROWS),
+        P(ROWS, BLK),
     )
     return jax.shard_map(
         on_device,
-        mesh=mesh,
+        mesh=fine,
         in_specs=placed,
-        out_specs=(P("rows", None, "blk"), P("rows", None, "blk")),
+        out_specs=(P(ROWS, None, BLK), P(ROWS, None, BLK)),
         check_vma=False,
     )

time: 549 us -> 212 us (0.39)
  waiting for transfers between devices: 473 us -> 82.9 us
  blocking collectives: 16.5 us -> 70.2 us
  starting transfers between devices: 19 us -> 32.2 us
  between operations: 14 us -> 1.03 us
    reduce_scatter x1 -> x0, waiting for transfers between devices: 216 us -> none  [on_device(): lax.psum_scatter(jnp.dot(hidden, down_weight, preferred_element_type=jnp....]
    all_gather x1 -> x0, waiting for transfers between devices: 131 us -> none  [on_device(): gathered = lax.all_gather(local_tokens, 'rows', axis=0, tiled=True)]
    psum x1 -> x0, waiting for transfers between devices: 74.4 us -> none  [on_device(): lax.psum((gate_part, up_part, squares), 'blk')]
    all_to_all x0 -> x4, blocking collectives: none -> 70.2 us  [the longest x2 37.4 us: collect(): lax.all_to_all(parts, axes, split_axis=0, concat_axis=0, tiled=True)]
    all_to_all x1 -> x3, waiting for transfers between devices: 52.2 us -> 81.1 us  [the longest x1 52.3 us: attention(): lax.all_to_all(outgoing, ROWS, split_axis=0, concat_axis=0, tiled=True)]
    psum x1 -> x0, blocking collectives: 16.5 us -> none  [on_device(): lax.psum((gate_part, up_part, squares), 'blk')]
    all_to_all x1 -> x3, starting transfers between devices: 18.9 us -> 28.4 us  [the longest x1 18.9 us: attention(): lax.all_to_all(outgoing, ROWS, split_axis=0, concat_axis=0, tiled=True)]
    dot_general x8 -> x11, matrix products: 13.1 us -> 9.93 us  [the longest x2 3.31 us: gated_parts(): up_part = jnp.dot(normed, up_weight, preferred_element_type=jnp.float32)]
  transfers between devices with their start and end apart: 4 -> 5, of which waited for: 4 -> 4; matrix products, arithmetic and copies ran while one was open for 1% -> 4% of each run, Pallas kernels for 0% -> 0%
where the time goes in v1:
time: 212 us; the launch traced here: 211 us
  waiting for transfers between devices  82.9 us (39%)
  blocking collectives  70.2 us (33%)
  starting transfers between devices  32.2 us (15%)
  matrix products  9.93 us (5%)
  local copies, waits for them, and re-layouts  7.67 us (4%)
  other arithmetic  7.42 us (4%)
    all_to_all x1, waiting for transfers between devices, attention(): lax.all_to_all(outgoing, ROWS, split_axis=0, concat_axis=0, tiled=True)  52.3 us
    all_to_all x2, blocking collectives, collect(): lax.all_to_all(parts, axes, split_axis=0, concat_axis=0, tiled=True)  37.4 us
    all_to_all x2, blocking collectives, spread(): lax.all_to_all(copies, axes, split_axis=0, concat_axis=0, tiled=True)  32.8 us
    all_to_all x1, starting transfers between devices, attention(): lax.all_to_all(outgoing, ROWS, split_axis=0, concat_axis=0, tiled=True)  18.9 us
    all_to_all x1, waiting for transfers between devices, collect(): lax.all_to_all(parts, axes, split_axis=0, concat_axis=0, tiled=True)  15.2 us
    all_to_all x1, waiting for transfers between devices, spread(): lax.all_to_all(copies, axes, split_axis=0, concat_axis=0, tiled=True)  13.5 us
    all_to_all x1, starting transfers between devices, collect(): lax.all_to_all(parts, axes, split_axis=0, concat_axis=0, tiled=True)  5.82 us
  transfers between devices with their start and end apart: 5, of which 4 were waited for; matrix products, arithmetic and copies ran while one was open for 4% of the time, Pallas kernels for 0%

profile of v1, /device:TPU:2, one launch (start us, length us, event | category | flops | bytes accessed | tf_op | source)
XLA Modules:
  0.0 211.5 jit_solution(13472306222196751379)
XLA Ops:
  0.6 0.8 fusion.24
  1.5 0.8 select_reduce_fusion
  2.4 0.7 multiply_add_fusion
  3.1 1.5 convolution_convert_fusion
  4.5 1.5 reshape.224
  6.1 18.9 %all-to-all-start = ((bf16[64,2,4096]{2,1,0:T(2,128)(2,1)}), bf16[64,2,4096]{2,1,0:T(2,128)(2,1)S(1)}, u32[]{:S(2)}, u32[]{:S(2)}) async-start(bf16[64,2,4096]{2,1,0:T(2,128)(2,1)} %reshape.224), calls=%async_computation | async-start | bytes 2097152 | tf_op jit(solution)/shard_map/all_to_all | solution.py:52
  25.0 1.0 copy.51
  26.1 0.6 pad_clamp_fusion
  26.7 0.7 iota_compare_fusion.3
  27.4 1.4 fusion.31
  28.8 52.3 %all-to-all-done = bf16[64,2,4096]{2,1,0:T(2,128)(2,1)S(1)} async-done(((bf16[64,2,4096]{2,1,0:T(2,128)(2,1)}), bf16[64,2,4096]{2,1,0:T(2,128)(2,1)S(1)}, u32[]{:S(2)}, u32[]{:S(2)}) %all-to-all-start) | async-done | bytes 1048608 | tf_op jit(solution)/shard_map/all_to_all | solution.py:52
  81.1 0.4 reshape.225
  81.5 1.2 pad_maximum_fusion
  82.7 1.3 gather_fusion
  84.0 0.2 copy.42
  84.3 0.2 fusion.28
  84.5 0.5 copy-done.3
  85.0 0.4 fusion.30
  85.4 0.2 fusion.13
  85.6 0.3 fusion.16
  85.9 0.2 fusion.4
  86.1 20.2 %all_to_all.35 = bf16[8,8,1024]{2,1,0:T(8,128)(2,1)S(1)} all-to-all(bf16[8,8,1024]{2,1,0:T(8,128)(2,1)S(1)} %broadcast_in_dim.44), channel_id=1, replica_groups=mesh['ylo'=2,'x'=4,'zhi'=4,'zlo'=4,'yhi'=2,'core'=2] {'zhi','yhi'}, dimensions={0} | all-to-all | bytes 262144 | tf_op jit(solution)/shard_map/all_to_all | solution.py:27
  106.3 0.9 broadcast_in_dim.73
  107.1 3.7 %all-to-all-start.2 = ((bf16[4,64,1024]{2,1,0:T(8,128)(2,1)}), bf16[4,64,1024]{2,1,0:T(8,128)(2,1)S(1)}, u32[]{:S(2)}, u32[]{:S(2)}) async-start(bf16[4,64,1024]{2,1,0:T(8,128)(2,1)} %broadcast_in_dim.73), calls=%async_computation.2 | async-start | bytes 1048576 | tf_op jit(solution)/shard_map/all_to_all | solution.py:27
  110.8 13.5 %all-to-all-done.2 = bf16[4,64,1024]{2,1,0:T(8,128)(2,1)S(1)} async-done(((bf16[4,64,1024]{2,1,0:T(8,128)(2,1)}), bf16[4,64,1024]{2,1,0:T(8,128)(2,1)S(1)}, u32[]{:S(2)}, u32[]{:S(2)}) %all-to-all-start.2) | async-done | bytes 524320 | tf_op jit(solution)/shard_map/all_to_all | solution.py:27
  124.4 0.2 multiply_reduce_fusion
  124.7 1.9 collective-permute-start
  126.6 1.6 convolution_convert_fusion.4
  128.2 1.6 convolution_convert_fusion.5
  129.9 0.4 concatenate.13
  130.3 0.2 fusion.8
  130.5 1.7 convolution_convert_fusion.2
  132.2 0.4 convolution_convert_fusion.3
  132.6 0.4 concatenate.14
  133.1 0.5 copy.33
  133.6 19.9 %all_to_all.36 = bf16[8,64,1024]{2,1,0:T(8,128)(2,1)S(1)} all-to-all(bf16[8,64,1024]{2,1,0:T(8,128)(2,1)S(1)} %bitcast.108), channel_id=1, replica_groups=mesh['ylo'=2,'x'=4,'zhi'=4,'zlo'=4,'yhi'=2,'core'=2] {'ylo','x'}, dimensions={0} | all-to-all | bytes 2097152 | tf_op jit(solution)/shard_map/all_to_all | solution.py:32
  153.5 0.2 convert_reduce_fusion
  153.7 0.2 fusion.22
  154.1 12.7 %all_to_all.37 = bf16[8,64,448]{2,1,0:T(8,128)(2,1)S(1)} all-to-all(bf16[8,64,448]{2,1,0:T(8,128)(2,1)S(1)} %broadcast_in_dim.74), channel_id=1, replica_groups=mesh['ylo'=2,'x'=4,'zhi'=4,'zlo'=4,'yhi'=2,'core'=2] {'ylo','x'}, dimensions={0} | all-to-all | bytes 917504 | tf_op jit(solution)/shard_map/all_to_all | solution.py:27
  166.8 0.4 convolution_convert_fusion.1
  167.3 1.9 collective-permute-start.1
  169.2 1.9 collective-permute-done.1
  171.1 0.4 add_convert_fusion
  171.5 17.5 %all_to_all.38 = bf16[4,64,1024]{2,1,0:T(8,128)(2,1)S(1)} all-to-all(bf16[4,64,1024]{2,1,0:T(8,128)(2,1)S(1)} %bitcast.109), channel_id=1, replica_groups=mesh['ylo'=2,'x'=4,'zhi'=4,'zlo'=4,'yhi'=2,'core'=2] {'zlo'}, dimensions={0} | all-to-all | bytes 1048576 | tf_op jit(solution)/shard_map/all_to_all | solution.py:32
  189.0 0.7 reduce_sum.89
  189.7 5.8 %all-to-all-start.6 = ((bf16[8,8,1024]{2,1,0:T(8,128)(2,1)}), bf16[8,8,1024]{2,1,0:T(8,128)(2,1)S(1)}, u32[]{:S(2)}, u32[]{:S(2)}) async-start(bf16[8,8,1024]{2,1,0:T(8,128)(2,1)} %bitcast.30), calls=%async_computation.6 | async-start | bytes 262144 | tf_op jit(solution)/shard_map/all_to_all | solution.py:32
  195.6 15.2 %all-to-all-done.6 = bf16[8,8,1024]{2,1,0:T(8,128)(2,1)S(1)} async-done(((bf16[8,8,1024]{2,1,0:T(8,128)(2,1)}), bf16[8,8,1024]{2,1,0:T(8,128)(2,1)S(1)}, u32[]{:S(2)}, u32[]{:S(2)}) %all-to-all-start.6) | async-done | bytes 131104 | tf_op jit(solution)/shard_map/all_to_all | solution.py:32
  210.8 0.6 add_convert_fusion.1
  (53 shorter events, 0.8 us)
Async XLA Ops:
  0.6 166.2 %copy-start = (bf16[448,1024]{1,0:T(8,128)(2,1)S(1)}, bf16[448,1024]{1,0:T(8,128)(2,1)}, u32[]{:S(2)}) copy-start(bf16[448,1024]{1,0:T(8,128)(2,1)} %param.21) | copy-start | bytes 2752516
  6.0 18.9 %copy-start.1 = (bf16[64,2,16,128]{3,2,1,0:T(8,128)(2,1)S(1)}, bf16[64,2,16,128]{3,2,1,0:T(8,128)(2,1)}, u32[]{:S(2)}) copy-start(bf16[64,2,16,128]{3,2,1,0:T(8,128)(2,1)} %param.13) | copy-start | bytes 1572868
  6.0 20.0 %copy-start.11 = (s32[2,64]{1,0:T(2,128)S(1)}, s32[2,64]{1,0:T(2,128)}, u32[]{:S(2)}) copy-start(s32[2,64]{1,0:T(2,128)} %param.16) | copy-start | bytes 1540
  6.0 20.0 %copy-start.5 = (bf16[2,4,1024]{2,1,0:T(4,128)(2,1)S(1)}, bf16[2,4,1024]{2,1,0:T(4,128)(2,1)}, u32[]{:S(2)}) copy-start(bf16[2,4,1024]{2,1,0:T(4,128)(2,1)} %param.11) | copy-start | bytes 49156
  6.0 20.1 %copy-start.7 = (bf16[2,4,2,128]{3,2,1,0:T(2,128)(2,1)S(1)}, bf16[2,4,2,128]{3,2,1,0:T(2,128)(2,1)}, u32[]{:S(2)}) copy-start(bf16[2,4,2,128]{3,2,1,0:T(2,128)(2,1)} %param.12) | copy-start | bytes 12292
  6.1 20.7 %copy-start.12 = (s32[2]{0:T(128)S(1)}, s32[2]{0:T(128)}, u32[]{:S(2)}) copy-start(s32[2]{0:T(128)} %param.17) | copy-start | bytes 28
  6.1 75.0 %all-to-all-start = ((bf16[64,2,4096]{2,1,0:T(2,128)(2,1)}), bf16[64,2,4096]{2,1,0:T(2,128)(2,1)S(1)}, u32[]{:S(2)}, u32[]{:S(2)}) async-start(bf16[64,2,4096]{2,1,0:T(2,128)(2,1)} %reshape.224), calls=%async_computation | async-start | bytes 2097152 | tf_op jit(solution)/shard_map/all_to_all | solution.py:52
  26.1 55.4 %copy-start.8 = (bf16[2,4,2,128]{3,1,0,2:T(4,128)(2,1)}, bf16[2,4,2,128]{3,1,0,2:T(4,128)(2,1)S(1)}, u32[]{:S(2)}) copy-start(bf16[2,4,2,128]{3,1,0,2:T(4,128)(2,1)S(1)} %copy.53) | copy-start | bytes 12292
  84.3 0.7 copy-start.3
  84.3 1.0 copy-start.6
  84.3 1.0 copy-start.4
  84.5 1.4 copy-start.9
  85.6 25.2 %copy-start.10 = (bf16[1024]{0:T(1024)(128)(2,1)S(1)}, bf16[1024]{0:T(1024)(128)(2,1)}, u32[]{:S(2)}) copy-start(bf16[1024]{0:T(1024)(128)(2,1)} %param.18) | copy-start | bytes 6148
  107.1 17.2 %all-to-all-start.2 = ((bf16[4,64,1024]{2,1,0:T(8,128)(2,1)}), bf16[4,64,1024]{2,1,0:T(8,128)(2,1)S(1)}, u32[]{:S(2)}, u32[]{:S(2)}) async-start(bf16[4,64,1024]{2,1,0:T(8,128)(2,1)} %broadcast_in_dim.73), calls=%async_computation.2 | async-start | bytes 1048576 | tf_op jit(solution)/shard_map/all_to_all | solution.py:27
  124.7 5.6 %collective-permute-start = (bf16[256,1024]{1,0:T(8,128)(2,1)S(1)}, bf16[256,1024]{1,0:T(8,128)(2,1)S(1)}, u32[]{:S(2)}, u32[]{:S(2)}) collective-permute-start(bf16[256,1024]{1,0:T(8,128)(2,1)S(1)} %bitcast.110), channel_id=1, source_target_pairs={{0,1},{1,0},{2,3},{3,2},{4,5},{5,4},{6,7},{7,6},{8,9},{9,8},{10,11... | collective-permute-start | bytes 1572872 | tf_op jit(solution)/shard_map/ppermute | solution.py:132
  130.2 1.9 copy-start.13
  167.3 3.8 %collective-permute-start.1 = (bf16[256,1024]{1,0:T(8,128)(2,1)S(1)}, bf16[256,1024]{1,0:T(8,128)(2,1)S(1)}, u32[]{:S(2)}, u32[]{:S(2)}) collective-permute-start(bf16[256,1024]{1,0:T(8,128)(2,1)S(1)} %convolution_convert_fusion.1), channel_id=1, source_target_pairs={{0,1},{1,0},{2,3},{3,2},{4,5},{5,4},{6,7},{7,6},{8,9},{9,8},{10,11... | collective-permute-start | bytes 1572872 | tf_op jit(solution)/shard_map/ppermute | solution.py:149
  189.7 21.1 %all-to-all-start.6 = ((bf16[8,8,1024]{2,1,0:T(8,128)(2,1)}), bf16[8,8,1024]{2,1,0:T(8,128)(2,1)S(1)}, u32[]{:S(2)}, u32[]{:S(2)}) async-start(bf16[8,8,1024]{2,1,0:T(8,128)(2,1)} %bitcast.30), calls=%async_computation.6 | async-start | bytes 262144 | tf_op jit(solution)/shard_map/all_to_all | solution.py:32
  195.6 15.9 %copy-start.2 = (bf16[2,4,1024]{2,1,0:T(4,128)(2,1)}, bf16[2,4,1024]{2,1,0:T(4,128)(2,1)S(1)}, u32[]{:S(2)}) copy-start(bf16[2,4,1024]{2,1,0:T(4,128)(2,1)S(1)} %convert_element_type.176) | copy-start | bytes 49156

commit v2 on v1

v2 whole, which is shorter than its diff:
```python
import math

import jax
import jax.numpy as jnp
from jax import lax
from jax.experimental import pallas as pl
from jax.experimental.pallas import tpu as pltpu
from jax.sharding import Mesh
from jax.sharding import PartitionSpec as P

GQ = 8
HD = 128
PAGE = 16
CAP = 2

AXES = ("ylo", "x", "zhi", "zlo", "yhi", "core")
SIZES = (2, 4, 4, 4, 2, 2)
BLK = ("ylo", "x")
ROWS = ("zhi", "zlo", "yhi", "core")
NEAR = ("zlo", "yhi", "core")
MID = ("zlo", "yhi")
SWAP = [(0, 1), (1, 0)]

epsilon = 1e-05


def spread(part, axes):
    count = lax.axis_size(axes)
    copies = jnp.broadcast_to(part[None], (count,) + part.shape)
    arrived = lax.all_to_all(copies, axes, split_axis=0, concat_axis=0, tiled=True)
    return arrived.reshape((count * part.shape[0],) + part.shape[1:])


def collect(parts, axes):
    arrived = lax.all_to_all(parts, axes, split_axis=0, concat_axis=0, tiled=True)
    return jnp.sum(arrived.astype(jnp.float32), axis=0)


def stack_heads(wide):
    count = wide.shape[1] // HD
    return jnp.concatenate([wide[:, g * HD : (g + 1) * HD] for g in range(count)], axis=0)


def attend_kernel(far_ref, *refs):
    pages_ref, resident_ref, new_ref, seen_ref, out_ref = refs[-5:]
    asked_refs = refs[:-5]
    far = far_ref[0]
    owners = len(asked_refs)
    tokens, columns = asked_refs[0].shape
    width = columns - HD
    heads = width // HD
    queries = heads * tokens
    score_scale = 1.0 / math.sqrt(HD)
    token = lax.broadcasted_iota(jnp.int32, (queries, 1), 0) & (tokens - 1)
    step_count = tokens // 2
    sign = jnp.where(token < step_count, 1.0, -1.0)

    def scores(asked, keys):
        return score_scale * lax.dot_general(
            asked, keys, (((1,), (1,)), ((), ())), preferred_element_type=jnp.float32
        )

    def mix(weight, values):
        high = weight.astype(jnp.bfloat16)
        low = (weight - high.astype(jnp.float32)).astype(jnp.bfloat16)
        return jnp.dot(high, values, preferred_element_type=jnp.float32) + jnp.dot(
            low, values, preferred_element_type=jnp.float32
        )

    def page_mask(seen):
        offset = lax.broadcasted_iota(jnp.int32, seen.shape, 1) & (PAGE - 1)
        return sign * seen > offset.astype(jnp.float32)

    def heads_of(index):
        return stack_heads(asked_refs[index][:, :width].astype(jnp.float32)).astype(jnp.bfloat16)

    asked = heads_of(0)
    pages = resident_ref.shape[0]
    keys = resident_ref[:, 0].reshape(pages * PAGE, HD)
    values = resident_ref[:, 1].reshape(pages * PAGE, HD)
    mask = page_mask(seen_ref[...])
    score = jnp.where(mask, scores(asked, keys), -1e30)
    fresh = scores(asked, new_ref[0])
    other = lax.broadcasted_iota(jnp.int32, (1, fresh.shape[1]), 1)
    start = jnp.where(token < step_count, 0, step_count)
    fresh_mask = (other >= start) & (other <= token)
    fresh = jnp.where(fresh_mask, fresh, -1e30)
    own_peak = jnp.maximum(
        jnp.max(score, axis=1, keepdims=True), jnp.max(fresh, axis=1, keepdims=True)
    )
    weight = jnp.exp(score - own_peak)
    fresh_weight = jnp.exp(fresh - own_peak)
    own_total = jnp.sum(weight, axis=1, keepdims=True) + jnp.sum(
        fresh_weight, axis=1, keepdims=True
    )
    own_mixed = mix(weight, values) + mix(fresh_weight, new_ref[1])

    senders, landed = pages_ref.shape[0], pages_ref.shape[1]
    slots = landed // owners
    key_count = senders * slots * PAGE
    place = lax.broadcasted_iota(jnp.int32, (HD, key_count), 1) // PAGE + far * (senders * slots)
    expand = (lax.broadcasted_iota(jnp.int32, (HD, key_count), 0) == place).astype(jnp.float32)
    lane = lax.broadcasted_iota(jnp.int32, (tokens, HD), 1)
    for back in range(owners):
        owner = (far - back) & (owners - 1)
        table = asked_refs[back][:, width:]
        seen = jnp.dot(table, expand.astype(jnp.bfloat16), preferred_element_type=jnp.float32)[0:1]
        asked = heads_of(back)
        mine = pages_ref[:, pl.ds(owner * slots, slots)]
        keys = mine[:, :, 0].reshape(key_count, HD)
        values = mine[:, :, 1].reshape(key_count, HD)
        mask = page_mask(seen)
        score = jnp.where(mask, scores(asked, keys), -1e30)
        peak = jnp.max(score, axis=1, keepdims=True)
        weight = jnp.where(mask, jnp.exp(score - peak), 0.0)
        total = jnp.sum(weight, axis=1, keepdims=True)
        mixed = mix(weight, values)
        top = jnp.maximum(peak, own_peak) if back == 0 else peak
        top = top.astype(jnp.bfloat16).astype(jnp.float32)
        here = jnp.where(total > 0.0, jnp.exp(jnp.minimum(peak - top, 80.0)), 0.0)
        total = here * total
        mixed = here * mixed
        if back == 0:
            own = jnp.exp(jnp.minimum(own_peak - top, 80.0))
            total = total + own * own_total
            mixed = mixed + own * own_mixed
        mixed = mixed / jnp.where(total > 0.0, total, 1.0)
        total_high = total.astype(jnp.bfloat16).astype(jnp.float32)
        total_low = total - total_high
        stats = jnp.zeros((tokens, HD), jnp.float32)
        for g in range(heads):
            rows = slice(g * tokens, (g + 1) * tokens)
            stats = jnp.where(lane == g, top[rows], stats)
            stats = jnp.where(lane == heads + g, total_high[rows], stats)
            stats = jnp.where(lane == 2 * heads + g, total_low[rows], stats)
        line = jnp.concatenate(
            [mixed[g * tokens : (g + 1) * tokens] for g in range(heads)] + [stats], axis=1
        ).astype(jnp.bfloat16)
        for copy in range(out_ref.shape[0]):
            out_ref[copy, owner] = line


def merge_kernel(far_ref, parts_ref, copies_ref, attended_ref):
    sources, owners, tokens, columns = parts_ref.shape
    width = columns - HD
    heads = width // HD
    count = owners * tokens
    parts = [parts_ref[i].reshape(count, columns) for i in range(sources)]
    stats = [part[:, width:].astype(jnp.float32) for part in parts]
    peaks = [stat[:, :heads] for stat in stats]
    totals = [stat[:, heads : 2 * heads] + stat[:, 2 * heads : 3 * heads] for stat in stats]
    top = peaks[0]
    for peak in peaks[1:]:
        top = jnp.maximum(top, peak)
    shares = [total * jnp.exp(peak - top) for peak, total in zip(peaks, totals)]
    whole = shares[0]
    for share in shares[1:]:
        whole = whole + share
    shares = [share / whole for share in shares]
    blocks = []
    for g in range(heads):
        block = jnp.zeros((count, HD), jnp.float32)
        for part, share in zip(parts, shares):
            block = block + share[:, g : g + 1] * part[:, g * HD : (g + 1) * HD].astype(jnp.float32)
        blocks.append(block)
    merged = jnp.concatenate(blocks, axis=1)
    line = merged.astype(jnp.bfloat16)
    for copy in range(copies_ref.shape[0]):
        copies_ref[copy] = line
    own = merged[:tokens]
    for owner in range(1, owners):
        own = jnp.where(far_ref[0] == owner, merged[owner * tokens : (owner + 1) * tokens], own)
    attended_ref[...] = own.astype(jnp.bfloat16)


def attention(queries, new_entries, resident, swap_area, swap_dest, page_table, lengths):
    owners = lax.axis_size(ROWS)
    far_count = lax.axis_size("zhi")
    near_count = lax.axis_size(NEAR)
    mid_count = lax.axis_size(MID)
    far = lax.axis_index("zhi").astype(jnp.int32).reshape(1)
    rows_here, step_count, width = queries.shape
    tokens = rows_here * step_count
    pages_row = page_table.shape[1]
    pages_here = resident.shape[0]

    first = jnp.arange(pages_row, dtype=jnp.int32)[None, :] * PAGE
    seen = jnp.clip(lengths[:, None] - first, 0, PAGE) * jnp.array([[1], [-1]], jnp.int32)
    entries = jnp.arange(pages_here + owners * CAP, dtype=jnp.int32)
    named = page_table[:, :, None] == entries[None, None, :]
    seen = jnp.sum(jnp.where(named, seen[:, :, None], 0), axis=(0, 1)).astype(jnp.float32)
    table = jnp.pad(seen[None, pages_here:].astype(jnp.bfloat16), ((0, tokens - 1), (0, 0)))
    asked = jnp.concatenate([queries.reshape(tokens, width), table], axis=1)
    asked = [asked] + [
        lax.ppermute(asked, "zhi", [(i, (i + back) % far_count) for i in range(far_count)])
        for back in range(1, far_count)
    ]
    seen_here = jnp.repeat(seen[:pages_here], PAGE)[None, :]

    swap_count = swap_area.shape[0]
    page_width = swap_area.shape[1] * swap_area.shape[2] * swap_area.shape[3]
    same = swap_dest[:, None] == swap_dest[None, :]
    earlier = jnp.arange(swap_count)[None, :] < jnp.arange(swap_count)[:, None]
    page_rank = jnp.sum((same & earlier).astype(jnp.int32), axis=1)
    send_slot = (swap_dest % near_count) * (far_count * CAP) + (
        swap_dest // near_count
    ) * CAP + page_rank
    placement = (jnp.arange(owners * CAP, dtype=jnp.int32)[:, None] == send_slot[None, :]).astype(
        jnp.bfloat16
    )
    outgoing = jnp.dot(
        placement, swap_area.reshape(swap_count, page_width), preferred_element_type=jnp.float32
    ).astype(jnp.bfloat16)
    outgoing = outgoing.reshape((near_count, far_count * CAP) + swap_area.shape[1:])
    landed = lax.all_to_all(outgoing, NEAR, split_axis=0, concat_axis=0, tiled=True)

    fresh = new_entries.reshape(tokens, 2, HD).transpose(1, 0, 2)
    fresh = jnp.pad(fresh, ((0, 0), (0, HD - tokens), (0, 0)))
    whole = pl.BlockSpec(memory_space=pltpu.VMEM)
    scalar = pl.BlockSpec(memory_space=pltpu.SMEM)
    parts = pl.pallas_call(
        attend_kernel,
        out_shape=jax.ShapeDtypeStruct((far_count, far_count, tokens, width + HD), jnp.bfloat16),
        in_specs=[scalar] + [whole] * (far_count + 4),
        out_specs=whole,
    )(far, *asked, landed, resident, fresh, seen_here)
    parts = lax.all_to_all(parts, "zhi", split_axis=0, concat_axis=0, tiled=True)
    copies, attended = pl.pallas_call(
        merge_kernel,
        out_shape=(
            jax.ShapeDtypeStruct((mid_count, far_count * tokens, width), jnp.bfloat16),
            jax.ShapeDtypeStruct((tokens, width), jnp.bfloat16),
        ),
        in_specs=[scalar, whole],
        out_specs=(whole, whole),
    )(far, parts)
    return copies, attended


def gated_parts(tokens, norm_gain, gate_weight, up_weight):
    wide = tokens.astype(jnp.float32)
    squares = jnp.sum(wide * wide, axis=1, keepdims=True)
    squares_high = squares.astype(jnp.bfloat16)
    squares_low = (squares - squares_high.astype(jnp.float32)).astype(jnp.bfloat16)
    normed = (wide * norm_gain.astype(jnp.float32)[None, :]).astype(jnp.bfloat16)
    gate_part = jnp.dot(normed, gate_weight, preferred_element_type=jnp.float32)
    up_part = jnp.dot(normed, up_weight, preferred_element_type=jnp.float32)
    count, units = gate_part.shape
    gap = jnp.zeros((count, 512 - units - 2), jnp.bfloat16)
    tail = jnp.zeros((count, 512 - units), jnp.bfloat16)
    return jnp.concatenate(
        [
            gate_part.astype(jnp.bfloat16),
            squares_high,
            squares_low,
            gap,
            up_part.astype(jnp.bfloat16),
            tail,
        ],
        axis=1,
    )


def mlp(copies, attended, norm_gain, gate_weight, up_weight, down_weight):
    tokens_here, width = attended.shape
    far = lax.axis_size("zhi")
    mid = lax.axis_size(MID)
    blk = lax.axis_size(BLK)
    units = gate_weight.shape[1]
    own = lax.all_to_all(copies, MID, split_axis=0, concat_axis=0, tiled=True).reshape(-1, width)
    other = lax.ppermute(own, "core", SWAP)
    half = own.shape[0]
    parts = jnp.concatenate(
        [
            gated_parts(own, norm_gain, gate_weight, up_weight),
            gated_parts(other, norm_gain, gate_weight, up_weight),
        ],
        axis=0,
    )
    summed = collect(parts.reshape(blk, 2 * half // blk, 1024), BLK)
    gate_sum = summed[:, :units]
    up_sum = summed[:, 512 : 512 + units]
    square_sum = summed[:, units : units + 1] + summed[:, units + 1 : units + 2]
    factor = lax.rsqrt(square_sum / (width * blk) + epsilon)
    hidden = (jax.nn.silu(factor * gate_sum) * (factor * up_sum)).astype(jnp.bfloat16)
    hidden = spread(hidden, BLK)
    away = jnp.dot(hidden[half:], down_weight, preferred_element_type=jnp.float32)
    received = lax.ppermute(away.astype(jnp.bfloat16), "core", SWAP)
    kept = jnp.dot(hidden[:half], down_weight, preferred_element_type=jnp.float32)
    kept = (kept + received.astype(jnp.float32)).astype(jnp.bfloat16)
    kept = collect(kept.reshape(mid, far * tokens_here, width), MID).astype(jnp.bfloat16)
    down_sum = collect(kept.reshape(far, tokens_here, width), "zhi")
    return (attended.astype(jnp.float32) + down_sum).astype(jnp.bfloat16)


def on_device(
    queries,
    new_entries,
    resident,
    swap_area,
    swap_dest,
    page_table,
    lengths,
    norm_gain,
    gate_weight,
    up_weight,
    down_weight,
):
    copies, attended = attention(
        queries, new_entries, resident, swap_area, swap_dest, page_table, lengths
    )
    layer_out = mlp(copies, attended, norm_gain, gate_weight, up_weight, down_weight)
    return attended.reshape(queries.shape), layer_out.reshape(queries.shape)


def solution(mesh):
    fine = Mesh(mesh.devices.reshape(SIZES), AXES)
    placed = (
        P(ROWS, None, BLK),
        P(ROWS, None, None, BLK),
        P(ROWS, None, None, BLK),
        P(ROWS, None, None, BLK),
        P(ROWS),
        P(ROWS, None),
        P(ROWS),
        P(BLK),
        P(BLK, ROWS),
        P(BLK, ROWS),
        P(ROWS, BLK),
    )
    return jax.shard_map(
        on_device,
        mesh=fine,
        in_specs=placed,
        out_specs=(P(ROWS, None, BLK), P(ROWS, None, BLK)),
        check_vma=False,
    )
```

time: 212 us -> 191 us (0.901)
  the two profiles are of different devices: /device:TPU:2 before, /device:TPU:32 now
where the time goes in v2:
time: 191 us; the launch traced here: 190 us
  blocking collectives  82.4 us (43%)
  starting transfers between devices  44.4 us (23%)
  waiting for transfers between devices  39.5 us (21%)
  matrix products  6.66 us (3%)
  local copies, waits for them, and re-layouts  6.37 us (3%)
  Pallas kernels  6.15 us (3%)
  other arithmetic  3.47 us (2%)
    all_to_all x2, blocking collectives, collect(): lax.all_to_all(parts, axes, split_axis=0, concat_axis=0, tiled=True)  41.3 us
    all_to_all x1, blocking collectives, attention(): lax.all_to_all(parts, 'zhi', split_axis=0, concat_axis=0, tiled=True)  28.5 us
    ppermute x3, starting transfers between devices, attention(): lax.ppermute(asked, 'zhi', [(i, (i + back) % far_count) for i in range(fa...  22.5 us
    all_to_all x1, waiting for transfers between devices, mlp(): lax.all_to_all(copies, MID, split_axis=0, concat_axis=0, tiled=True)  14.5 us
    all_to_all x1, waiting for transfers between devices, collect(): lax.all_to_all(parts, axes, split_axis=0, concat_axis=0, tiled=True)  12.7 us
    all_to_all x1, blocking collectives, spread(): lax.all_to_all(copies, axes, split_axis=0, concat_axis=0, tiled=True)  12.6 us
    ppermute x3, waiting for transfers between devices, attention(): lax.ppermute(asked, 'zhi', [(i, (i + back) % far_count) for i in range(fa...  10.4 us
    all_to_all x1, starting transfers between devices, attention(): lax.all_to_all(outgoing, NEAR, split_axis=0, concat_axis=0, tiled=True)  9.08 us
  transfers between devices with their start and end apart: 8, of which 4 were waited for; matrix products, arithmetic and copies ran while one was open for 3% of the time, Pallas kernels for 0%

profile of v2, /device:TPU:32, one launch (start us, length us, event | category | flops | bytes accessed | tf_op | source)
XLA Modules:
  0.0 190.0 jit_solution(16121136745597886234)
XLA Ops:
  0.6 0.9 convert_reduce_fusion.2
  1.6 0.7 fusion.19
  2.3 1.5 fusion
  3.7 1.2 copy.26
  5.0 9.1 %all-to-all-start = ((bf16[16,8,2,16,128]{4,3,2,1,0:T(8,128)(2,1)}), bf16[16,8,2,16,128]{4,3,2,1,0:T(8,128)(2,1)S(1)}, u32[]{:S(2)}, u32[]{:S(2)}) async-start(bf16[16,8,2,16,128]{4,3,2,1,0:T(8,128)(2,1)} %bitcast.17), calls=%async_computation | async-start | bytes 2097152 | tf_op jit(solution)/shard_map/all_to_all | solution.py:215
  14.1 0.1 clamp_multiply_fusion
  14.2 0.1 select_reduce_fusion
  14.3 0.1 slice_bitcast_fusion
  14.4 8.8 %collective-permute-start = (bf16[8,1152]{1,0:T(8,128)(2,1)S(1)}, bf16[8,1152]{1,0:T(8,128)(2,1)S(1)}, u32[]{:S(2)}, u32[]{:S(2)}) collective-permute-start(bf16[8,1152]{1,0:T(8,128)(2,1)S(1)} %fusion.16.refs_0_), channel_id=1, source_target_pairs={{0,16},{16,32},{32,48},{48,0},{1,17},{17,33},{33,49},{49,1},{2,18}... | collective-permute-start | bytes 55304 | tf_op jit(solution)/shard_map/ppermute | solution.py:195
  23.2 8.2 %collective-permute-start.1 = (bf16[8,1152]{1,0:T(8,128)(2,1)S(1)}, bf16[8,1152]{1,0:T(8,128)(2,1)S(1)}, u32[]{:S(2)}, u32[]{:S(2)}) collective-permute-start(bf16[8,1152]{1,0:T(8,128)(2,1)S(1)} %fusion.16.refs_0_), channel_id=1, source_target_pairs={{0,32},{16,48},{32,0},{48,16},{1,33},{17,49},{33,1},{49,17},{2,34}... | collective-permute-start | bytes 55304 | tf_op jit(solution)/shard_map/ppermute | solution.py:195
  31.4 5.5 %collective-permute-start.2 = (bf16[8,1152]{1,0:T(8,128)(2,1)S(1)}, bf16[8,1152]{1,0:T(8,128)(2,1)S(1)}, u32[]{:S(2)}, u32[]{:S(2)}) collective-permute-start(bf16[8,1152]{1,0:T(8,128)(2,1)S(1)} %fusion.16.refs_0_), channel_id=1, source_target_pairs={{0,48},{16,0},{32,16},{48,32},{1,49},{17,1},{33,17},{49,33},{2,50}... | collective-permute-start | bytes 55304 | tf_op jit(solution)/shard_map/ppermute | solution.py:195
  37.0 0.7 broadcast_in_dim_reshape.3.refs_7_
  37.7 0.6 pad.9.refs_6_
  38.3 10.4 %collective-permute-done.refs_1_ = bf16[8,1152]{1,0:T(8,128)(2,1)S(1)} collective-permute-done((bf16[8,1152]{1,0:T(8,128)(2,1)S(1)}, bf16[8,1152]{1,0:T(8,128)(2,1)S(1)}, u32[]{:S(2)}, u32[]{:S(2)}) %collective-permute-start) | collective-permute-done | bytes 18464 | tf_op jit(solution)/shard_map/ppermute | solution.py:195
  48.8 0.5 copy-done.4
  49.4 0.4 copy-done.1
  49.8 4.1 %shard_map.134 = bf16[4,4,8,1152]{3,2,1,0:T(8,128)(2,1)} custom-call(s32[1]{0:T(128)} %bitcast.far_ref, bf16[8,1152]{1,0:T(8,128)(2,1)} %copy-done.2, bf16[8,1152]{1,0:T(8,128)(2,1)} %copy-done.4, bf16[8,1152]{1,0:T(8,128)(2,1)} %copy-done.5, bf16[8,1152]{1,0:T(8,128)(2,1)} %copy-done.6, bf16[16,8,2,16,128]{4,3,2,1,0:T(8,128)(2,1)} %copy-done.1, ...), custom_call_target="tpu_custom_call" | custom-call | tf_op jit(solution)/shard_map/pallas_call | solution.py:221
  53.8 28.5 %all_to_all.35.parts_ref = bf16[4,4,8,1152]{3,2,1,0:T(8,128)(2,1)} all-to-all(bf16[4,4,8,1152]{3,2,1,0:T(8,128)(2,1)} %shard_map.134), channel_id=1, replica_groups=mesh['ylo'=2,'x'=4,'zhi'=4,'zlo'=4,'yhi'=2,'core'=2] {'zhi'}, dimensions={0} | all-to-all | bytes 589824 | tf_op jit(solution)/shard_map/all_to_all | solution.py:227
  82.3 2.1 %shard_map.135 = (bf16[8,32,1024]{2,1,0:T(8,128)(2,1)}, bf16[8,1024]{1,0:T(8,128)(2,1)}) custom-call(s32[1]{0:T(128)} %bitcast.far_ref, bf16[4,4,8,1152]{3,2,1,0:T(8,128)(2,1)} %all_to_all.35.parts_ref), custom_call_target="tpu_custom_call" | custom-call | tf_op jit(solution)/shard_map/pallas_call | solution.py:228
  84.4 5.8 %all-to-all-start.2 = ((bf16[8,32,1024]{2,1,0:T(8,128)(2,1)}), bf16[8,32,1024]{2,1,0:T(8,128)(2,1)S(1)}, u32[]{:S(2)}, u32[]{:S(2)}) async-start(bf16[8,32,1024]{2,1,0:T(8,128)(2,1)} %get-tuple-element.5), calls=%async_computation.2 | async-start | bytes 1048576 | tf_op jit(solution)/shard_map/all_to_all | solution.py:270
  90.2 14.5 %all-to-all-done.2 = bf16[8,32,1024]{2,1,0:T(8,128)(2,1)S(1)} async-done(((bf16[8,32,1024]{2,1,0:T(8,128)(2,1)}), bf16[8,32,1024]{2,1,0:T(8,128)(2,1)S(1)}, u32[]{:S(2)}, u32[]{:S(2)}) %all-to-all-start.2) | async-done | bytes 524320 | tf_op jit(solution)/shard_map/all_to_all | solution.py:270
  104.7 1.9 %collective-permute-start.3 = (bf16[256,1024]{1,0:T(8,128)(2,1)S(1)}, bf16[256,1024]{1,0:T(8,128)(2,1)S(1)}, u32[]{:S(2)}, u32[]{:S(2)}) collective-permute-start(bf16[256,1024]{1,0:T(8,128)(2,1)S(1)} %bitcast.32), channel_id=1, source_target_pairs={{0,1},{1,0},{2,3},{3,2},{4,5},{5,4},{6,7},{7,6},{8,9},{9,8},{10,11... | collective-permute-start | bytes 1572872 | tf_op jit(solution)/shard_map/ppermute | solution.py:271
  106.6 0.2 multiply_reduce_fusion
  106.8 0.1 reduce_sum.73
  106.9 1.7 convolution_convert_fusion.5
  108.6 0.4 convolution_convert_fusion.4
  109.1 0.4 concatenate.13
  109.5 0.2 fusion.2
  109.7 1.7 convolution_convert_fusion.3
  111.4 0.4 convolution_convert_fusion.2
  111.8 0.4 concatenate.14
  112.2 0.1 pad_maximum_fusion
  112.3 0.5 copy.24
  112.9 20.6 %all_to_all.36 = bf16[8,64,1024]{2,1,0:T(8,128)(2,1)S(1)} all-to-all(bf16[8,64,1024]{2,1,0:T(8,128)(2,1)S(1)} %bitcast.30), channel_id=1, replica_groups=mesh['ylo'=2,'x'=4,'zhi'=4,'zlo'=4,'yhi'=2,'core'=2] {'ylo','x'}, dimensions={0} | all-to-all | bytes 2097152 | tf_op jit(solution)/shard_map/all_to_all | solution.py:35
  133.4 0.2 convert_reduce_fusion
  133.6 0.2 fusion.13
  133.8 0.1 fusion.8
  134.0 12.6 %all_to_all.37 = bf16[8,64,448]{2,1,0:T(8,128)(2,1)S(1)} all-to-all(bf16[8,64,448]{2,1,0:T(8,128)(2,1)S(1)} %broadcast_in_dim.19), channel_id=1, replica_groups=mesh['ylo'=2,'x'=4,'zhi'=4,'zlo'=4,'yhi'=2,'core'=2] {'ylo','x'}, dimensions={0} | all-to-all | bytes 917504 | tf_op jit(solution)/shard_map/all_to_all | solution.py:30
  146.7 0.4 convolution_convert_fusion.1
  147.1 1.9 %collective-permute-start.4 = (bf16[256,1024]{1,0:T(8,128)(2,1)S(1)}, bf16[256,1024]{1,0:T(8,128)(2,1)S(1)}, u32[]{:S(2)}, u32[]{:S(2)}) collective-permute-start(bf16[256,1024]{1,0:T(8,128)(2,1)S(1)} %convolution_convert_fusion.1), channel_id=1, source_target_pairs={{0,1},{1,0},{2,3},{3,2},{4,5},{5,4},{6,7},{7,6},{8,9},{9,8},{10,11... | collective-permute-start | bytes 1572872 | tf_op jit(solution)/shard_map/ppermute | solution.py:288
  149.0 1.9 collective-permute-done.4
  150.9 0.4 add_convert_fusion
  151.4 20.7 %all_to_all.38 = bf16[8,32,1024]{2,1,0:T(8,128)(2,1)S(1)} all-to-all(bf16[8,32,1024]{2,1,0:T(8,128)(2,1)S(1)} %bitcast.31), channel_id=1, replica_groups=mesh['ylo'=2,'x'=4,'zhi'=4,'zlo'=4,'yhi'=2,'core'=2] {'zlo','yhi'}, dimensions={0} | all-to-all | bytes 1048576 | tf_op jit(solution)/shard_map/all_to_all | solution.py:35
  172.1 0.7 reduce_sum.77
  172.8 3.3 %all-to-all-start.6 = ((bf16[4,8,1024]{2,1,0:T(8,128)(2,1)}), bf16[4,8,1024]{2,1,0:T(8,128)(2,1)S(1)}, u32[]{:S(2)}, u32[]{:S(2)}) async-start(bf16[4,8,1024]{2,1,0:T(8,128)(2,1)} %bitcast.10), calls=%async_computation.6 | async-start | bytes 131072 | tf_op jit(solution)/shard_map/all_to_all | solution.py:35
  176.1 0.6 reshape.163
  176.7 12.7 %all-to-all-done.6 = bf16[4,8,1024]{2,1,0:T(8,128)(2,1)S(1)} async-done(((bf16[4,8,1024]{2,1,0:T(8,128)(2,1)}), bf16[4,8,1024]{2,1,0:T(8,128)(2,1)S(1)}, u32[]{:S(2)}, u32[]{:S(2)}) %all-to-all-start.6) | async-done | bytes 65568 | tf_op jit(solution)/shard_map/all_to_all | solution.py:35
  189.4 0.6 reshape.168
  (49 shorter events, 0.3 us)
Async XLA Ops:
  0.6 146.0 %copy-start = (bf16[448,1024]{1,0:T(8,128)(2,1)S(1)}, bf16[448,1024]{1,0:T(8,128)(2,1)}, u32[]{:S(2)}) copy-start(bf16[448,1024]{1,0:T(8,128)(2,1)} %param.22) | copy-start | bytes 2752516
  4.9 9.1 %copy-start.7 = (bf16[2,4,1024]{2,1,0:T(4,128)(2,1)S(1)}, bf16[2,4,1024]{2,1,0:T(4,128)(2,1)}, u32[]{:S(2)}) copy-start(bf16[2,4,1024]{2,1,0:T(4,128)(2,1)} %param.12) | copy-start | bytes 49156
  4.9 9.1 %copy-start.11 = (s32[2]{0:T(128)S(1)}, s32[2]{0:T(128)}, u32[]{:S(2)}) copy-start(s32[2]{0:T(128)} %param.18) | copy-start | bytes 28
  4.9 9.1 %copy-start.12 = (s32[2]{0:T(128)S(1)}, s32[2]{0:T(128)}, u32[]{:S(2)}) copy-start(s32[2]{0:T(128)} %constant.66) | copy-start | bytes 28
  4.9 9.2 %copy-start.10 = (s32[2,64]{1,0:T(2,128)S(1)}, s32[2,64]{1,0:T(2,128)}, u32[]{:S(2)}) copy-start(s32[2,64]{1,0:T(2,128)} %param.17) | copy-start | bytes 1540
  4.9 31.9 %copy-start.8 = (bf16[2,4,2,128]{3,2,1,0:T(2,128)(2,1)S(1)}, bf16[2,4,2,128]{3,2,1,0:T(2,128)(2,1)}, u32[]{:S(2)}) copy-start(bf16[2,4,2,128]{3,2,1,0:T(2,128)(2,1)} %param.13) | copy-start | bytes 12292
  5.0 43.8 %all-to-all-start = ((bf16[16,8,2,16,128]{4,3,2,1,0:T(8,128)(2,1)}), bf16[16,8,2,16,128]{4,3,2,1,0:T(8,128)(2,1)S(1)}, u32[]{:S(2)}, u32[]{:S(2)}) async-start(bf16[16,8,2,16,128]{4,3,2,1,0:T(8,128)(2,1)} %bitcast.17), calls=%async_computation | async-start | bytes 2097152 | tf_op jit(solution)/shard_map/all_to_all | solution.py:215
  14.4 34.4 %copy-start.2 = (bf16[8,1152]{1,0:T(8,128)(2,1)}, bf16[8,1152]{1,0:T(8,128)(2,1)S(1)}, u32[]{:S(2)}) copy-start(bf16[8,1152]{1,0:T(8,128)(2,1)S(1)} %fusion.16.refs_0_) | copy-start | bytes 55300
  14.4 34.4 %collective-permute-start = (bf16[8,1152]{1,0:T(8,128)(2,1)S(1)}, bf16[8,1152]{1,0:T(8,128)(2,1)S(1)}, u32[]{:S(2)}, u32[]{:S(2)}) collective-permute-start(bf16[8,1152]{1,0:T(8,128)(2,1)S(1)} %fusion.16.refs_0_), channel_id=1, source_target_pairs={{0,16},{16,32},{32,48},{48,0},{1,17},{17,33},{33,49},{49,1},{2,18}... | collective-permute-start | bytes 55304 | tf_op jit(solution)/shard_map/ppermute | solution.py:195
  23.2 25.6 %collective-permute-start.1 = (bf16[8,1152]{1,0:T(8,128)(2,1)S(1)}, bf16[8,1152]{1,0:T(8,128)(2,1)S(1)}, u32[]{:S(2)}, u32[]{:S(2)}) collective-permute-start(bf16[8,1152]{1,0:T(8,128)(2,1)S(1)} %fusion.16.refs_0_), channel_id=1, source_target_pairs={{0,32},{16,48},{32,0},{48,16},{1,33},{17,49},{33,1},{49,17},{2,34}... | collective-permute-start | bytes 55304 | tf_op jit(solution)/shard_map/ppermute | solution.py:195
  31.4 17.4 %collective-permute-start.2 = (bf16[8,1152]{1,0:T(8,128)(2,1)S(1)}, bf16[8,1152]{1,0:T(8,128)(2,1)S(1)}, u32[]{:S(2)}, u32[]{:S(2)}) collective-permute-start(bf16[8,1152]{1,0:T(8,128)(2,1)S(1)} %fusion.16.refs_0_), channel_id=1, source_target_pairs={{0,48},{16,0},{32,16},{48,32},{1,49},{17,1},{33,17},{49,33},{2,50}... | collective-permute-start | bytes 55304 | tf_op jit(solution)/shard_map/ppermute | solution.py:195
  48.7 0.6 copy-start.4
  48.8 0.6 copy-start.5
  48.8 0.6 copy-start.6
  48.8 1.0 copy-start.1
  53.8 36.4 %copy-start.9 = (bf16[1024]{0:T(1024)(128)(2,1)S(1)}, bf16[1024]{0:T(1024)(128)(2,1)}, u32[]{:S(2)}) copy-start(bf16[1024]{0:T(1024)(128)(2,1)} %param.19) | copy-start | bytes 6148
  84.4 20.3 %all-to-all-start.2 = ((bf16[8,32,1024]{2,1,0:T(8,128)(2,1)}), bf16[8,32,1024]{2,1,0:T(8,128)(2,1)S(1)}, u32[]{:S(2)}, u32[]{:S(2)}) async-start(bf16[8,32,1024]{2,1,0:T(8,128)(2,1)} %get-tuple-element.5), calls=%async_computation.2 | async-start | bytes 1048576 | tf_op jit(solution)/shard_map/all_to_all | solution.py:270
  104.7 4.8 %collective-permute-start.3 = (bf16[256,1024]{1,0:T(8,128)(2,1)S(1)}, bf16[256,1024]{1,0:T(8,128)(2,1)S(1)}, u32[]{:S(2)}, u32[]{:S(2)}) collective-permute-start(bf16[256,1024]{1,0:T(8,128)(2,1)S(1)} %bitcast.32), channel_id=1, source_target_pairs={{0,1},{1,0},{2,3},{3,2},{4,5},{5,4},{6,7},{7,6},{8,9},{9,8},{10,11... | collective-permute-start | bytes 1572872 | tf_op jit(solution)/shard_map/ppermute | solution.py:271
  106.9 1.7 copy-start.13
  109.6 1.7 copy-start.14
  147.1 3.8 %collective-permute-start.4 = (bf16[256,1024]{1,0:T(8,128)(2,1)S(1)}, bf16[256,1024]{1,0:T(8,128)(2,1)S(1)}, u32[]{:S(2)}, u32[]{:S(2)}) collective-permute-start(bf16[256,1024]{1,0:T(8,128)(2,1)S(1)} %convolution_convert_fusion.1), channel_id=1, source_target_pairs={{0,1},{1,0},{2,3},{3,2},{4,5},{5,4},{6,7},{7,6},{8,9},{9,8},{10,11... | collective-permute-start | bytes 1572872 | tf_op jit(solution)/shard_map/ppermute | solution.py:288
  151.4 24.7 %copy-start.3 = (bf16[8,1024]{1,0:T(8,128)(2,1)S(1)}, bf16[8,1024]{1,0:T(8,128)(2,1)}, u32[]{:S(2)}) copy-start(bf16[8,1024]{1,0:T(8,128)(2,1)} %get-tuple-element.4) | copy-start | bytes 49156
  172.8 16.6 %all-to-all-start.6 = ((bf16[4,8,1024]{2,1,0:T(8,128)(2,1)}), bf16[4,8,1024]{2,1,0:T(8,128)(2,1)S(1)}, u32[]{:S(2)}, u32[]{:S(2)}) async-start(bf16[4,8,1024]{2,1,0:T(8,128)(2,1)} %bitcast.10), calls=%async_computation.6 | async-start | bytes 131072 | tf_op jit(solution)/shard_map/all_to_all | solution.py:35

commit v3 on v2

--- a/solution.py
+++ b/solution.py
@@ -41,89 +41,98 @@
     return jnp.concatenate([wide[:, g * HD : (g + 1) * HD] for g in range(count)], axis=0)
 
 
-def attend_kernel(far_ref, *refs):
-    pages_ref, resident_ref, new_ref, seen_ref, out_ref = refs[-5:]
-    asked_refs = refs[:-5]
-    far = far_ref[0]
-    owners = len(asked_refs)
-    tokens, columns = asked_refs[0].shape
+def head_rows(wide):
+    return stack_heads(wide.astype(jnp.float32)).astype(jnp.bfloat16)
+
+
+def scores(asked, keys):
+    return (1.0 / math.sqrt(HD)) * lax.dot_general(
+        asked, keys, (((1,), (1,)), ((), ())), preferred_element_type=jnp.float32
+    )
+
+
+def mix(weight, values):
+    high = weight.astype(jnp.bfloat16)
+    low = (weight - high.astype(jnp.float32)).astype(jnp.bfloat16)
+    return jnp.dot(high, values, preferred_element_type=jnp.float32) + jnp.dot(
+        low, values, preferred_element_type=jnp.float32
+    )
+
+
+def page_mask(token, step_count, seen):
+    sign = jnp.where(token < step_count, 1.0, -1.0)
+    offset = lax.broadcasted_iota(jnp.int32, seen.shape, 1) & (PAGE - 1)
+    return sign * seen > offset.astype(jnp.float32)
+
+
+def resident_kernel(asked_ref, resident_ref, new_ref, seen_ref, mixed_ref, peak_ref, total_ref):
+    tokens, columns = asked_ref.shape
     width = columns - HD
-    heads = width // HD
-    queries = heads * tokens
-    score_scale = 1.0 / math.sqrt(HD)
+    step_count = tokens // 2
+    queries = width // HD * tokens
     token = lax.broadcasted_iota(jnp.int32, (queries, 1), 0) & (tokens - 1)
-    step_count = tokens // 2
-    sign = jnp.where(token < step_count, 1.0, -1.0)
-
-    def scores(asked, keys):
-        return score_scale * lax.dot_general(
-            asked, keys, (((1,), (1,)), ((), ())), preferred_element_type=jnp.float32
-        )
-
-    def mix(weight, values):
-        high = weight.astype(jnp.bfloat16)
-        low = (weight - high.astype(jnp.float32)).astype(jnp.bfloat16)
-        return jnp.dot(high, values, preferred_element_type=jnp.float32) + jnp.dot(
-            low, values, preferred_element_type=jnp.float32
-        )
-
-    def page_mask(seen):
-        offset = lax.broadcasted_iota(jnp.int32, seen.shape, 1) & (PAGE - 1)
-        return sign * seen > offset.astype(jnp.float32)
-
-    def heads_of(index):
-        return stack_heads(asked_refs[index][:, :width].astype(jnp.float32)).astype(jnp.bfloat16)
-
-    asked = heads_of(0)
+    asked = head_rows(asked_ref[:, :width])
     pages = resident_ref.shape[0]
     keys = resident_ref[:, 0].reshape(pages * PAGE, HD)
     values = resident_ref[:, 1].reshape(pages * PAGE, HD)
-    mask = page_mask(seen_ref[...])
+    mask = page_mask(token, step_count, seen_ref[...])
     score = jnp.where(mask, scores(asked, keys), -1e30)
     fresh = scores(asked, new_ref[0])
     other = lax.broadcasted_iota(jnp.int32, (1, fresh.shape[1]), 1)
     start = jnp.where(token < step_count, 0, step_count)
-    fresh_mask = (other >= start) & (other <= token)
-    fresh = jnp.where(fresh_mask, fresh, -1e30)
-    own_peak = jnp.maximum(
+    fresh = jnp.where((other >= start) & (other <= token), fresh, -1e30)
+    peak = jnp.maximum(
         jnp.max(score, axis=1, keepdims=True), jnp.max(fresh, axis=1, keepdims=True)
     )
-    weight = jnp.exp(score - own_peak)
-    fresh_weight = jnp.exp(fresh - own_peak)
-    own_total = jnp.sum(weight, axis=1, keepdims=True) + jnp.sum(
-        fresh_weight, axis=1, keepdims=True
-    )
-    own_mixed = mix(weight, values) + mix(fresh_weight, new_ref[1])
-
+    weight = jnp.exp(score - peak)
+    fresh_weight = jnp.exp(fresh - peak)
+    total = jnp.sum(weight, axis=1, keepdims=True) + jnp.sum(fresh_weight, axis=1, keepdims=True)
+    mixed_ref[...] = mix(weight, values) + mix(fresh_weight, new_ref[1])
+    peak_ref[...] = jnp.broadcast_to(peak, peak_ref.shape)
+    total_ref[...] = jnp.broadcast_to(total, total_ref.shape)
+
+
+def attend_kernel(far_ref, *refs):
+    far = far_ref[0]
+    pages_ref, mixed_ref, peak_ref, total_ref, out_ref = refs[-5:]
+    asked_of = [ref[...] for ref in refs[:-5]]
+    owners = len(asked_of)
+    tokens, columns = asked_of[0].shape
+    width = columns - HD
+    heads = width // HD
+    queries = heads * tokens
+    token = lax.broadcasted_iota(jnp.int32, (queries, 1), 0) & (tokens - 1)
     senders, landed = pages_ref.shape[0], pages_ref.shape[1]
     slots = landed // owners
     key_count = senders * slots * PAGE
     place = lax.broadcasted_iota(jnp.int32, (HD, key_count), 1) // PAGE + far * (senders * slots)
     expand = (lax.broadcasted_iota(jnp.int32, (HD, key_count), 0) == place).astype(jnp.float32)
+    expand = expand.astype(jnp.bfloat16)
     lane = lax.broadcasted_iota(jnp.int32, (tokens, HD), 1)
-    for back in range(owners):
-        owner = (far - back) & (owners - 1)
-        table = asked_refs[back][:, width:]
-        seen = jnp.dot(table, expand.astype(jnp.bfloat16), preferred_element_type=jnp.float32)[0:1]
-        asked = heads_of(back)
+    for flip in range(owners):
+        owner = far ^ flip
+        table = asked_of[flip][:, width:]
+        seen = jnp.dot(table, expand, preferred_element_type=jnp.float32)[0:1]
+        asked = head_rows(asked_of[flip][:, :width])
         mine = pages_ref[:, pl.ds(owner * slots, slots)]
         keys = mine[:, :, 0].reshape(key_count, HD)
         values = mine[:, :, 1].reshape(key_count, HD)
-        mask = page_mask(seen)
+        mask = page_mask(token, tokens // 2, seen)
         score = jnp.where(mask, scores(asked, keys), -1e30)
         peak = jnp.max(score, axis=1, keepdims=True)
         weight = jnp.where(mask, jnp.exp(score - peak), 0.0)
         total = jnp.sum(weight, axis=1, keepdims=True)
         mixed = mix(weight, values)
-        top = jnp.maximum(peak, own_peak) if back == 0 else peak
+        own_peak = peak_ref[:, :1]
+        top = jnp.maximum(peak, own_peak) if flip == 0 else peak
         top = top.astype(jnp.bfloat16).astype(jnp.float32)
         here = jnp.where(total > 0.0, jnp.exp(jnp.minimum(peak - top, 80.0)), 0.0)
         total = here * total
         mixed = here * mixed
-        if back == 0:
+        if flip == 0:
             own = jnp.exp(jnp.minimum(own_peak - top, 80.0))
-            total = total + own * own_total
-            mixed = mixed + own * own_mixed
+            total = total + own * total_ref[:, :1]
+            mixed = mixed + own * mixed_ref[...]
         mixed = mixed / jnp.where(total > 0.0, total, 1.0)
         total_high = total.astype(jnp.bfloat16).astype(jnp.float32)
         total_low = total - total_high
@@ -173,7 +182,9 @@
     attended_ref[...] = own.astype(jnp.bfloat16)
 
 
-def attention(queries, new_entries, resident, swap_area, swap_dest, page_table, lengths):
+def attention(
+    queries, new_entries, resident, swap_area, swap_dest, page_table, lengths, weights
+):
     owners = lax.axis_size(ROWS)
     far_count = lax.axis_size("zhi")
     near_count = lax.axis_size(NEAR)
@@ -192,8 +203,8 @@
     table = jnp.pad(seen[None, pages_here:].astype(jnp.bfloat16), ((0, tokens - 1), (0, 0)))
     asked = jnp.concatenate([queries.reshape(tokens, width), table], axis=1)
     asked = [asked] + [
-        lax.ppermute(asked, "zhi", [(i, (i + back) % far_count) for i in range(far_count)])
-        for back in range(1, far_count)
+        lax.ppermute(asked, "zhi", [(i, i ^ flip) for i in range(far_count)])
+        for flip in range(1, far_count)
     ]
     seen_here = jnp.repeat(seen[:pages_here], PAGE)[None, :]
 
@@ -218,12 +229,26 @@
     fresh = jnp.pad(fresh, ((0, 0), (0, HD - tokens), (0, 0)))
     whole = pl.BlockSpec(memory_space=pltpu.VMEM)
     scalar = pl.BlockSpec(memory_space=pltpu.SMEM)
+    queries_here = width // HD * tokens
+    square = jax.ShapeDtypeStruct((queries_here, HD), jnp.float32)
+    found = pl.pallas_call(
+        resident_kernel,
+        out_shape=(square, square, square),
+        in_specs=[whole] * 4,
+        out_specs=(whole, whole, whole),
+        cost_estimate=pl.CostEstimate(
+            flops=6 * queries_here * HD * pages_here * PAGE,
+            bytes_accessed=2 * resident.size,
+            transcendentals=queries_here * pages_here * PAGE,
+        ),
+    )(asked[0], resident, fresh, seen_here)
     parts = pl.pallas_call(
         attend_kernel,
         out_shape=jax.ShapeDtypeStruct((far_count, far_count, tokens, width + HD), jnp.bfloat16),
         in_specs=[scalar] + [whole] * (far_count + 4),
         out_specs=whole,
-    )(far, *asked, landed, resident, fresh, seen_here)
+    )(far, *asked, landed, *found)
+    parts, weights = lax.optimization_barrier((parts, weights))
     parts = lax.all_to_all(parts, "zhi", split_axis=0, concat_axis=0, tiled=True)
     copies, attended = pl.pallas_call(
         merge_kernel,
@@ -234,46 +259,39 @@
         in_specs=[scalar, whole],
         out_specs=(whole, whole),
     )(far, parts)
-    return copies, attended
-
-
-def gated_parts(tokens, norm_gain, gate_weight, up_weight):
+    return copies, attended, weights
+
+
+def join_weights(gate_weight, up_weight):
+    units = gate_weight.shape[1]
+    gap = jnp.zeros((gate_weight.shape[0], 512 - units), gate_weight.dtype)
+    return jnp.concatenate([gate_weight, gap, up_weight, gap], axis=1)
+
+
+def gated_parts(tokens, norm_gain, weights, units):
     wide = tokens.astype(jnp.float32)
     squares = jnp.sum(wide * wide, axis=1, keepdims=True)
-    squares_high = squares.astype(jnp.bfloat16)
-    squares_low = (squares - squares_high.astype(jnp.float32)).astype(jnp.bfloat16)
+    squares_high = squares.astype(jnp.bfloat16).astype(jnp.float32)
     normed = (wide * norm_gain.astype(jnp.float32)[None, :]).astype(jnp.bfloat16)
-    gate_part = jnp.dot(normed, gate_weight, preferred_element_type=jnp.float32)
-    up_part = jnp.dot(normed, up_weight, preferred_element_type=jnp.float32)
-    count, units = gate_part.shape
-    gap = jnp.zeros((count, 512 - units - 2), jnp.bfloat16)
-    tail = jnp.zeros((count, 512 - units), jnp.bfloat16)
-    return jnp.concatenate(
-        [
-            gate_part.astype(jnp.bfloat16),
-            squares_high,
-            squares_low,
-            gap,
-            up_part.astype(jnp.bfloat16),
-            tail,
-        ],
-        axis=1,
-    )
-
-
-def mlp(copies, attended, norm_gain, gate_weight, up_weight, down_weight):
+    both = jnp.dot(normed, weights, preferred_element_type=jnp.float32)
+    column = jnp.arange(both.shape[1], dtype=jnp.int32)[None, :]
+    both = jnp.where(column == units, squares_high, both)
+    both = jnp.where(column == units + 1, squares - squares_high, both)
+    return both.astype(jnp.bfloat16)
+
+
+def mlp(copies, attended, norm_gain, weights, units, down_weight):
     tokens_here, width = attended.shape
     far = lax.axis_size("zhi")
     mid = lax.axis_size(MID)
     blk = lax.axis_size(BLK)
-    units = gate_weight.shape[1]
     own = lax.all_to_all(copies, MID, split_axis=0, concat_axis=0, tiled=True).reshape(-1, width)
     other = lax.ppermute(own, "core", SWAP)
     half = own.shape[0]
     parts = jnp.concatenate(
         [
-            gated_parts(own, norm_gain, gate_weight, up_weight),
-            gated_parts(other, norm_gain, gate_weight, up_weight),
+            gated_parts(own, norm_gain, weights, units),
+            gated_parts(other, norm_gain, weights, units),
         ],
         axis=0,
     )
@@ -306,10 +324,12 @@
     up_weight,
     down_weight,
 ):
-    copies, attended = attention(
-        queries, new_entries, resident, swap_area, swap_dest, page_table, lengths
-    )
-    layer_out = mlp(copies, attended, norm_gain, gate_weight, up_weight, down_weight)
+    weights = join_weights(gate_weight, up_weight)
+    copies, attended, weights = attention(
+        queries, new_entries, resident, swap_area, swap_dest, page_table, lengths, weights
+    )
+    units = gate_weight.shape[1]
+    layer_out = mlp(copies, attended, norm_gain, weights, units, down_weight)
     return attended.reshape(queries.shape), layer_out.reshape(queries.shape)
 
 

time: 191 us -> 187 us (0.979)
  starting transfers between devices: 44.4 us -> 40.8 us
  other arithmetic: 3.47 us -> 6.77 us
  matrix products: 6.66 us -> 4.59 us
    ppermute x3, starting transfers between devices: 22.5 us -> 18.9 us  [attention(): lax.ppermute(asked, 'zhi', [(i, i ^ flip) for i in range(far_count)])]
    concatenate x1 -> x2, other arithmetic: 0.08 us -> 2.81 us  [the longest x1 2.73 us: join_weights(): return jnp.concatenate([gate_weight, gap, up_weight, gap], axis=1)]
    pallas_call x0 -> x1, Pallas kernels: none -> 2.23 us  [attention(): pl.pallas_call(resident_kernel, out_shape=(square, square, square), in_sp...]
    dot_general x4 -> x2, matrix products: 4.3 us -> 2.24 us  [gated_parts(): both = jnp.dot(normed, weights, preferred_element_type=jnp.float32)]
  transfers between devices with their start and end apart: 8 -> 8, of which waited for: 4 -> 6; matrix products, arithmetic and copies ran while one was open for 3% -> 4% of each run, Pallas kernels for 0% -> 1%
where the time goes in v3:
time: 187 us; the launch traced here: 186 us
  blocking collectives  81.7 us (44%)
  starting transfers between devices  40.8 us (22%)
  waiting for transfers between devices  37.8 us (20%)
  Pallas kernels  7.83 us (4%)
  other arithmetic  6.77 us (4%)
  local copies, waits for them, and re-layouts  5.15 us (3%)
  matrix products  4.59 us (2%)
    all_to_all x2, blocking collectives, collect(): lax.all_to_all(parts, axes, split_axis=0, concat_axis=0, tiled=True)  40.9 us
    all_to_all x1, blocking collectives, attention(): lax.all_to_all(parts, 'zhi', split_axis=0, concat_axis=0, tiled=True)  28.5 us
    ppermute x3, starting transfers between devices, attention(): lax.ppermute(asked, 'zhi', [(i, i ^ flip) for i in range(far_count)])  18.9 us
    all_to_all x1, waiting for transfers between devices, mlp(): lax.all_to_all(copies, MID, split_axis=0, concat_axis=0, tiled=True)  13.9 us
    all_to_all x1, waiting for transfers between devices, collect(): lax.all_to_all(parts, axes, split_axis=0, concat_axis=0, tiled=True)  12.7 us
    all_to_all x1, blocking collectives, spread(): lax.all_to_all(copies, axes, split_axis=0, concat_axis=0, tiled=True)  12.3 us
    ppermute x3, waiting for transfers between devices, attention(): lax.ppermute(asked, 'zhi', [(i, i ^ flip) for i in range(far_count)])  8.98 us
    all_to_all x1, starting transfers between devices, attention(): lax.all_to_all(outgoing, NEAR, split_axis=0, concat_axis=0, tiled=True)  8.94 us
  transfers between devices with their start and end apart: 8, of which 6 were waited for; matrix products, arithmetic and copies ran while one was open for 4% of the time, Pallas kernels for 1%

profile of v3, /device:TPU:32, one launch (start us, length us, event | category | flops | bytes accessed | tf_op | source)
XLA Modules:
  0.0 185.6 jit_solution(14578155094204067146)
XLA Ops:
  0.6 0.9 convert_reduce_fusion.2
  1.6 0.7 fusion.24
  2.3 1.5 fusion
  3.8 1.2 copy.22
  5.0 8.9 %all-to-all-start = ((bf16[16,8,2,16,128]{4,3,2,1,0:T(8,128)(2,1)}), bf16[16,8,2,16,128]{4,3,2,1,0:T(8,128)(2,1)S(1)}, u32[]{:S(2)}, u32[]{:S(2)}) async-start(bf16[16,8,2,16,128]{4,3,2,1,0:T(8,128)(2,1)} %bitcast.16), calls=%async_computation | async-start | bytes 2097152 | tf_op jit(solution)/shard_map/all_to_all | solution.py:226
  14.0 0.1 clamp_multiply_fusion
  14.1 0.1 select_reduce_fusion
  14.2 0.1 slice_bitcast_fusion
  14.3 8.8 %collective-permute-start = (bf16[8,1152]{1,0:T(8,128)(2,1)S(1)}, bf16[8,1152]{1,0:T(8,128)(2,1)S(1)}, u32[]{:S(2)}, u32[]{:S(2)}) collective-permute-start(bf16[8,1152]{1,0:T(8,128)(2,1)S(1)} %fusion.21.asked_ref.refs_0_), channel_id=1, source_target_pairs={{0,16},{16,0},{32,48},{48,32},{1,17},{17,1},{33,49},{49,33},{2,18}... | collective-permute-start | bytes 55304 | tf_op jit(solution)/shard_map/ppermute | solution.py:206
  23.1 8.2 %collective-permute-start.1 = (bf16[8,1152]{1,0:T(8,128)(2,1)S(1)}, bf16[8,1152]{1,0:T(8,128)(2,1)S(1)}, u32[]{:S(2)}, u32[]{:S(2)}) collective-permute-start(bf16[8,1152]{1,0:T(8,128)(2,1)S(1)} %fusion.21.asked_ref.refs_0_), channel_id=1, source_target_pairs={{0,32},{16,48},{32,0},{48,16},{1,33},{17,49},{33,1},{49,17},{2,34}... | collective-permute-start | bytes 55304 | tf_op jit(solution)/shard_map/ppermute | solution.py:206
  31.3 1.9 %collective-permute-start.2 = (bf16[8,1152]{1,0:T(8,128)(2,1)S(1)}, bf16[8,1152]{1,0:T(8,128)(2,1)S(1)}, u32[]{:S(2)}, u32[]{:S(2)}) collective-permute-start(bf16[8,1152]{1,0:T(8,128)(2,1)S(1)} %fusion.21.asked_ref.refs_0_), channel_id=1, source_target_pairs={{0,48},{16,32},{32,16},{48,0},{1,49},{17,33},{33,17},{49,1},{2,50}... | collective-permute-start | bytes 55304 | tf_op jit(solution)/shard_map/ppermute | solution.py:206
  33.3 2.7 %pad_maximum_fusion = bf16[1024,1024]{0,1:T(8,128)(2,1)} fusion(bf16[1024,64]{0,1:T(8,128)(2,1)S(1)} %broadcast_in_dim.91, bf16[1024,448]{0,1:T(8,128)(2,1)S(1)} %copy-done.3, bf16[1024,448]{0,1:T(8,128)(2,1)} %param.20), kind=kLoop, calls=%fused_computation.1 | loop fusion | flops 8388608 | bytes 4063232 | tf_op jit(solution)/shard_map/concatenate | solution.py:268
  36.0 0.1 broadcast_in_dim.90
  36.1 0.7 broadcast_in_dim_reshape.3.seen_ref
  36.8 0.6 pad.9.new_ref
  37.4 2.2 %shard_map.134 = (f32[64,128]{1,0:T(8,128)}, f32[64,128]{1,0:T(8,128)}, f32[64,128]{1,0:T(8,128)}) custom-call(bf16[8,1152]{1,0:T(8,128)(2,1)} %copy-done.4, bf16[64,2,16,128]{3,2,1,0:T(8,128)(2,1)} %resident_ref.1, bf16[2,128,128]{2,1,0:T(8,128)(2,1)} %pad.9.new_ref, f32[1,1024]{1,0:T(1,128)} %broadcast_in_dim_reshape.3.seen_ref), custom_call_target="tpu_custom_call" | custom-call | flops 50331648 | bytes 524288 | tf_op jit(solution)/shard_map/pallas_call | solution.py:234
  39.7 1.3 collective-permute-done.1.refs_2_
  41.0 7.7 %collective-permute-done.2.refs_3_ = bf16[8,1152]{1,0:T(8,128)(2,1)S(1)} collective-permute-done((bf16[8,1152]{1,0:T(8,128)(2,1)S(1)}, bf16[8,1152]{1,0:T(8,128)(2,1)S(1)}, u32[]{:S(2)}, u32[]{:S(2)}) %collective-permute-start.2) | collective-permute-done | bytes 18464 | tf_op jit(solution)/shard_map/ppermute | solution.py:206
  48.7 0.6 copy-done.8
  49.3 0.4 copy-done.1
  49.6 3.5 %shard_map.135 = bf16[4,4,8,1152]{3,2,1,0:T(8,128)(2,1)} custom-call(s32[1]{0:T(128)} %bitcast.far_ref, bf16[8,1152]{1,0:T(8,128)(2,1)} %copy-done.4, bf16[8,1152]{1,0:T(8,128)(2,1)} %copy-done.6, bf16[8,1152]{1,0:T(8,128)(2,1)} %copy-done.7, bf16[8,1152]{1,0:T(8,128)(2,1)} %copy-done.8, bf16[16,8,2,16,128]{4,3,2,1,0:T(8,128)(2,1)} %copy-done.1, ...), custom_call_target="tpu_custom_call" | custom-call | tf_op jit(solution)/shard_map/pallas_call | solution.py:245
  53.1 28.5 %all_to_all.35.parts_ref = bf16[4,4,8,1152]{3,2,1,0:T(8,128)(2,1)} all-to-all(bf16[4,4,8,1152]{3,2,1,0:T(8,128)(2,1)} %shard_map.135), channel_id=1, replica_groups=mesh['ylo'=2,'x'=4,'zhi'=4,'zlo'=4,'yhi'=2,'core'=2] {'zhi'}, dimensions={0} | all-to-all | bytes 589824 | tf_op jit(solution)/shard_map/all_to_all | solution.py:252
  81.7 2.1 %shard_map.136 = (bf16[8,32,1024]{2,1,0:T(8,128)(2,1)}, bf16[8,1024]{1,0:T(8,128)(2,1)}) custom-call(s32[1]{0:T(128)} %bitcast.far_ref, bf16[4,4,8,1152]{3,2,1,0:T(8,128)(2,1)} %all_to_all.35.parts_ref), custom_call_target="tpu_custom_call" | custom-call | tf_op jit(solution)/shard_map/pallas_call | solution.py:253
  83.8 5.8 %all-to-all-start.2 = ((bf16[8,32,1024]{2,1,0:T(8,128)(2,1)}), bf16[8,32,1024]{2,1,0:T(8,128)(2,1)S(1)}, u32[]{:S(2)}, u32[]{:S(2)}) async-start(bf16[8,32,1024]{2,1,0:T(8,128)(2,1)} %get-tuple-element.14), calls=%async_computation.2 | async-start | bytes 1048576 | tf_op jit(solution)/shard_map/all_to_all | solution.py:288
  89.6 0.6 iota_compare_fusion.5
  90.1 13.9 %all-to-all-done.2 = bf16[8,32,1024]{2,1,0:T(8,128)(2,1)S(1)} async-done(((bf16[8,32,1024]{2,1,0:T(8,128)(2,1)}), bf16[8,32,1024]{2,1,0:T(8,128)(2,1)S(1)}, u32[]{:S(2)}, u32[]{:S(2)}) %all-to-all-start.2) | async-done | bytes 524320 | tf_op jit(solution)/shard_map/all_to_all | solution.py:288
  104.1 0.2 multiply_reduce_fusion
  104.2 0.1 reduce_sum.71
  104.3 1.9 %collective-permute-start.3 = (bf16[256,1024]{1,0:T(8,128)(2,1)S(1)}, bf16[256,1024]{1,0:T(8,128)(2,1)S(1)}, u32[]{:S(2)}, u32[]{:S(2)}) collective-permute-start(bf16[256,1024]{1,0:T(8,128)(2,1)S(1)} %bitcast.29), channel_id=1, source_target_pairs={{0,1},{1,0},{2,3},{3,2},{4,5},{5,4},{6,7},{7,6},{8,9},{9,8},{10,11... | collective-permute-start | bytes 1572872 | tf_op jit(solution)/shard_map/ppermute | solution.py:289
  106.3 1.5 fusion.2
  107.8 0.3 collective-permute-done.3
  108.1 0.2 fusion.3
  108.3 0.7 select_convert_fusion
  109.2 20.2 %all_to_all.36 = bf16[8,64,1024]{2,1,0:T(8,128)(2,1)S(1)} all-to-all(bf16[8,64,1024]{2,1,0:T(8,128)(2,1)S(1)} %bitcast.27), channel_id=1, replica_groups=mesh['ylo'=2,'x'=4,'zhi'=4,'zlo'=4,'yhi'=2,'core'=2] {'ylo','x'}, dimensions={0} | all-to-all | bytes 2097152 | tf_op jit(solution)/shard_map/all_to_all | solution.py:35
  129.4 0.2 convert_reduce_fusion
  129.6 0.2 fusion.18
  129.8 0.1 fusion.13
  129.9 12.3 %all_to_all.37 = bf16[8,64,448]{2,1,0:T(8,128)(2,1)S(1)} all-to-all(bf16[8,64,448]{2,1,0:T(8,128)(2,1)S(1)} %broadcast_in_dim.98), channel_id=1, replica_groups=mesh['ylo'=2,'x'=4,'zhi'=4,'zlo'=4,'yhi'=2,'core'=2] {'ylo','x'}, dimensions={0} | all-to-all | bytes 917504 | tf_op jit(solution)/shard_map/all_to_all | solution.py:30
  142.2 0.4 convolution_convert_fusion.1
  142.7 1.9 %collective-permute-start.4 = (bf16[256,1024]{1,0:T(8,128)(2,1)S(1)}, bf16[256,1024]{1,0:T(8,128)(2,1)S(1)}, u32[]{:S(2)}, u32[]{:S(2)}) collective-permute-start(bf16[256,1024]{1,0:T(8,128)(2,1)S(1)} %convolution_convert_fusion.1), channel_id=1, source_target_pairs={{0,1},{1,0},{2,3},{3,2},{4,5},{5,4},{6,7},{7,6},{8,9},{9,8},{10,11... | collective-permute-start | bytes 1572872 | tf_op jit(solution)/shard_map/ppermute | solution.py:306
  144.6 1.9 %collective-permute-done.4 = bf16[256,1024]{1,0:T(8,128)(2,1)S(1)} collective-permute-done((bf16[256,1024]{1,0:T(8,128)(2,1)S(1)}, bf16[256,1024]{1,0:T(8,128)(2,1)S(1)}, u32[]{:S(2)}, u32[]{:S(2)}) %collective-permute-start.4) | collective-permute-done | bytes 524320 | tf_op jit(solution)/shard_map/ppermute | solution.py:306
  146.5 0.4 add_convert_fusion
  147.0 20.7 %all_to_all.38 = bf16[8,32,1024]{2,1,0:T(8,128)(2,1)S(1)} all-to-all(bf16[8,32,1024]{2,1,0:T(8,128)(2,1)S(1)} %bitcast.28), channel_id=1, replica_groups=mesh['ylo'=2,'x'=4,'zhi'=4,'zlo'=4,'yhi'=2,'core'=2] {'zlo','yhi'}, dimensions={0} | all-to-all | bytes 1048576 | tf_op jit(solution)/shard_map/all_to_all | solution.py:35
  167.6 0.7 reduce_sum.74
  168.4 3.3 %all-to-all-start.6 = ((bf16[4,8,1024]{2,1,0:T(8,128)(2,1)}), bf16[4,8,1024]{2,1,0:T(8,128)(2,1)S(1)}, u32[]{:S(2)}, u32[]{:S(2)}) async-start(bf16[4,8,1024]{2,1,0:T(8,128)(2,1)} %bitcast.9), calls=%async_computation.6 | async-start | bytes 131072 | tf_op jit(solution)/shard_map/all_to_all | solution.py:35
  171.7 0.6 reshape.142
  172.3 12.7 %all-to-all-done.6 = bf16[4,8,1024]{2,1,0:T(8,128)(2,1)S(1)} async-done(((bf16[4,8,1024]{2,1,0:T(8,128)(2,1)}), bf16[4,8,1024]{2,1,0:T(8,128)(2,1)S(1)}, u32[]{:S(2)}, u32[]{:S(2)}) %all-to-all-start.6) | async-done | bytes 65568 | tf_op jit(solution)/shard_map/all_to_all | solution.py:35
  185.0 0.6 reshape.147
  (49 shorter events, 0.3 us)
Async XLA Ops:
  0.6 141.6 %copy-start = (bf16[448,1024]{1,0:T(8,128)(2,1)S(1)}, bf16[448,1024]{1,0:T(8,128)(2,1)}, u32[]{:S(2)}) copy-start(bf16[448,1024]{1,0:T(8,128)(2,1)} %param.22) | copy-start | bytes 2752516
  3.7 10.2 %copy-start.9 = (bf16[2,4,1024]{2,1,0:T(4,128)(2,1)S(1)}, bf16[2,4,1024]{2,1,0:T(4,128)(2,1)}, u32[]{:S(2)}) copy-start(bf16[2,4,1024]{2,1,0:T(4,128)(2,1)} %param.12) | copy-start | bytes 49156
  3.7 10.2 %copy-start.14 = (s32[2]{0:T(128)S(1)}, s32[2]{0:T(128)}, u32[]{:S(2)}) copy-start(s32[2]{0:T(128)} %param.18) | copy-start | bytes 28
  3.8 10.2 %copy-start.15 = (s32[2]{0:T(128)S(1)}, s32[2]{0:T(128)}, u32[]{:S(2)}) copy-start(s32[2]{0:T(128)} %constant.69) | copy-start | bytes 28
  3.8 10.3 %copy-start.12 = (s32[2,64]{1,0:T(2,128)S(1)}, s32[2,64]{1,0:T(2,128)}, u32[]{:S(2)}) copy-start(s32[2,64]{1,0:T(2,128)} %param.17) | copy-start | bytes 1540
  3.8 29.5 %copy-start.3 = (bf16[1024,448]{0,1:T(8,128)(2,1)S(1)}, bf16[1024,448]{0,1:T(8,128)(2,1)}, u32[]{:S(2)}) copy-start(bf16[1024,448]{0,1:T(8,128)(2,1)} %param.21) | copy-start | bytes 2752516
  5.0 43.7 %all-to-all-start = ((bf16[16,8,2,16,128]{4,3,2,1,0:T(8,128)(2,1)}), bf16[16,8,2,16,128]{4,3,2,1,0:T(8,128)(2,1)S(1)}, u32[]{:S(2)}, u32[]{:S(2)}) async-start(bf16[16,8,2,16,128]{4,3,2,1,0:T(8,128)(2,1)} %bitcast.16), calls=%async_computation | async-start | bytes 2097152 | tf_op jit(solution)/shard_map/all_to_all | solution.py:226
  14.3 21.7 %copy-start.4 = (bf16[8,1152]{1,0:T(8,128)(2,1)}, bf16[8,1152]{1,0:T(8,128)(2,1)S(1)}, u32[]{:S(2)}) copy-start(bf16[8,1152]{1,0:T(8,128)(2,1)S(1)} %fusion.21.asked_ref.refs_0_) | copy-start | bytes 55300
  14.3 25.4 %collective-permute-start = (bf16[8,1152]{1,0:T(8,128)(2,1)S(1)}, bf16[8,1152]{1,0:T(8,128)(2,1)S(1)}, u32[]{:S(2)}, u32[]{:S(2)}) collective-permute-start(bf16[8,1152]{1,0:T(8,128)(2,1)S(1)} %fusion.21.asked_ref.refs_0_), channel_id=1, source_target_pairs={{0,16},{16,0},{32,48},{48,32},{1,17},{17,1},{33,49},{49,33},{2,18}... | collective-permute-start | bytes 55304 | tf_op jit(solution)/shard_map/ppermute | solution.py:206
  23.1 17.9 %collective-permute-start.1 = (bf16[8,1152]{1,0:T(8,128)(2,1)S(1)}, bf16[8,1152]{1,0:T(8,128)(2,1)S(1)}, u32[]{:S(2)}, u32[]{:S(2)}) collective-permute-start(bf16[8,1152]{1,0:T(8,128)(2,1)S(1)} %fusion.21.asked_ref.refs_0_), channel_id=1, source_target_pairs={{0,32},{16,48},{32,0},{48,16},{1,33},{17,49},{33,1},{49,17},{2,34}... | collective-permute-start | bytes 55304 | tf_op jit(solution)/shard_map/ppermute | solution.py:206
  31.3 17.3 %collective-permute-start.2 = (bf16[8,1152]{1,0:T(8,128)(2,1)S(1)}, bf16[8,1152]{1,0:T(8,128)(2,1)S(1)}, u32[]{:S(2)}, u32[]{:S(2)}) collective-permute-start(bf16[8,1152]{1,0:T(8,128)(2,1)S(1)} %fusion.21.asked_ref.refs_0_), channel_id=1, source_target_pairs={{0,48},{16,32},{32,16},{48,0},{1,49},{17,33},{33,17},{49,1},{2,50}... | collective-permute-start | bytes 55304 | tf_op jit(solution)/shard_map/ppermute | solution.py:206
  33.3 3.5 %copy-start.10 = (bf16[2,4,2,128]{3,2,1,0:T(2,128)(2,1)S(1)}, bf16[2,4,2,128]{3,2,1,0:T(2,128)(2,1)}, u32[]{:S(2)}) copy-start(bf16[2,4,2,128]{3,2,1,0:T(2,128)(2,1)} %param.13) | copy-start | bytes 12292
  36.1 53.5 %copy-start.11 = (bf16[1024]{0:T(1024)(128)(2,1)S(1)}, bf16[1024]{0:T(1024)(128)(2,1)}, u32[]{:S(2)}) copy-start(bf16[1024]{0:T(1024)(128)(2,1)} %param.19) | copy-start | bytes 6148
  39.7 9.0 %copy-start.6 = (bf16[8,1152]{1,0:T(8,128)(2,1)}, bf16[8,1152]{1,0:T(8,128)(2,1)S(1)}, u32[]{:S(2)}) copy-start(bf16[8,1152]{1,0:T(8,128)(2,1)S(1)} %collective-permute-done.refs_1_) | copy-start | bytes 55300
  41.0 7.7 %copy-start.7 = (bf16[8,1152]{1,0:T(8,128)(2,1)}, bf16[8,1152]{1,0:T(8,128)(2,1)S(1)}, u32[]{:S(2)}) copy-start(bf16[8,1152]{1,0:T(8,128)(2,1)S(1)} %collective-permute-done.1.refs_2_) | copy-start | bytes 55300
  48.7 0.6 copy-start.8
  48.7 1.0 copy-start.1
  53.1 53.1 %copy-start.2 = (bf16[1024,1024]{0,1:T(8,128)(2,1)S(1)}, bf16[1024,1024]{0,1:T(8,128)(2,1)}, u32[]{:S(2)}) copy-start(bf16[1024,1024]{0,1:T(8,128)(2,1)} %pad_maximum_fusion) | copy-start | bytes 6291460
  83.8 20.3 %all-to-all-start.2 = ((bf16[8,32,1024]{2,1,0:T(8,128)(2,1)}), bf16[8,32,1024]{2,1,0:T(8,128)(2,1)S(1)}, u32[]{:S(2)}, u32[]{:S(2)}) async-start(bf16[8,32,1024]{2,1,0:T(8,128)(2,1)} %get-tuple-element.14), calls=%async_computation.2 | async-start | bytes 1048576 | tf_op jit(solution)/shard_map/all_to_all | solution.py:288
  104.3 3.8 %collective-permute-start.3 = (bf16[256,1024]{1,0:T(8,128)(2,1)S(1)}, bf16[256,1024]{1,0:T(8,128)(2,1)S(1)}, u32[]{:S(2)}, u32[]{:S(2)}) collective-permute-start(bf16[256,1024]{1,0:T(8,128)(2,1)S(1)} %bitcast.29), channel_id=1, source_target_pairs={{0,1},{1,0},{2,3},{3,2},{4,5},{5,4},{6,7},{7,6},{8,9},{9,8},{10,11... | collective-permute-start | bytes 1572872 | tf_op jit(solution)/shard_map/ppermute | solution.py:289
  106.3 2.1 %copy-start.13 = (pred[1024]{0:T(1024)(128)(4,1)S(1)}, pred[1024]{0:T(1024)(128)(4,1)}, u32[]{:S(2)}) copy-start(pred[1024]{0:T(1024)(128)(4,1)} %get-tuple-element.21) | copy-start | bytes 3076
  142.7 29.0 %copy-start.5 = (bf16[8,1024]{1,0:T(8,128)(2,1)S(1)}, bf16[8,1024]{1,0:T(8,128)(2,1)}, u32[]{:S(2)}) copy-start(bf16[8,1024]{1,0:T(8,128)(2,1)} %get-tuple-element.13) | copy-start | bytes 49156
  142.7 3.8 %collective-permute-start.4 = (bf16[256,1024]{1,0:T(8,128)(2,1)S(1)}, bf16[256,1024]{1,0:T(8,128)(2,1)S(1)}, u32[]{:S(2)}, u32[]{:S(2)}) collective-permute-start(bf16[256,1024]{1,0:T(8,128)(2,1)S(1)} %convolution_convert_fusion.1), channel_id=1, source_target_pairs={{0,1},{1,0},{2,3},{3,2},{4,5},{5,4},{6,7},{7,6},{8,9},{9,8},{10,11... | collective-permute-start | bytes 1572872 | tf_op jit(solution)/shard_map/ppermute | solution.py:306
  168.4 16.6 %all-to-all-start.6 = ((bf16[4,8,1024]{2,1,0:T(8,128)(2,1)}), bf16[4,8,1024]{2,1,0:T(8,128)(2,1)S(1)}, u32[]{:S(2)}, u32[]{:S(2)}) async-start(bf16[4,8,1024]{2,1,0:T(8,128)(2,1)} %bitcast.9), calls=%async_computation.6 | async-start | bytes 131072 | tf_op jit(solution)/shard_map/all_to_all | solution.py:35

commit v4 on v3

--- a/solution.py
+++ b/solution.py
@@ -242,14 +242,16 @@
             transcendentals=queries_here * pages_here * PAGE,
         ),
     )(asked[0], resident, fresh, seen_here)
+    found, weights = lax.optimization_barrier((found, weights))
+    weights = join_weights(*weights)
     parts = pl.pallas_call(
         attend_kernel,
         out_shape=jax.ShapeDtypeStruct((far_count, far_count, tokens, width + HD), jnp.bfloat16),
         in_specs=[scalar] + [whole] * (far_count + 4),
         out_specs=whole,
     )(far, *asked, landed, *found)
+    parts = lax.all_to_all(parts, "zhi", split_axis=0, concat_axis=0, tiled=True)
     parts, weights = lax.optimization_barrier((parts, weights))
-    parts = lax.all_to_all(parts, "zhi", split_axis=0, concat_axis=0, tiled=True)
     copies, attended = pl.pallas_call(
         merge_kernel,
         out_shape=(
@@ -262,10 +264,13 @@
     return copies, attended, weights
 
 
-def join_weights(gate_weight, up_weight):
-    units = gate_weight.shape[1]
-    gap = jnp.zeros((gate_weight.shape[0], 512 - units), gate_weight.dtype)
-    return jnp.concatenate([gate_weight, gap, up_weight, gap], axis=1)
+def join_weights(gate_weight, up_weight, down_weight):
+    units, width = down_weight.shape
+    gate, up = gate_weight.T, up_weight.T
+    there = lax.ppermute(jnp.concatenate([gate, up, down_weight], axis=0), "core", SWAP)
+    gap = jnp.zeros((128, width), gate_weight.dtype)
+    wide = jnp.concatenate([gate, there[:units], up, there[units : 2 * units], gap], axis=0)
+    return wide, jnp.concatenate([down_weight, there[2 * units :]], axis=0)
 
 
 def gated_parts(tokens, norm_gain, weights, units):
@@ -273,39 +278,31 @@
     squares = jnp.sum(wide * wide, axis=1, keepdims=True)
     squares_high = squares.astype(jnp.bfloat16).astype(jnp.float32)
     normed = (wide * norm_gain.astype(jnp.float32)[None, :]).astype(jnp.bfloat16)
-    both = jnp.dot(normed, weights, preferred_element_type=jnp.float32)
+    both = lax.dot_general(
+        normed, weights, (((1,), (1,)), ((), ())), preferred_element_type=jnp.float32
+    )
     column = jnp.arange(both.shape[1], dtype=jnp.int32)[None, :]
-    both = jnp.where(column == units, squares_high, both)
-    both = jnp.where(column == units + 1, squares - squares_high, both)
+    both = jnp.where(column == 2 * units, squares_high, both)
+    both = jnp.where(column == 2 * units + 1, squares - squares_high, both)
     return both.astype(jnp.bfloat16)
 
 
-def mlp(copies, attended, norm_gain, weights, units, down_weight):
+def mlp(copies, attended, norm_gain, weights, units):
+    wide_weight, down_weight = weights
     tokens_here, width = attended.shape
     far = lax.axis_size("zhi")
     mid = lax.axis_size(MID)
     blk = lax.axis_size(BLK)
     own = lax.all_to_all(copies, MID, split_axis=0, concat_axis=0, tiled=True).reshape(-1, width)
-    other = lax.ppermute(own, "core", SWAP)
-    half = own.shape[0]
-    parts = jnp.concatenate(
-        [
-            gated_parts(own, norm_gain, weights, units),
-            gated_parts(other, norm_gain, weights, units),
-        ],
-        axis=0,
-    )
-    summed = collect(parts.reshape(blk, 2 * half // blk, 1024), BLK)
+    parts = gated_parts(own, norm_gain, wide_weight, units)
+    summed = collect(parts.reshape(blk, own.shape[0] // blk, parts.shape[1]), BLK)
+    square_sum = summed[:, 2 * units : 2 * units + 1] + summed[:, 2 * units + 1 : 2 * units + 2]
+    factor = lax.rsqrt(square_sum / (width * blk) + epsilon)
     gate_sum = summed[:, :units]
-    up_sum = summed[:, 512 : 512 + units]
-    square_sum = summed[:, units : units + 1] + summed[:, units + 1 : units + 2]
-    factor = lax.rsqrt(square_sum / (width * blk) + epsilon)
+    up_sum = summed[:, units : 2 * units]
     hidden = (jax.nn.silu(factor * gate_sum) * (factor * up_sum)).astype(jnp.bfloat16)
     hidden = spread(hidden, BLK)
-    away = jnp.dot(hidden[half:], down_weight, preferred_element_type=jnp.float32)
-    received = lax.ppermute(away.astype(jnp.bfloat16), "core", SWAP)
-    kept = jnp.dot(hidden[:half], down_weight, preferred_element_type=jnp.float32)
-    kept = (kept + received.astype(jnp.float32)).astype(jnp.bfloat16)
+    kept = jnp.dot(hidden, down_weight, preferred_element_type=jnp.float32).astype(jnp.bfloat16)
     kept = collect(kept.reshape(mid, far * tokens_here, width), MID).astype(jnp.bfloat16)
     down_sum = collect(kept.reshape(far, tokens_here, width), "zhi")
     return (attended.astype(jnp.float32) + down_sum).astype(jnp.bfloat16)
@@ -324,12 +321,12 @@
     up_weight,
     down_weight,
 ):
-    weights = join_weights(gate_weight, up_weight)
+    weights = (gate_weight, up_weight, down_weight)
     copies, attended, weights = attention(
         queries, new_entries, resident, swap_area, swap_dest, page_table, lengths, weights
     )
-    units = gate_weight.shape[1]
-    layer_out = mlp(copies, attended, norm_gain, weights, units, down_weight)
+    units = 2 * gate_weight.shape[1]
+    layer_out = mlp(copies, attended, norm_gain, weights, units)
     return attended.reshape(queries.shape), layer_out.reshape(queries.shape)
 
 

time: 187 us -> 179 us (0.957)
  blocking collectives: 81.7 us -> 46.8 us
  local copies, waits for them, and re-layouts: 5.15 us -> 14.4 us
  starting transfers between devices: 40.8 us -> 49.8 us
  waiting for transfers between devices: 37.8 us -> 45.4 us
    all_to_all x1 -> x0, blocking collectives: 28.5 us -> none  [attention(): lax.all_to_all(parts, 'zhi', split_axis=0, concat_axis=0, tiled=True)]
    all_to_all x0 -> x1, waiting for transfers between devices: none -> 12.7 us  [attention(): lax.all_to_all(parts, 'zhi', split_axis=0, concat_axis=0, tiled=True)]
    unnamed x34 -> x35, local copies, waits for them, and re-layouts: 2.26 us -> 8.27 us
    all_to_all x0 -> x1, starting transfers between devices: none -> 5.52 us  [attention(): lax.all_to_all(parts, 'zhi', split_axis=0, concat_axis=0, tiled=True)]
    all_to_all x2, blocking collectives: 40.9 us -> 36 us  [collect(): lax.all_to_all(parts, axes, split_axis=0, concat_axis=0, tiled=True)]
    all_to_all x1, starting transfers between devices: 3.28 us -> 7.05 us  [collect(): lax.all_to_all(parts, axes, split_axis=0, concat_axis=0, tiled=True)]
    slice x1, local copies, waits for them, and re-layouts: 0.03 us -> 2.55 us  [join_weights(): return (wide, jnp.concatenate([down_weight, there[2 * units:]], axis=0))]
    ppermute x2 -> x1, waiting for transfers between devices: 2.22 us -> 0.01 us  [join_weights(): lax.ppermute(jnp.concatenate([gate, up, down_weight], axis=0), 'core', SWAP)]
  transfers between devices with their start and end apart: 8 -> 8, of which waited for: 6 -> 5; matrix products, arithmetic and copies ran while one was open for 4% -> 8% of each run, Pallas kernels for 1% -> 3%
where the time goes in v4:
time: 179 us; the launch traced here: 178 us
  starting transfers between devices  49.8 us (28%)
  blocking collectives  46.8 us (26%)
  waiting for transfers between devices  45.4 us (25%)
  local copies, waits for them, and re-layouts  14.4 us (8%)
  Pallas kernels  7.83 us (4%)
  other arithmetic  7.17 us (4%)
  matrix products  5.63 us (3%)
    all_to_all x2, blocking collectives, collect(): lax.all_to_all(parts, axes, split_axis=0, concat_axis=0, tiled=True)  36 us
    ppermute x3, starting transfers between devices, attention(): lax.ppermute(asked, 'zhi', [(i, i ^ flip) for i in range(far_count)])  19 us
    all_to_all x1, waiting for transfers between devices, mlp(): lax.all_to_all(copies, MID, split_axis=0, concat_axis=0, tiled=True)  13.1 us
    all_to_all x1, waiting for transfers between devices, collect(): lax.all_to_all(parts, axes, split_axis=0, concat_axis=0, tiled=True)  12.7 us
    all_to_all x1, waiting for transfers between devices, attention(): lax.all_to_all(parts, 'zhi', split_axis=0, concat_axis=0, tiled=True)  12.7 us
    all_to_all x1, blocking collectives, spread(): lax.all_to_all(copies, axes, split_axis=0, concat_axis=0, tiled=True)  10.8 us
    all_to_all x1, starting transfers between devices, attention(): lax.all_to_all(outgoing, NEAR, split_axis=0, concat_axis=0, tiled=True)  8.95 us
    unnamed x35, local copies, waits for them, and re-layouts  8.27 us
  transfers between devices with their start and end apart: 8, of which 5 were waited for; matrix products, arithmetic and copies ran while one was open for 8% of the time, Pallas kernels for 3%

profile of v4, /device:TPU:32, one launch (start us, length us, event | category | flops | bytes accessed | tf_op | source)
XLA Modules:
  0.0 177.8 jit_solution(3228360010526143576)
XLA Ops:
  0.7 1.0 convert_reduce_fusion.2
  1.7 0.7 fusion.18
  2.4 1.5 fusion.2
  3.8 1.2 copy.22
  5.0 9.0 %all-to-all-start = ((bf16[16,8,2,16,128]{4,3,2,1,0:T(8,128)(2,1)}), bf16[16,8,2,16,128]{4,3,2,1,0:T(8,128)(2,1)S(1)}, u32[]{:S(2)}, u32[]{:S(2)}) async-start(bf16[16,8,2,16,128]{4,3,2,1,0:T(8,128)(2,1)} %bitcast.17), calls=%async_computation | async-start | bytes 2097152 | tf_op jit(solution)/shard_map/all_to_all | solution.py:226
  14.1 0.1 select_reduce_fusion
  14.3 0.7 broadcast_in_dim_reshape.3.seen_ref
  15.0 0.6 pad.9.new_ref
  15.7 0.6 fusion.11.asked_ref.refs_0_
  16.3 2.2 %shard_map.134 = (f32[64,128]{1,0:T(8,128)}, f32[64,128]{1,0:T(8,128)}, f32[64,128]{1,0:T(8,128)}) custom-call(bf16[8,1152]{1,0:T(8,128)(2,1)} %fusion.11.asked_ref.refs_0_, bf16[64,2,16,128]{3,2,1,0:T(8,128)(2,1)} %resident_ref.1, bf16[2,128,128]{2,1,0:T(8,128)(2,1)} %pad.9.new_ref, f32[1,1024]{1,0:T(1,128)} %broadcast_in_dim_reshape.3.seen_ref), custom_call_target="tpu_custom_call" | custom-call | flops 50331648 | bytes 524288 | tf_op jit(solution)/shard_map/pallas_call | solution.py:234
  18.6 3.0 %pad_maximum_fusion = bf16[1344,1024]{1,0:T(8,128)(2,1)} fusion(bf16[448,1024]{1,0:T(8,128)(2,1)S(1)} %copy-done.1, bf16[448,1024]{1,0:T(8,128)(2,1)} %bitcast.32, bf16[448,1024]{1,0:T(8,128)(2,1)S(1)} %bitcast.31), kind=kLoop, calls=%fused_computation.1 | loop fusion | flops 8257536 | bytes 5505024 | tf_op jit(solution)/shard_map/concatenate | solution.py:270
  21.6 2.0 %collective-permute-start.3 = (bf16[1344,1024]{1,0:T(8,128)(2,1)}, bf16[1344,1024]{1,0:T(8,128)(2,1)}, u32[]{:S(2)}, u32[]{:S(2)}) collective-permute-start(bf16[1344,1024]{1,0:T(8,128)(2,1)} %pad_maximum_fusion), channel_id=1, source_target_pairs={{0,1},{1,0},{2,3},{3,2},{4,5},{5,4},{6,7},{7,6},{8,9},{9,8},{10,11... | collective-permute-start | bytes 8257544 | tf_op jit(solution)/shard_map/ppermute | solution.py:270
  23.6 8.8 %collective-permute-start = (bf16[8,1152]{1,0:T(8,128)(2,1)S(1)}, bf16[8,1152]{1,0:T(8,128)(2,1)S(1)}, u32[]{:S(2)}, u32[]{:S(2)}) collective-permute-start(bf16[8,1152]{1,0:T(8,128)(2,1)S(1)} %copy-done.4), channel_id=1, source_target_pairs={{0,16},{16,0},{32,48},{48,32},{1,17},{17,1},{33,49},{49,33},{2,18}... | collective-permute-start | bytes 55304 | tf_op jit(solution)/shard_map/ppermute | solution.py:206
  32.5 8.2 %collective-permute-start.1 = (bf16[8,1152]{1,0:T(8,128)(2,1)S(1)}, bf16[8,1152]{1,0:T(8,128)(2,1)S(1)}, u32[]{:S(2)}, u32[]{:S(2)}) collective-permute-start(bf16[8,1152]{1,0:T(8,128)(2,1)S(1)} %copy-done.4), channel_id=1, source_target_pairs={{0,32},{16,48},{32,0},{48,16},{1,33},{17,49},{33,1},{49,17},{2,34}... | collective-permute-start | bytes 55304 | tf_op jit(solution)/shard_map/ppermute | solution.py:206
  40.7 1.9 %collective-permute-start.2 = (bf16[8,1152]{1,0:T(8,128)(2,1)S(1)}, bf16[8,1152]{1,0:T(8,128)(2,1)S(1)}, u32[]{:S(2)}, u32[]{:S(2)}) collective-permute-start(bf16[8,1152]{1,0:T(8,128)(2,1)S(1)} %copy-done.4), channel_id=1, source_target_pairs={{0,48},{16,32},{32,16},{48,0},{1,49},{17,33},{33,17},{49,1},{2,50}... | collective-permute-start | bytes 55304 | tf_op jit(solution)/shard_map/ppermute | solution.py:206
  42.6 1.0 constant_dynamic-update-slice_fusion.1
  43.6 5.2 %collective-permute-done.1.refs_2_ = bf16[8,1152]{1,0:T(8,128)(2,1)S(1)} collective-permute-done((bf16[8,1152]{1,0:T(8,128)(2,1)S(1)}, bf16[8,1152]{1,0:T(8,128)(2,1)S(1)}, u32[]{:S(2)}, u32[]{:S(2)}) %collective-permute-start.1) | collective-permute-done | bytes 18464 | tf_op jit(solution)/shard_map/ppermute | solution.py:206
  48.8 1.7 collective-permute-done.2.refs_3_
  50.5 0.6 copy-done.8
  51.0 0.4 copy-done
  51.4 3.5 %shard_map.135 = bf16[4,4,8,1152]{3,2,1,0:T(8,128)(2,1)} custom-call(s32[1]{0:T(128)} %bitcast.far_ref, bf16[8,1152]{1,0:T(8,128)(2,1)} %fusion.11.asked_ref.refs_0_, bf16[8,1152]{1,0:T(8,128)(2,1)} %copy-done.6, bf16[8,1152]{1,0:T(8,128)(2,1)} %copy-done.7, bf16[8,1152]{1,0:T(8,128)(2,1)} %copy-done.8, bf16[16,8,2,16,128]{4,3,2,1,0:T(8,128)(2,1)} %copy-done, ...), custom_call_target="tpu_custom_call" | custom-call | tf_op jit(solution)/shard_map/pallas_call | solution.py:247
  54.9 5.5 %all-to-all-start.1 = ((bf16[4,4,8,1152]{3,2,1,0:T(8,128)(2,1)}), bf16[4,4,8,1152]{3,2,1,0:T(8,128)(2,1)S(1)}, u32[]{:S(2)}, u32[]{:S(2)}) async-start(bf16[4,4,8,1152]{3,2,1,0:T(8,128)(2,1)} %shard_map.135), calls=%async_computation.1 | async-start | bytes 589824 | tf_op jit(solution)/shard_map/all_to_all | solution.py:253
  60.4 2.2 %slice_dynamic-update-slice_fusion.1 = bf16[1920,1024]{1,0:T(8,128)(2,1)} fusion(bf16[1920,1024]{1,0:T(8,128)(2,1)} %constant_dynamic-update-slice_fusion.1, bf16[1344,1024]{1,0:T(8,128)(2,1)} %collective-permute-done.3), kind=kLoop, calls=%fused_computation.13 | loop fusion | bytes 1835008
  62.7 2.2 %constant_dynamic-update-slice_fusion = bf16[1920,1024]{1,0:T(8,128)(2,1)} fusion(bf16[1920,1024]{1,0:T(8,128)(2,1)} %slice_dynamic-update-slice_fusion.1, bf16[1024,448]{0,1:T(8,128)(2,1)} %param.21), kind=kLoop, calls=%fused_computation.38 | loop fusion | bytes 1835008
  64.8 2.6 %fusion.20 = (bf16[448,1024]{1,0:T(8,128)(2,1)S(1)}, bf16[1920,1024]{1,0:T(8,128)(2,1)}) fusion(bf16[1344,1024]{1,0:T(8,128)(2,1)} %collective-permute-done.3, bf16[1920,1024]{1,0:T(8,128)(2,1)} %constant_dynamic-update-slice_fusion), kind=kLoop, calls=%fused_computation.56 | loop fusion | bytes 3670016 | tf_op jit(solution)/shard_map/slice | solution.py:273
  67.4 0.7 broadcast_dynamic-update-slice_fusion
  68.1 0.2 pad_maximum_fusion.1
  68.4 12.7 %all-to-all-done.1.parts_ref = bf16[4,4,8,1152]{3,2,1,0:T(8,128)(2,1)S(1)} async-done(((bf16[4,4,8,1152]{3,2,1,0:T(8,128)(2,1)}), bf16[4,4,8,1152]{3,2,1,0:T(8,128)(2,1)S(1)}, u32[]{:S(2)}, u32[]{:S(2)}) %all-to-all-start.1) | async-done | bytes 294944 | tf_op jit(solution)/shard_map/all_to_all | solution.py:253
  81.0 0.7 copy-done.3
  81.7 2.1 %shard_map.136 = (bf16[8,32,1024]{2,1,0:T(8,128)(2,1)}, bf16[8,1024]{1,0:T(8,128)(2,1)}) custom-call(s32[1]{0:T(128)} %bitcast.far_ref, bf16[4,4,8,1152]{3,2,1,0:T(8,128)(2,1)} %copy-done.3), custom_call_target="tpu_custom_call" | custom-call | tf_op jit(solution)/shard_map/pallas_call | solution.py:255
  83.8 7.2 %all-to-all-start.2 = ((bf16[8,32,1024]{2,1,0:T(8,128)(2,1)}), bf16[8,32,1024]{2,1,0:T(8,128)(2,1)S(1)}, u32[]{:S(2)}, u32[]{:S(2)}) async-start(bf16[8,32,1024]{2,1,0:T(8,128)(2,1)} %get-tuple-element.27), calls=%async_computation.2 | async-start | bytes 1048576 | tf_op jit(solution)/shard_map/all_to_all | solution.py:296
  91.1 13.1 %all-to-all-done.2 = bf16[8,32,1024]{2,1,0:T(8,128)(2,1)S(1)} async-done(((bf16[8,32,1024]{2,1,0:T(8,128)(2,1)}), bf16[8,32,1024]{2,1,0:T(8,128)(2,1)S(1)}, u32[]{:S(2)}, u32[]{:S(2)}) %all-to-all-start.2) | async-done | bytes 524320 | tf_op jit(solution)/shard_map/all_to_all | solution.py:296
  104.2 0.2 multiply_reduce_fusion
  104.4 0.1 reduce_sum.62
  104.5 0.1 fusion.3
  104.6 3.5 %fusion.1 = bf16[256,1920]{1,0:T(8,128)(2,1)S(1)} fusion(bf16[256,1024]{1,0:T(8,128)(2,1)S(1)} %fusion.3, bf16[1920,1024]{1,0:T(8,128)(2,1)} %broadcast_dynamic-update-slice_fusion, bf16[256]{0:T(256)(128)(2,1)S(1)} %convert_element_type.118, bf16[256]{0:T(256)(128)(2,1)S(1)} %fusion.19, pred[1920]{0:T(1024)(128)(4,1)S(1)} %get-tuple-element.34, ...), kind=kOutput, calls=%fused_computation.4 | convolution fusion | flops 1007616000 | bytes 5444352 | tf_op jit(solution)/shard_map/dot_general | solution.py:281
  108.1 15.4 %all_to_all.35 = bf16[8,32,1920]{2,1,0:T(8,128)(2,1)S(1)} all-to-all(bf16[8,32,1920]{2,1,0:T(8,128)(2,1)S(1)} %bitcast.33), channel_id=1, replica_groups=mesh['ylo'=2,'x'=4,'zhi'=4,'zlo'=4,'yhi'=2,'core'=2] {'ylo','x'}, dimensions={0} | all-to-all | bytes 1966080 | tf_op jit(solution)/shard_map/all_to_all | solution.py:35
  123.5 0.1 convert_reduce_fusion
  123.6 0.2 fusion.15
  123.8 0.1 fusion.7
  124.0 10.8 %all_to_all.36 = bf16[8,32,896]{2,1,0:T(8,128)(2,1)S(1)} all-to-all(bf16[8,32,896]{2,1,0:T(8,128)(2,1)S(1)} %broadcast_in_dim.73), channel_id=1, replica_groups=mesh['ylo'=2,'x'=4,'zhi'=4,'zlo'=4,'yhi'=2,'core'=2] {'ylo','x'}, dimensions={0} | all-to-all | bytes 917504 | tf_op jit(solution)/shard_map/all_to_all | solution.py:30
  134.8 0.7 convolution_convert_fusion.1
  135.5 20.6 %all_to_all.37 = bf16[8,32,1024]{2,1,0:T(8,128)(2,1)S(1)} all-to-all(bf16[8,32,1024]{2,1,0:T(8,128)(2,1)S(1)} %bitcast.35), channel_id=1, replica_groups=mesh['ylo'=2,'x'=4,'zhi'=4,'zlo'=4,'yhi'=2,'core'=2] {'zlo','yhi'}, dimensions={0} | all-to-all | bytes 1048576 | tf_op jit(solution)/shard_map/all_to_all | solution.py:35
  156.1 0.7 reduce_sum.64
  156.8 7.1 %all-to-all-start.6 = ((bf16[4,8,1024]{2,1,0:T(8,128)(2,1)}), bf16[4,8,1024]{2,1,0:T(8,128)(2,1)S(1)}, u32[]{:S(2)}, u32[]{:S(2)}) async-start(bf16[4,8,1024]{2,1,0:T(8,128)(2,1)} %bitcast.10), calls=%async_computation.6 | async-start | bytes 131072 | tf_op jit(solution)/shard_map/all_to_all | solution.py:35
  163.8 0.6 reshape.132
  164.4 12.7 %all-to-all-done.6 = bf16[4,8,1024]{2,1,0:T(8,128)(2,1)S(1)} async-done(((bf16[4,8,1024]{2,1,0:T(8,128)(2,1)}), bf16[4,8,1024]{2,1,0:T(8,128)(2,1)S(1)}, u32[]{:S(2)}, u32[]{:S(2)}) %all-to-all-start.6) | async-done | bytes 65568 | tf_op jit(solution)/shard_map/all_to_all | solution.py:35
  177.2 0.6 reshape.137
  (45 shorter events, 0.4 us)
Async XLA Ops:
  0.6 13.3 %copy-start.14 = (s32[2]{0:T(128)S(1)}, s32[2]{0:T(128)}, u32[]{:S(2)}) copy-start(s32[2]{0:T(128)} %constant.69) | copy-start | bytes 28
  0.6 13.3 %copy-start.13 = (s32[2]{0:T(128)S(1)}, s32[2]{0:T(128)}, u32[]{:S(2)}) copy-start(s32[2]{0:T(128)} %param.18) | copy-start | bytes 28
  0.7 13.4 %copy-start.9 = (bf16[2,4,1024]{2,1,0:T(4,128)(2,1)S(1)}, bf16[2,4,1024]{2,1,0:T(4,128)(2,1)}, u32[]{:S(2)}) copy-start(bf16[2,4,1024]{2,1,0:T(4,128)(2,1)} %param.12) | copy-start | bytes 49156
  0.7 13.4 %copy-start.12 = (s32[2,64]{1,0:T(2,128)S(1)}, s32[2,64]{1,0:T(2,128)}, u32[]{:S(2)}) copy-start(s32[2,64]{1,0:T(2,128)} %param.17) | copy-start | bytes 1540
  0.7 14.3 %copy-start.10 = (bf16[2,4,2,128]{3,2,1,0:T(2,128)(2,1)S(1)}, bf16[2,4,2,128]{3,2,1,0:T(2,128)(2,1)}, u32[]{:S(2)}) copy-start(bf16[2,4,2,128]{3,2,1,0:T(2,128)(2,1)} %param.13) | copy-start | bytes 12292
  0.7 17.9 %copy-start.2 = (bf16[1024,448]{0,1:T(8,128)(2,1)S(1)}, bf16[1024,448]{0,1:T(8,128)(2,1)}, u32[]{:S(2)}) copy-start(bf16[1024,448]{0,1:T(8,128)(2,1)} %param.20) | copy-start | bytes 2752516
  0.7 17.9 %copy-start.1 = (bf16[448,1024]{1,0:T(8,128)(2,1)S(1)}, bf16[448,1024]{1,0:T(8,128)(2,1)}, u32[]{:S(2)}) copy-start(bf16[448,1024]{1,0:T(8,128)(2,1)} %param.22) | copy-start | bytes 2752516
  5.0 45.4 %all-to-all-start = ((bf16[16,8,2,16,128]{4,3,2,1,0:T(8,128)(2,1)}), bf16[16,8,2,16,128]{4,3,2,1,0:T(8,128)(2,1)S(1)}, u32[]{:S(2)}, u32[]{:S(2)}) async-start(bf16[16,8,2,16,128]{4,3,2,1,0:T(8,128)(2,1)} %bitcast.17), calls=%async_computation | async-start | bytes 2097152 | tf_op jit(solution)/shard_map/all_to_all | solution.py:226
  16.3 7.3 %copy-start.4 = (bf16[8,1152]{1,0:T(8,128)(2,1)S(1)}, bf16[8,1152]{1,0:T(8,128)(2,1)}, u32[]{:S(2)}) copy-start(bf16[8,1152]{1,0:T(8,128)(2,1)} %fusion.11.asked_ref.refs_0_) | copy-start | bytes 55300
  21.6 38.9 %collective-permute-start.3 = (bf16[1344,1024]{1,0:T(8,128)(2,1)}, bf16[1344,1024]{1,0:T(8,128)(2,1)}, u32[]{:S(2)}, u32[]{:S(2)}) collective-permute-start(bf16[1344,1024]{1,0:T(8,128)(2,1)} %pad_maximum_fusion), channel_id=1, source_target_pairs={{0,1},{1,0},{2,3},{3,2},{4,5},{5,4},{6,7},{7,6},{8,9},{9,8},{10,11... | collective-permute-start | bytes 8257544 | tf_op jit(solution)/shard_map/ppermute | solution.py:270
  23.6 20.0 %collective-permute-start = (bf16[8,1152]{1,0:T(8,128)(2,1)S(1)}, bf16[8,1152]{1,0:T(8,128)(2,1)S(1)}, u32[]{:S(2)}, u32[]{:S(2)}) collective-permute-start(bf16[8,1152]{1,0:T(8,128)(2,1)S(1)} %copy-done.4), channel_id=1, source_target_pairs={{0,16},{16,0},{32,48},{48,32},{1,17},{17,1},{33,49},{49,33},{2,18}... | collective-permute-start | bytes 55304 | tf_op jit(solution)/shard_map/ppermute | solution.py:206
  32.5 16.3 %collective-permute-start.1 = (bf16[8,1152]{1,0:T(8,128)(2,1)S(1)}, bf16[8,1152]{1,0:T(8,128)(2,1)S(1)}, u32[]{:S(2)}, u32[]{:S(2)}) collective-permute-start(bf16[8,1152]{1,0:T(8,128)(2,1)S(1)} %copy-done.4), channel_id=1, source_target_pairs={{0,32},{16,48},{32,0},{48,16},{1,33},{17,49},{33,1},{49,17},{2,34}... | collective-permute-start | bytes 55304 | tf_op jit(solution)/shard_map/ppermute | solution.py:206
  40.7 9.7 %collective-permute-start.2 = (bf16[8,1152]{1,0:T(8,128)(2,1)S(1)}, bf16[8,1152]{1,0:T(8,128)(2,1)S(1)}, u32[]{:S(2)}, u32[]{:S(2)}) collective-permute-start(bf16[8,1152]{1,0:T(8,128)(2,1)S(1)} %copy-done.4), channel_id=1, source_target_pairs={{0,48},{16,32},{32,16},{48,0},{1,49},{17,33},{33,17},{49,1},{2,50}... | collective-permute-start | bytes 55304 | tf_op jit(solution)/shard_map/ppermute | solution.py:206
  43.6 6.8 %copy-start.6 = (bf16[8,1152]{1,0:T(8,128)(2,1)}, bf16[8,1152]{1,0:T(8,128)(2,1)S(1)}, u32[]{:S(2)}) copy-start(bf16[8,1152]{1,0:T(8,128)(2,1)S(1)} %collective-permute-done.refs_1_) | copy-start | bytes 55300
  48.8 1.7 copy-start.7
  50.5 0.6 copy-start.8
  50.5 1.0 copy-start
  54.9 26.1 %all-to-all-start.1 = ((bf16[4,4,8,1152]{3,2,1,0:T(8,128)(2,1)}), bf16[4,4,8,1152]{3,2,1,0:T(8,128)(2,1)S(1)}, u32[]{:S(2)}, u32[]{:S(2)}) async-start(bf16[4,4,8,1152]{3,2,1,0:T(8,128)(2,1)} %shard_map.135), calls=%async_computation.1 | async-start | bytes 589824 | tf_op jit(solution)/shard_map/all_to_all | solution.py:253
  64.8 26.2 %copy-start.11 = (bf16[1024]{0:T(1024)(128)(2,1)S(1)}, bf16[1024]{0:T(1024)(128)(2,1)}, u32[]{:S(2)}) copy-start(bf16[1024]{0:T(1024)(128)(2,1)} %param.19) | copy-start | bytes 6148
  81.0 0.7 copy-start.3
  83.8 20.4 %all-to-all-start.2 = ((bf16[8,32,1024]{2,1,0:T(8,128)(2,1)}), bf16[8,32,1024]{2,1,0:T(8,128)(2,1)S(1)}, u32[]{:S(2)}, u32[]{:S(2)}) async-start(bf16[8,32,1024]{2,1,0:T(8,128)(2,1)} %get-tuple-element.27), calls=%async_computation.2 | async-start | bytes 1048576 | tf_op jit(solution)/shard_map/all_to_all | solution.py:296
  123.5 40.3 %copy-start.5 = (bf16[8,1024]{1,0:T(8,128)(2,1)S(1)}, bf16[8,1024]{1,0:T(8,128)(2,1)}, u32[]{:S(2)}) copy-start(bf16[8,1024]{1,0:T(8,128)(2,1)} %get-tuple-element.26) | copy-start | bytes 49156
  156.8 20.4 %all-to-all-start.6 = ((bf16[4,8,1024]{2,1,0:T(8,128)(2,1)}), bf16[4,8,1024]{2,1,0:T(8,128)(2,1)S(1)}, u32[]{:S(2)}, u32[]{:S(2)}) async-start(bf16[4,8,1024]{2,1,0:T(8,128)(2,1)} %bitcast.10), calls=%async_computation.6 | async-start | bytes 131072 | tf_op jit(solution)/shard_map/all_to_all | solution.py:35

commit v5 on v4

--- a/solution.py
+++ b/solution.py
@@ -236,6 +236,7 @@
         out_shape=(square, square, square),
         in_specs=[whole] * 4,
         out_specs=(whole, whole, whole),
+        compiler_params=pltpu.CompilerParams(vmem_limit_bytes=8 << 20),
         cost_estimate=pl.CostEstimate(
             flops=6 * queries_here * HD * pages_here * PAGE,
             bytes_accessed=2 * resident.size,
@@ -249,6 +250,7 @@
         out_shape=jax.ShapeDtypeStruct((far_count, far_count, tokens, width + HD), jnp.bfloat16),
         in_specs=[scalar] + [whole] * (far_count + 4),
         out_specs=whole,
+        compiler_params=pltpu.CompilerParams(vmem_limit_bytes=12 << 20),
     )(far, *asked, landed, *found)
     parts = lax.all_to_all(parts, "zhi", split_axis=0, concat_axis=0, tiled=True)
     parts, weights = lax.optimization_barrier((parts, weights))
@@ -260,6 +262,7 @@
         ),
         in_specs=[scalar, whole],
         out_specs=(whole, whole),
+        compiler_params=pltpu.CompilerParams(vmem_limit_bytes=6 << 20),
     )(far, parts)
     return copies, attended, weights
 

time: 179 us -> 172 us (0.961)
  Pallas kernels: 7.83 us -> 3.83 us
  local copies, waits for them, and re-layouts: 14.4 us -> 11.5 us
  waiting for transfers between devices: 45.4 us -> 47.9 us
    unnamed x35 -> x23, local copies, waits for them, and re-layouts: 8.27 us -> 6.6 us
  transfers between devices with their start and end apart: 8 -> 8, of which waited for: 5 -> 5; matrix products, arithmetic and copies ran while one was open for 8% -> 8% of each run, Pallas kernels for 3% -> 2%
where the time goes in v5:
time: 172 us; the launch traced here: 171 us
  starting transfers between devices  48.2 us (28%)
  waiting for transfers between devices  47.9 us (28%)
  blocking collectives  46.8 us (27%)
  local copies, waits for them, and re-layouts  11.5 us (7%)
  other arithmetic  6.56 us (4%)
  matrix products  5.63 us (3%)
  Pallas kernels  3.83 us (2%)
    all_to_all x2, blocking collectives, collect(): lax.all_to_all(parts, axes, split_axis=0, concat_axis=0, tiled=True)  36.1 us
    ppermute x3, starting transfers between devices, attention(): lax.ppermute(asked, 'zhi', [(i, i ^ flip) for i in range(far_count)])  19 us
    all_to_all x1, waiting for transfers between devices, mlp(): lax.all_to_all(copies, MID, split_axis=0, concat_axis=0, tiled=True)  13.5 us
    all_to_all x1, waiting for transfers between devices, attention(): lax.all_to_all(parts, 'zhi', split_axis=0, concat_axis=0, tiled=True)  13.2 us
    all_to_all x1, waiting for transfers between devices, collect(): lax.all_to_all(parts, axes, split_axis=0, concat_axis=0, tiled=True)  12.7 us
    all_to_all x1, blocking collectives, spread(): lax.all_to_all(copies, axes, split_axis=0, concat_axis=0, tiled=True)  10.8 us
    all_to_all x1, starting transfers between devices, attention(): lax.all_to_all(outgoing, NEAR, split_axis=0, concat_axis=0, tiled=True)  8.94 us
    ppermute x3, waiting for transfers between devices, attention(): lax.ppermute(asked, 'zhi', [(i, i ^ flip) for i in range(far_count)])  8.53 us
  transfers between devices with their start and end apart: 8, of which 5 were waited for; matrix products, arithmetic and copies ran while one was open for 8% of the time, Pallas kernels for 2%

profile of v5, /device:TPU:32, one launch (start us, length us, event | category | flops | bytes accessed | tf_op | source)
XLA Modules:
  0.0 171.4 jit_solution(2734542136784793557)
XLA Ops:
  0.6 0.0 copy-start.8
  0.7 1.0 convert_reduce_fusion.2
  1.7 0.7 fusion.18
  2.4 1.5 fusion.2
  3.9 1.2 copy.22
  5.1 8.9 %all-to-all-start = ((bf16[16,8,2,16,128]{4,3,2,1,0:T(8,128)(2,1)}), bf16[16,8,2,16,128]{4,3,2,1,0:T(8,128)(2,1)S(1)}, u32[]{:S(2)}, u32[]{:S(2)}) async-start(bf16[16,8,2,16,128]{4,3,2,1,0:T(8,128)(2,1)} %bitcast.17), calls=%async_computation | async-start | bytes 2097152 | tf_op jit(solution)/shard_map/all_to_all | solution.py:226
  14.0 0.1 clamp_multiply_fusion
  14.1 0.1 select_reduce_fusion
  14.3 0.1 broadcast_in_dim.67
  14.3 0.1 broadcast_in_dim_reshape.3.seen_ref
  14.5 0.1 slice_bitcast_fusion
  14.5 0.6 shard_map.134
  15.2 3.0 %pad_maximum_fusion = bf16[1344,1024]{1,0:T(8,128)(2,1)} fusion(bf16[448,1024]{1,0:T(8,128)(2,1)S(1)} %copy-done.1, bf16[448,1024]{1,0:T(8,128)(2,1)} %bitcast.32, bf16[448,1024]{1,0:T(8,128)(2,1)S(1)} %bitcast.31), kind=kLoop, calls=%fused_computation.1 | loop fusion | flops 8257536 | bytes 5505024 | tf_op jit(solution)/shard_map/concatenate | solution.py:273
  18.2 2.0 %collective-permute-start.3 = (bf16[1344,1024]{1,0:T(8,128)(2,1)}, bf16[1344,1024]{1,0:T(8,128)(2,1)}, u32[]{:S(2)}, u32[]{:S(2)}) collective-permute-start(bf16[1344,1024]{1,0:T(8,128)(2,1)} %pad_maximum_fusion), channel_id=1, source_target_pairs={{0,1},{1,0},{2,3},{3,2},{4,5},{5,4},{6,7},{7,6},{8,9},{9,8},{10,11... | collective-permute-start | bytes 8257544 | tf_op jit(solution)/shard_map/ppermute | solution.py:273
  20.2 8.8 %collective-permute-start = (bf16[8,1152]{1,0:T(8,128)(2,1)S(1)}, bf16[8,1152]{1,0:T(8,128)(2,1)S(1)}, u32[]{:S(2)}, u32[]{:S(2)}) collective-permute-start(bf16[8,1152]{1,0:T(8,128)(2,1)S(1)} %fusion.11.asked_ref.refs_0_), channel_id=1, source_target_pairs={{0,16},{16,0},{32,48},{48,32},{1,17},{17,1},{33,49},{49,33},{2,18}... | collective-permute-start | bytes 55304 | tf_op jit(solution)/shard_map/ppermute | solution.py:206
  29.0 8.2 %collective-permute-start.1 = (bf16[8,1152]{1,0:T(8,128)(2,1)S(1)}, bf16[8,1152]{1,0:T(8,128)(2,1)S(1)}, u32[]{:S(2)}, u32[]{:S(2)}) collective-permute-start(bf16[8,1152]{1,0:T(8,128)(2,1)S(1)} %fusion.11.asked_ref.refs_0_), channel_id=1, source_target_pairs={{0,32},{16,48},{32,0},{48,16},{1,33},{17,49},{33,1},{49,17},{2,34}... | collective-permute-start | bytes 55304 | tf_op jit(solution)/shard_map/ppermute | solution.py:206
  37.3 1.9 %collective-permute-start.2 = (bf16[8,1152]{1,0:T(8,128)(2,1)S(1)}, bf16[8,1152]{1,0:T(8,128)(2,1)S(1)}, u32[]{:S(2)}, u32[]{:S(2)}) collective-permute-start(bf16[8,1152]{1,0:T(8,128)(2,1)S(1)} %fusion.11.asked_ref.refs_0_), channel_id=1, source_target_pairs={{0,48},{16,32},{32,16},{48,0},{1,49},{17,33},{33,17},{49,1},{2,50}... | collective-permute-start | bytes 55304 | tf_op jit(solution)/shard_map/ppermute | solution.py:206
  39.2 1.0 constant_dynamic-update-slice_fusion.1
  40.2 0.0 collective-permute-done.refs_1_
  40.2 3.2 %collective-permute-done.1.refs_2_ = bf16[8,1152]{1,0:T(8,128)(2,1)S(1)} collective-permute-done((bf16[8,1152]{1,0:T(8,128)(2,1)S(1)}, bf16[8,1152]{1,0:T(8,128)(2,1)S(1)}, u32[]{:S(2)}, u32[]{:S(2)}) %collective-permute-start.1) | collective-permute-done | bytes 18464 | tf_op jit(solution)/shard_map/ppermute | solution.py:206
  43.4 5.3 %collective-permute-done.2.refs_3_ = bf16[8,1152]{1,0:T(8,128)(2,1)S(1)} collective-permute-done((bf16[8,1152]{1,0:T(8,128)(2,1)S(1)}, bf16[8,1152]{1,0:T(8,128)(2,1)S(1)}, u32[]{:S(2)}, u32[]{:S(2)}) %collective-permute-start.2) | collective-permute-done | bytes 18464 | tf_op jit(solution)/shard_map/ppermute | solution.py:206
  48.7 2.1 %shard_map.135 = bf16[4,4,8,1152]{3,2,1,0:T(8,128)(2,1)} custom-call(s32[1]{0:T(128)} %bitcast.far_ref, bf16[8,1152]{1,0:T(8,128)(2,1)S(1)} %fusion.11.asked_ref.refs_0_, bf16[8,1152]{1,0:T(8,128)(2,1)S(1)} %collective-permute-done.refs_1_, bf16[8,1152]{1,0:T(8,128)(2,1)S(1)} %collective-permute-done.1.refs_2_, ...), custom_call_target="tpu_custom_call" | custom-call | tf_op jit(solution)/shard_map/pallas_call | solution.py:248
  50.9 5.7 %all-to-all-start.1 = ((bf16[4,4,8,1152]{3,2,1,0:T(8,128)(2,1)}), bf16[4,4,8,1152]{3,2,1,0:T(8,128)(2,1)S(1)}, u32[]{:S(2)}, u32[]{:S(2)}) async-start(bf16[4,4,8,1152]{3,2,1,0:T(8,128)(2,1)} %shard_map.135), calls=%async_computation.1 | async-start | bytes 589824 | tf_op jit(solution)/shard_map/all_to_all | solution.py:255
  56.6 2.2 %slice_dynamic-update-slice_fusion.1 = bf16[1920,1024]{1,0:T(8,128)(2,1)} fusion(bf16[1920,1024]{1,0:T(8,128)(2,1)} %constant_dynamic-update-slice_fusion.1, bf16[1344,1024]{1,0:T(8,128)(2,1)} %collective-permute-done.3), kind=kLoop, calls=%fused_computation.13 | loop fusion | bytes 1835008
  58.8 2.2 %constant_dynamic-update-slice_fusion = bf16[1920,1024]{1,0:T(8,128)(2,1)} fusion(bf16[1920,1024]{1,0:T(8,128)(2,1)} %slice_dynamic-update-slice_fusion.1, bf16[1024,448]{0,1:T(8,128)(2,1)} %param.21), kind=kLoop, calls=%fused_computation.38 | loop fusion | bytes 1835008
  60.9 2.5 %fusion.20 = (bf16[448,1024]{1,0:T(8,128)(2,1)S(1)}, bf16[1920,1024]{1,0:T(8,128)(2,1)}) fusion(bf16[1344,1024]{1,0:T(8,128)(2,1)} %collective-permute-done.3, bf16[1920,1024]{1,0:T(8,128)(2,1)} %constant_dynamic-update-slice_fusion), kind=kLoop, calls=%fused_computation.56 | loop fusion | bytes 3670016 | tf_op jit(solution)/shard_map/slice | solution.py:276
  63.5 0.7 broadcast_dynamic-update-slice_fusion
  64.2 0.2 pad_maximum_fusion.1
  64.4 13.2 %all-to-all-done.1.parts_ref = bf16[4,4,8,1152]{3,2,1,0:T(8,128)(2,1)S(1)} async-done(((bf16[4,4,8,1152]{3,2,1,0:T(8,128)(2,1)}), bf16[4,4,8,1152]{3,2,1,0:T(8,128)(2,1)S(1)}, u32[]{:S(2)}, u32[]{:S(2)}) %all-to-all-start.1) | async-done | bytes 294944 | tf_op jit(solution)/shard_map/all_to_all | solution.py:255
  77.6 1.1 shard_map.136
  78.7 6.7 %all-to-all-start.2 = ((bf16[8,32,1024]{2,1,0:T(8,128)(2,1)}), bf16[8,32,1024]{2,1,0:T(8,128)(2,1)S(1)}, u32[]{:S(2)}, u32[]{:S(2)}) async-start(bf16[8,32,1024]{2,1,0:T(8,128)(2,1)} %get-tuple-element.27), calls=%async_computation.2 | async-start | bytes 1048576 | tf_op jit(solution)/shard_map/all_to_all | solution.py:299
  85.5 13.5 %all-to-all-done.2 = bf16[8,32,1024]{2,1,0:T(8,128)(2,1)S(1)} async-done(((bf16[8,32,1024]{2,1,0:T(8,128)(2,1)}), bf16[8,32,1024]{2,1,0:T(8,128)(2,1)S(1)}, u32[]{:S(2)}, u32[]{:S(2)}) %all-to-all-start.2) | async-done | bytes 524320 | tf_op jit(solution)/shard_map/all_to_all | solution.py:299
  99.0 0.2 multiply_reduce_fusion
  99.2 0.1 reduce_sum.62
  99.3 0.1 fusion.3
  99.4 3.5 %fusion.1 = bf16[256,1920]{1,0:T(8,128)(2,1)S(1)} fusion(bf16[256,1024]{1,0:T(8,128)(2,1)S(1)} %fusion.3, bf16[1920,1024]{1,0:T(8,128)(2,1)} %broadcast_dynamic-update-slice_fusion, bf16[256]{0:T(256)(128)(2,1)S(1)} %convert_element_type.118, bf16[256]{0:T(256)(128)(2,1)S(1)} %fusion.19, pred[1920]{0:T(1024)(128)(4,1)S(1)} %get-tuple-element.34, ...), kind=kOutput, calls=%fused_computation.4 | convolution fusion | flops 1007616000 | bytes 5444352 | tf_op jit(solution)/shard_map/dot_general | solution.py:284
  102.8 15.5 %all_to_all.35 = bf16[8,32,1920]{2,1,0:T(8,128)(2,1)S(1)} all-to-all(bf16[8,32,1920]{2,1,0:T(8,128)(2,1)S(1)} %bitcast.33), channel_id=1, replica_groups=mesh['ylo'=2,'x'=4,'zhi'=4,'zlo'=4,'yhi'=2,'core'=2] {'ylo','x'}, dimensions={0} | all-to-all | bytes 1966080 | tf_op jit(solution)/shard_map/all_to_all | solution.py:35
  118.3 0.1 convert_reduce_fusion
  118.5 0.2 fusion.15
  118.6 0.1 fusion.7
  118.8 10.8 %all_to_all.36 = bf16[8,32,896]{2,1,0:T(8,128)(2,1)S(1)} all-to-all(bf16[8,32,896]{2,1,0:T(8,128)(2,1)S(1)} %broadcast_in_dim.73), channel_id=1, replica_groups=mesh['ylo'=2,'x'=4,'zhi'=4,'zlo'=4,'yhi'=2,'core'=2] {'ylo','x'}, dimensions={0} | all-to-all | bytes 917504 | tf_op jit(solution)/shard_map/all_to_all | solution.py:30
  129.6 0.7 convolution_convert_fusion.1
  130.3 20.6 %all_to_all.37 = bf16[8,32,1024]{2,1,0:T(8,128)(2,1)S(1)} all-to-all(bf16[8,32,1024]{2,1,0:T(8,128)(2,1)S(1)} %bitcast.35), channel_id=1, replica_groups=mesh['ylo'=2,'x'=4,'zhi'=4,'zlo'=4,'yhi'=2,'core'=2] {'zlo','yhi'}, dimensions={0} | all-to-all | bytes 1048576 | tf_op jit(solution)/shard_map/all_to_all | solution.py:35
  150.9 0.7 reduce_sum.64
  151.6 5.8 %all-to-all-start.6 = ((bf16[4,8,1024]{2,1,0:T(8,128)(2,1)}), bf16[4,8,1024]{2,1,0:T(8,128)(2,1)S(1)}, u32[]{:S(2)}, u32[]{:S(2)}) async-start(bf16[4,8,1024]{2,1,0:T(8,128)(2,1)} %bitcast.10), calls=%async_computation.6 | async-start | bytes 131072 | tf_op jit(solution)/shard_map/all_to_all | solution.py:35
  157.4 0.6 reshape.132
  158.0 12.7 %all-to-all-done.6 = bf16[4,8,1024]{2,1,0:T(8,128)(2,1)S(1)} async-done(((bf16[4,8,1024]{2,1,0:T(8,128)(2,1)}), bf16[4,8,1024]{2,1,0:T(8,128)(2,1)S(1)}, u32[]{:S(2)}, u32[]{:S(2)}) %all-to-all-start.6) | async-done | bytes 65568 | tf_op jit(solution)/shard_map/all_to_all | solution.py:35
  170.8 0.6 reshape.137
  (33 shorter events, 0.2 us)
Async XLA Ops:
  0.6 13.4 %copy-start.8 = (s32[2]{0:T(128)S(1)}, s32[2]{0:T(128)}, u32[]{:S(2)}) copy-start(s32[2]{0:T(128)} %constant.69) | copy-start | bytes 28
  0.6 13.4 %copy-start.7 = (s32[2]{0:T(128)S(1)}, s32[2]{0:T(128)}, u32[]{:S(2)}) copy-start(s32[2]{0:T(128)} %param.18) | copy-start | bytes 28
  0.7 13.5 %copy-start.3 = (bf16[2,4,1024]{2,1,0:T(4,128)(2,1)S(1)}, bf16[2,4,1024]{2,1,0:T(4,128)(2,1)}, u32[]{:S(2)}) copy-start(bf16[2,4,1024]{2,1,0:T(4,128)(2,1)} %param.12) | copy-start | bytes 49156
  0.7 13.5 %copy-start.6 = (s32[2,64]{1,0:T(2,128)S(1)}, s32[2,64]{1,0:T(2,128)}, u32[]{:S(2)}) copy-start(s32[2,64]{1,0:T(2,128)} %param.17) | copy-start | bytes 1540
  0.7 13.8 %copy-start.4 = (bf16[2,4,2,128]{3,2,1,0:T(2,128)(2,1)S(1)}, bf16[2,4,2,128]{3,2,1,0:T(2,128)(2,1)}, u32[]{:S(2)}) copy-start(bf16[2,4,2,128]{3,2,1,0:T(2,128)(2,1)} %param.13) | copy-start | bytes 12292
  0.7 13.9 %copy-start = (bf16[64,2,16,128]{3,2,1,0:T(8,128)(2,1)S(1)}, bf16[64,2,16,128]{3,2,1,0:T(8,128)(2,1)}, u32[]{:S(2)}) copy-start(bf16[64,2,16,128]{3,2,1,0:T(8,128)(2,1)} %resident_ref.1) | copy-start | bytes 1572868
  0.7 14.4 %copy-start.2 = (bf16[1024,448]{0,1:T(8,128)(2,1)S(1)}, bf16[1024,448]{0,1:T(8,128)(2,1)}, u32[]{:S(2)}) copy-start(bf16[1024,448]{0,1:T(8,128)(2,1)} %param.20) | copy-start | bytes 2752516
  0.7 14.4 %copy-start.1 = (bf16[448,1024]{1,0:T(8,128)(2,1)S(1)}, bf16[448,1024]{1,0:T(8,128)(2,1)}, u32[]{:S(2)}) copy-start(bf16[448,1024]{1,0:T(8,128)(2,1)} %param.22) | copy-start | bytes 2752516
  5.1 43.7 %all-to-all-start = ((bf16[16,8,2,16,128]{4,3,2,1,0:T(8,128)(2,1)}), bf16[16,8,2,16,128]{4,3,2,1,0:T(8,128)(2,1)S(1)}, u32[]{:S(2)}, u32[]{:S(2)}) async-start(bf16[16,8,2,16,128]{4,3,2,1,0:T(8,128)(2,1)} %bitcast.17), calls=%async_computation | async-start | bytes 2097152 | tf_op jit(solution)/shard_map/all_to_all | solution.py:226
  18.2 38.4 %collective-permute-start.3 = (bf16[1344,1024]{1,0:T(8,128)(2,1)}, bf16[1344,1024]{1,0:T(8,128)(2,1)}, u32[]{:S(2)}, u32[]{:S(2)}) collective-permute-start(bf16[1344,1024]{1,0:T(8,128)(2,1)} %pad_maximum_fusion), channel_id=1, source_target_pairs={{0,1},{1,0},{2,3},{3,2},{4,5},{5,4},{6,7},{7,6},{8,9},{9,8},{10,11... | collective-permute-start | bytes 8257544 | tf_op jit(solution)/shard_map/ppermute | solution.py:273
  20.2 20.0 %collective-permute-start = (bf16[8,1152]{1,0:T(8,128)(2,1)S(1)}, bf16[8,1152]{1,0:T(8,128)(2,1)S(1)}, u32[]{:S(2)}, u32[]{:S(2)}) collective-permute-start(bf16[8,1152]{1,0:T(8,128)(2,1)S(1)} %fusion.11.asked_ref.refs_0_), channel_id=1, source_target_pairs={{0,16},{16,0},{32,48},{48,32},{1,17},{17,1},{33,49},{49,33},{2,18}... | collective-permute-start | bytes 55304 | tf_op jit(solution)/shard_map/ppermute | solution.py:206
  29.0 14.4 %collective-permute-start.1 = (bf16[8,1152]{1,0:T(8,128)(2,1)S(1)}, bf16[8,1152]{1,0:T(8,128)(2,1)S(1)}, u32[]{:S(2)}, u32[]{:S(2)}) collective-permute-start(bf16[8,1152]{1,0:T(8,128)(2,1)S(1)} %fusion.11.asked_ref.refs_0_), channel_id=1, source_target_pairs={{0,32},{16,48},{32,0},{48,16},{1,33},{17,49},{33,1},{49,17},{2,34}... | collective-permute-start | bytes 55304 | tf_op jit(solution)/shard_map/ppermute | solution.py:206
  37.3 11.5 %collective-permute-start.2 = (bf16[8,1152]{1,0:T(8,128)(2,1)S(1)}, bf16[8,1152]{1,0:T(8,128)(2,1)S(1)}, u32[]{:S(2)}, u32[]{:S(2)}) collective-permute-start(bf16[8,1152]{1,0:T(8,128)(2,1)S(1)} %fusion.11.asked_ref.refs_0_), channel_id=1, source_target_pairs={{0,48},{16,32},{32,16},{48,0},{1,49},{17,33},{33,17},{49,1},{2,50}... | collective-permute-start | bytes 55304 | tf_op jit(solution)/shard_map/ppermute | solution.py:206
  50.9 26.7 %all-to-all-start.1 = ((bf16[4,4,8,1152]{3,2,1,0:T(8,128)(2,1)}), bf16[4,4,8,1152]{3,2,1,0:T(8,128)(2,1)S(1)}, u32[]{:S(2)}, u32[]{:S(2)}) async-start(bf16[4,4,8,1152]{3,2,1,0:T(8,128)(2,1)} %shard_map.135), calls=%async_computation.1 | async-start | bytes 589824 | tf_op jit(solution)/shard_map/all_to_all | solution.py:255
  60.9 24.5 %copy-start.5 = (bf16[1024]{0:T(1024)(128)(2,1)S(1)}, bf16[1024]{0:T(1024)(128)(2,1)}, u32[]{:S(2)}) copy-start(bf16[1024]{0:T(1024)(128)(2,1)} %param.19) | copy-start | bytes 6148
  78.7 20.3 %all-to-all-start.2 = ((bf16[8,32,1024]{2,1,0:T(8,128)(2,1)}), bf16[8,32,1024]{2,1,0:T(8,128)(2,1)S(1)}, u32[]{:S(2)}, u32[]{:S(2)}) async-start(bf16[8,32,1024]{2,1,0:T(8,128)(2,1)} %get-tuple-element.27), calls=%async_computation.2 | async-start | bytes 1048576 | tf_op jit(solution)/shard_map/all_to_all | solution.py:299
  151.6 19.2 %all-to-all-start.6 = ((bf16[4,8,1024]{2,1,0:T(8,128)(2,1)}), bf16[4,8,1024]{2,1,0:T(8,128)(2,1)S(1)}, u32[]{:S(2)}, u32[]{:S(2)}) async-start(bf16[4,8,1024]{2,1,0:T(8,128)(2,1)} %bitcast.10), calls=%async_computation.6 | async-start | bytes 131072 | tf_op jit(solution)/shard_map/all_to_all | solution.py:35

commit v6 on v5

--- a/solution.py
+++ b/solution.py
@@ -209,19 +209,16 @@
     seen_here = jnp.repeat(seen[:pages_here], PAGE)[None, :]
 
     swap_count = swap_area.shape[0]
-    page_width = swap_area.shape[1] * swap_area.shape[2] * swap_area.shape[3]
     same = swap_dest[:, None] == swap_dest[None, :]
     earlier = jnp.arange(swap_count)[None, :] < jnp.arange(swap_count)[:, None]
     page_rank = jnp.sum((same & earlier).astype(jnp.int32), axis=1)
     send_slot = (swap_dest % near_count) * (far_count * CAP) + (
         swap_dest // near_count
     ) * CAP + page_rank
-    placement = (jnp.arange(owners * CAP, dtype=jnp.int32)[:, None] == send_slot[None, :]).astype(
-        jnp.bfloat16
-    )
-    outgoing = jnp.dot(
-        placement, swap_area.reshape(swap_count, page_width), preferred_element_type=jnp.float32
-    ).astype(jnp.bfloat16)
+    slots = jnp.arange(owners * CAP, dtype=jnp.int32)[:, None]
+    pages = jnp.arange(swap_count, dtype=jnp.int32)[None, :]
+    source = jnp.sum(jnp.where(slots == send_slot[None, :], pages, 0), axis=1)
+    outgoing = swap_area.at[source].get(mode="promise_in_bounds")
     outgoing = outgoing.reshape((near_count, far_count * CAP) + swap_area.shape[1:])
     landed = lax.all_to_all(outgoing, NEAR, split_axis=0, concat_axis=0, tiled=True)
 
@@ -271,39 +268,44 @@
     units, width = down_weight.shape
     gate, up = gate_weight.T, up_weight.T
     there = lax.ppermute(jnp.concatenate([gate, up, down_weight], axis=0), "core", SWAP)
-    gap = jnp.zeros((128, width), gate_weight.dtype)
-    wide = jnp.concatenate([gate, there[:units], up, there[units : 2 * units], gap], axis=0)
-    return wide, jnp.concatenate([down_weight, there[2 * units :]], axis=0)
-
-
-def gated_parts(tokens, norm_gain, weights, units):
+    own = jnp.concatenate([gate, up], axis=0)
+    down = jnp.concatenate([down_weight, there[2 * units :]], axis=0)
+    return own, there[: 2 * units], down
+
+
+def gated_parts(tokens, norm_gain, weights):
     wide = tokens.astype(jnp.float32)
     squares = jnp.sum(wide * wide, axis=1, keepdims=True)
     squares_high = squares.astype(jnp.bfloat16).astype(jnp.float32)
     normed = (wide * norm_gain.astype(jnp.float32)[None, :]).astype(jnp.bfloat16)
-    both = lax.dot_general(
-        normed, weights, (((1,), (1,)), ((), ())), preferred_element_type=jnp.float32
-    )
-    column = jnp.arange(both.shape[1], dtype=jnp.int32)[None, :]
-    both = jnp.where(column == 2 * units, squares_high, both)
-    both = jnp.where(column == 2 * units + 1, squares - squares_high, both)
-    return both.astype(jnp.bfloat16)
+    blocks = [
+        lax.dot_general(
+            normed, weight, (((1,), (1,)), ((), ())), preferred_element_type=jnp.float32
+        ).astype(jnp.bfloat16)
+        for weight in weights
+    ]
+    column = jnp.arange(128, dtype=jnp.int32)[None, :]
+    last = jnp.where(column == 0, squares_high, squares - squares_high).astype(jnp.bfloat16)
+    return jnp.concatenate(blocks + [last], axis=1)
 
 
 def mlp(copies, attended, norm_gain, weights, units):
-    wide_weight, down_weight = weights
+    *wide_weights, down_weight = weights
     tokens_here, width = attended.shape
     far = lax.axis_size("zhi")
     mid = lax.axis_size(MID)
     blk = lax.axis_size(BLK)
     own = lax.all_to_all(copies, MID, split_axis=0, concat_axis=0, tiled=True).reshape(-1, width)
-    parts = gated_parts(own, norm_gain, wide_weight, units)
+    parts = gated_parts(own, norm_gain, wide_weights)
     summed = collect(parts.reshape(blk, own.shape[0] // blk, parts.shape[1]), BLK)
-    square_sum = summed[:, 2 * units : 2 * units + 1] + summed[:, 2 * units + 1 : 2 * units + 2]
+    square_sum = summed[:, 4 * units : 4 * units + 1] + summed[:, 4 * units + 1 : 4 * units + 2]
     factor = lax.rsqrt(square_sum / (width * blk) + epsilon)
-    gate_sum = summed[:, :units]
-    up_sum = summed[:, units : 2 * units]
-    hidden = (jax.nn.silu(factor * gate_sum) * (factor * up_sum)).astype(jnp.bfloat16)
+    hidden = []
+    for first in (0, 2 * units):
+        gate_sum = summed[:, first : first + units]
+        up_sum = summed[:, first + units : first + 2 * units]
+        hidden.append((jax.nn.silu(factor * gate_sum) * (factor * up_sum)).astype(jnp.bfloat16))
+    hidden = jnp.concatenate(hidden, axis=1)
     hidden = spread(hidden, BLK)
     kept = jnp.dot(hidden, down_weight, preferred_element_type=jnp.float32).astype(jnp.bfloat16)
     kept = collect(kept.reshape(mid, far * tokens_here, width), MID).astype(jnp.bfloat16)
@@ -328,7 +330,7 @@
     copies, attended, weights = attention(
         queries, new_entries, resident, swap_area, swap_dest, page_table, lengths, weights
     )
-    units = 2 * gate_weight.shape[1]
+    units = gate_weight.shape[1]
     layer_out = mlp(copies, attended, norm_gain, weights, units)
     return attended.reshape(queries.shape), layer_out.reshape(queries.shape)
 

time: 172 us -> 171 us (level)
  other arithmetic: 6.56 us -> 10.9 us
  local copies, waits for them, and re-layouts: 11.5 us -> 7.57 us
  matrix products: 5.63 us -> 3.81 us
    unnamed x23 -> x25, local copies, waits for them, and re-layouts: 6.6 us -> 0.07 us
    concatenate x1 -> x4, other arithmetic: 0.22 us -> 4.16 us  [the longest x1 2.6 us: join_weights(): own = jnp.concatenate([gate, up], axis=0)]
    dot_general x2, matrix products: 4.92 us -> 3.1 us  [gated_parts(): lax.dot_general(normed, weight, (((1,), (1,)), ((), ())), preferred_eleme...]
    slice x1 -> x2, local copies, waits for them, and re-layouts: 2.54 us -> 4.19 us  [the longest x1 2.95 us: join_weights(): return (own, there[:2 * units], down)]
  transfers between devices with their start and end apart: 8 -> 8, of which waited for: 5 -> 5; matrix products, arithmetic and copies ran while one was open for 8% -> 7% of each run, Pallas kernels for 2% -> 2%
where the time goes in v6:
time: 171 us
  waiting for transfers between devices  48.3 us (28%)
  starting transfers between devices  47.6 us (28%)
  blocking collectives  47.5 us (28%)
  other arithmetic  10.9 us (6%)
  local copies, waits for them, and re-layouts  7.57 us (4%)
  Pallas kernels  3.89 us (2%)
  matrix products  3.81 us (2%)
    all_to_all x2, blocking collectives, collect(): lax.all_to_all(parts, axes, split_axis=0, concat_axis=0, tiled=True)  36.6 us
    ppermute x3, starting transfers between devices, attention(): lax.ppermute(asked, 'zhi', [(i, i ^ flip) for i in range(far_count)])  19 us
    all_to_all x1, waiting for transfers between devices, mlp(): lax.all_to_all(copies, MID, split_axis=0, concat_axis=0, tiled=True)  14.2 us
    all_to_all x1, waiting for transfers between devices, collect(): lax.all_to_all(parts, axes, split_axis=0, concat_axis=0, tiled=True)  12.7 us
    all_to_all x1, waiting for transfers between devices, attention(): lax.all_to_all(parts, 'zhi', split_axis=0, concat_axis=0, tiled=True)  12.1 us
    all_to_all x1, blocking collectives, spread(): lax.all_to_all(copies, axes, split_axis=0, concat_axis=0, tiled=True)  10.9 us
    ppermute x3, waiting for transfers between devices, attention(): lax.ppermute(asked, 'zhi', [(i, i ^ flip) for i in range(far_count)])  9.23 us
    all_to_all x1, starting transfers between devices, attention(): lax.all_to_all(outgoing, NEAR, split_axis=0, concat_axis=0, tiled=True)  9.07 us
  transfers between devices with their start and end apart: 8, of which 5 were waited for; matrix products, arithmetic and copies ran while one was open for 7% of the time, Pallas kernels for 2%

profile of v6, /device:TPU:32, one launch (start us, length us, event | category | flops | bytes accessed | tf_op | source)
XLA Modules:
  0.0 170.5 jit_solution(10390654933897633369)
XLA Ops:
  0.6 0.9 convert_reduce_fusion.2
  1.6 0.7 fusion.14
  2.2 0.1 select_reduce_fusion.1
  2.4 1.7 gather_fusion
  4.1 9.1 %all-to-all-start = ((bf16[16,8,2,16,128]{4,3,2,1,0:T(8,128)(2,1)}), bf16[16,8,2,16,128]{4,3,2,1,0:T(8,128)(2,1)S(1)}, u32[]{:S(2)}, u32[]{:S(2)}) async-start(bf16[16,8,2,16,128]{4,3,2,1,0:T(8,128)(2,1)} %bitcast.4), calls=%async_computation | async-start | bytes 2097152 | tf_op jit(solution)/shard_map/all_to_all | solution.py:223
  13.3 0.1 clamp_multiply_fusion
  13.3 0.1 select_reduce_fusion
  13.5 0.1 broadcast_in_dim.78
  13.5 0.1 broadcast_in_dim_reshape.3.seen_ref
  13.7 0.1 slice_bitcast_fusion
  13.8 0.6 shard_map.134
  14.3 3.3 %pad_maximum_fusion = bf16[1344,1024]{1,0:T(8,128)(2,1)} fusion(bf16[448,1024]{1,0:T(8,128)(2,1)} %param.22, bf16[448,1024]{1,0:T(8,128)(2,1)S(1)} %bitcast.28, bf16[448,1024]{1,0:T(8,128)(2,1)} %bitcast.30), kind=kLoop, calls=%fused_computation.1 | loop fusion | flops 8257536 | bytes 5505024 | tf_op jit(solution)/shard_map/concatenate | solution.py:270
  17.6 2.0 %collective-permute-start.3 = (bf16[1344,1024]{1,0:T(8,128)(2,1)}, bf16[1344,1024]{1,0:T(8,128)(2,1)}, u32[]{:S(2)}, u32[]{:S(2)}) collective-permute-start(bf16[1344,1024]{1,0:T(8,128)(2,1)} %pad_maximum_fusion), channel_id=1, source_target_pairs={{0,1},{1,0},{2,3},{3,2},{4,5},{5,4},{6,7},{7,6},{8,9},{9,8},{10,11... | collective-permute-start | bytes 8257544 | tf_op jit(solution)/shard_map/ppermute | solution.py:270
  19.7 8.8 %collective-permute-start = (bf16[8,1152]{1,0:T(8,128)(2,1)S(1)}, bf16[8,1152]{1,0:T(8,128)(2,1)S(1)}, u32[]{:S(2)}, u32[]{:S(2)}) collective-permute-start(bf16[8,1152]{1,0:T(8,128)(2,1)S(1)} %fusion.7.asked_ref.refs_0_), channel_id=1, source_target_pairs={{0,16},{16,0},{32,48},{48,32},{1,17},{17,1},{33,49},{49,33},{2,18}... | collective-permute-start | bytes 55304 | tf_op jit(solution)/shard_map/ppermute | solution.py:206
  28.5 8.2 %collective-permute-start.1 = (bf16[8,1152]{1,0:T(8,128)(2,1)S(1)}, bf16[8,1152]{1,0:T(8,128)(2,1)S(1)}, u32[]{:S(2)}, u32[]{:S(2)}) collective-permute-start(bf16[8,1152]{1,0:T(8,128)(2,1)S(1)} %fusion.7.asked_ref.refs_0_), channel_id=1, source_target_pairs={{0,32},{16,48},{32,0},{48,16},{1,33},{17,49},{33,1},{49,17},{2,34}... | collective-permute-start | bytes 55304 | tf_op jit(solution)/shard_map/ppermute | solution.py:206
  36.7 1.9 %collective-permute-start.2 = (bf16[8,1152]{1,0:T(8,128)(2,1)S(1)}, bf16[8,1152]{1,0:T(8,128)(2,1)S(1)}, u32[]{:S(2)}, u32[]{:S(2)}) collective-permute-start(bf16[8,1152]{1,0:T(8,128)(2,1)S(1)} %fusion.7.asked_ref.refs_0_), channel_id=1, source_target_pairs={{0,48},{16,32},{32,16},{48,0},{1,49},{17,33},{33,17},{49,1},{2,50}... | collective-permute-start | bytes 55304 | tf_op jit(solution)/shard_map/ppermute | solution.py:206
  38.7 4.2 %collective-permute-done.1.refs_2_ = bf16[8,1152]{1,0:T(8,128)(2,1)S(1)} collective-permute-done((bf16[8,1152]{1,0:T(8,128)(2,1)S(1)}, bf16[8,1152]{1,0:T(8,128)(2,1)S(1)}, u32[]{:S(2)}, u32[]{:S(2)}) %collective-permute-start.1) | collective-permute-done | bytes 18464 | tf_op jit(solution)/shard_map/ppermute | solution.py:206
  42.9 5.0 %collective-permute-done.2.refs_3_ = bf16[8,1152]{1,0:T(8,128)(2,1)S(1)} collective-permute-done((bf16[8,1152]{1,0:T(8,128)(2,1)S(1)}, bf16[8,1152]{1,0:T(8,128)(2,1)S(1)}, u32[]{:S(2)}, u32[]{:S(2)}) %collective-permute-start.2) | collective-permute-done | bytes 18464 | tf_op jit(solution)/shard_map/ppermute | solution.py:206
  47.9 2.1 %shard_map.135 = bf16[4,4,8,1152]{3,2,1,0:T(8,128)(2,1)} custom-call(s32[1]{0:T(128)} %bitcast.far_ref, bf16[8,1152]{1,0:T(8,128)(2,1)S(1)} %fusion.7.asked_ref.refs_0_, bf16[8,1152]{1,0:T(8,128)(2,1)S(1)} %collective-permute-done.refs_1_, bf16[8,1152]{1,0:T(8,128)(2,1)S(1)} %collective-permute-done.1.refs_2_, ...), custom_call_target="tpu_custom_call" | custom-call | tf_op jit(solution)/shard_map/pallas_call | solution.py:245
  50.1 5.7 %all-to-all-start.1 = ((bf16[4,4,8,1152]{3,2,1,0:T(8,128)(2,1)}), bf16[4,4,8,1152]{3,2,1,0:T(8,128)(2,1)S(1)}, u32[]{:S(2)}, u32[]{:S(2)}) async-start(bf16[4,4,8,1152]{3,2,1,0:T(8,128)(2,1)} %shard_map.135), calls=%async_computation.1 | async-start | bytes 589824 | tf_op jit(solution)/shard_map/all_to_all | solution.py:252
  55.8 2.6 %pad_maximum_fusion.1 = bf16[896,1024]{1,0:T(8,128)(2,1)} fusion(bf16[448,1024]{1,0:T(8,128)(2,1)S(1)} %bitcast.29, bf16[448,1024]{1,0:T(8,128)(2,1)} %bitcast.31), kind=kLoop, calls=%fused_computation.3 | loop fusion | flops 3670016 | bytes 3670016 | tf_op jit(solution)/shard_map/concatenate | solution.py:271
  58.4 1.2 slice.44
  59.6 3.0 %slice.43 = bf16[896,1024]{1,0:T(8,128)(2,1)} slice(bf16[1344,1024]{1,0:T(8,128)(2,1)} %collective-permute-done.3), slice={[0:896], [0:1024]} | slice | bytes 3670016 | tf_op jit(solution)/shard_map/slice | solution.py:273
  62.6 1.4 pad_maximum_fusion.2
  64.0 12.1 %all-to-all-done.1.parts_ref = bf16[4,4,8,1152]{3,2,1,0:T(8,128)(2,1)S(1)} async-done(((bf16[4,4,8,1152]{3,2,1,0:T(8,128)(2,1)}), bf16[4,4,8,1152]{3,2,1,0:T(8,128)(2,1)S(1)}, u32[]{:S(2)}, u32[]{:S(2)}) %all-to-all-start.1) | async-done | bytes 294944 | tf_op jit(solution)/shard_map/all_to_all | solution.py:252
  76.1 1.2 shard_map.136
  77.3 7.3 %all-to-all-start.2 = ((bf16[8,32,1024]{2,1,0:T(8,128)(2,1)}), bf16[8,32,1024]{2,1,0:T(8,128)(2,1)S(1)}, u32[]{:S(2)}, u32[]{:S(2)}) async-start(bf16[8,32,1024]{2,1,0:T(8,128)(2,1)} %get-tuple-element.28), calls=%async_computation.2 | async-start | bytes 1048576 | tf_op jit(solution)/shard_map/all_to_all | solution.py:298
  84.6 14.2 %all-to-all-done.2 = bf16[8,32,1024]{2,1,0:T(8,128)(2,1)S(1)} async-done(((bf16[8,32,1024]{2,1,0:T(8,128)(2,1)}), bf16[8,32,1024]{2,1,0:T(8,128)(2,1)S(1)}, u32[]{:S(2)}, u32[]{:S(2)}) %all-to-all-start.2) | async-done | bytes 524320 | tf_op jit(solution)/shard_map/all_to_all | solution.py:298
  98.8 0.2 multiply_reduce_fusion
  99.0 0.1 reduce_sum.75
  99.0 0.1 fusion
  99.2 2.4 %convolution_convert_fusion.2 = bf16[256,896]{1,0:T(8,128)(2,1)S(1)} fusion(bf16[256,1024]{1,0:T(8,128)(2,1)S(1)} %fusion, bf16[896,1024]{1,0:T(8,128)(2,1)} %pad_maximum_fusion.1), kind=kOutput, calls=%fused_computation.7 | convolution fusion | flops 469991424 | bytes 2818048 | tf_op jit(solution)/shard_map/dot_general | solution.py:282
  101.5 0.7 convolution_convert_fusion.1
  102.3 0.1 select_convert_fusion
  102.4 0.1 pad_maximum_fusion.3
  102.5 15.3 %all_to_all.35 = bf16[8,32,1920]{2,1,0:T(8,128)(2,1)S(1)} all-to-all(bf16[8,32,1920]{2,1,0:T(8,128)(2,1)S(1)} %bitcast.27), channel_id=1, replica_groups=mesh['ylo'=2,'x'=4,'zhi'=4,'zlo'=4,'yhi'=2,'core'=2] {'ylo','x'}, dimensions={0} | all-to-all | bytes 1966080 | tf_op jit(solution)/shard_map/all_to_all | solution.py:35
  117.8 0.1 convert_reduce_fusion
  117.9 0.2 fusion.11
  118.1 0.1 fusion.4
  118.2 0.1 pad_maximum_fusion.4
  118.3 10.9 %all_to_all.36 = bf16[8,32,896]{2,1,0:T(8,128)(2,1)S(1)} all-to-all(bf16[8,32,896]{2,1,0:T(8,128)(2,1)S(1)} %broadcast_in_dim.82), channel_id=1, replica_groups=mesh['ylo'=2,'x'=4,'zhi'=4,'zlo'=4,'yhi'=2,'core'=2] {'ylo','x'}, dimensions={0} | all-to-all | bytes 917504 | tf_op jit(solution)/shard_map/all_to_all | solution.py:30
  129.2 0.7 convolution_convert_fusion
  129.9 21.3 %all_to_all.37 = bf16[8,32,1024]{2,1,0:T(8,128)(2,1)S(1)} all-to-all(bf16[8,32,1024]{2,1,0:T(8,128)(2,1)S(1)} %bitcast.32), channel_id=1, replica_groups=mesh['ylo'=2,'x'=4,'zhi'=4,'zlo'=4,'yhi'=2,'core'=2] {'zlo','yhi'}, dimensions={0} | all-to-all | bytes 1048576 | tf_op jit(solution)/shard_map/all_to_all | solution.py:35
  151.3 0.7 reduce_sum.77
  152.0 4.5 %all-to-all-start.6 = ((bf16[4,8,1024]{2,1,0:T(8,128)(2,1)}), bf16[4,8,1024]{2,1,0:T(8,128)(2,1)S(1)}, u32[]{:S(2)}, u32[]{:S(2)}) async-start(bf16[4,8,1024]{2,1,0:T(8,128)(2,1)} %bitcast.13), calls=%async_computation.6 | async-start | bytes 131072 | tf_op jit(solution)/shard_map/all_to_all | solution.py:35
  156.5 0.6 reshape.136
  157.1 12.7 %all-to-all-done.6 = bf16[4,8,1024]{2,1,0:T(8,128)(2,1)S(1)} async-done(((bf16[4,8,1024]{2,1,0:T(8,128)(2,1)}), bf16[4,8,1024]{2,1,0:T(8,128)(2,1)S(1)}, u32[]{:S(2)}, u32[]{:S(2)}) %all-to-all-start.6) | async-done | bytes 65568 | tf_op jit(solution)/shard_map/all_to_all | solution.py:35
  169.9 0.6 reshape.141
  (43 shorter events, 0.2 us)
Async XLA Ops:
  0.6 1.7 %copy-start = (bf16[64,2,16,128]{3,2,1,0:T(8,128)(2,1)S(1)}, bf16[64,2,16,128]{3,2,1,0:T(8,128)(2,1)}, u32[]{:S(2)}) copy-start(bf16[64,2,16,128]{3,2,1,0:T(8,128)(2,1)} %param.15) | copy-start | bytes 1572868
  2.4 10.8 %copy-start.6 = (bf16[2,4,1024]{2,1,0:T(4,128)(2,1)S(1)}, bf16[2,4,1024]{2,1,0:T(4,128)(2,1)}, u32[]{:S(2)}) copy-start(bf16[2,4,1024]{2,1,0:T(4,128)(2,1)} %param.12) | copy-start | bytes 49156
  2.4 10.9 %copy-start.10 = (s32[2]{0:T(128)S(1)}, s32[2]{0:T(128)}, u32[]{:S(2)}) copy-start(s32[2]{0:T(128)} %param.18) | copy-start | bytes 28
  2.4 10.9 %copy-start.11 = (s32[2]{0:T(128)S(1)}, s32[2]{0:T(128)}, u32[]{:S(2)}) copy-start(s32[2]{0:T(128)} %constant.69) | copy-start | bytes 28
  2.4 10.9 %copy-start.9 = (s32[2,64]{1,0:T(2,128)S(1)}, s32[2,64]{1,0:T(2,128)}, u32[]{:S(2)}) copy-start(s32[2,64]{1,0:T(2,128)} %param.17) | copy-start | bytes 1540
  2.4 11.2 %copy-start.7 = (bf16[2,4,2,128]{3,2,1,0:T(2,128)(2,1)S(1)}, bf16[2,4,2,128]{3,2,1,0:T(2,128)(2,1)}, u32[]{:S(2)}) copy-start(bf16[2,4,2,128]{3,2,1,0:T(2,128)(2,1)} %param.13) | copy-start | bytes 12292
  2.4 11.3 %copy-start.1 = (bf16[64,2,16,128]{3,2,1,0:T(8,128)(2,1)S(1)}, bf16[64,2,16,128]{3,2,1,0:T(8,128)(2,1)}, u32[]{:S(2)}) copy-start(bf16[64,2,16,128]{3,2,1,0:T(8,128)(2,1)} %resident_ref.1) | copy-start | bytes 1572868
  4.1 10.2 %copy-start.2 = (bf16[1024,448]{0,1:T(8,128)(2,1)S(1)}, bf16[1024,448]{0,1:T(8,128)(2,1)}, u32[]{:S(2)}) copy-start(bf16[1024,448]{0,1:T(8,128)(2,1)} %param.21) | copy-start | bytes 2752516
  4.1 43.8 %all-to-all-start = ((bf16[16,8,2,16,128]{4,3,2,1,0:T(8,128)(2,1)}), bf16[16,8,2,16,128]{4,3,2,1,0:T(8,128)(2,1)S(1)}, u32[]{:S(2)}, u32[]{:S(2)}) async-start(bf16[16,8,2,16,128]{4,3,2,1,0:T(8,128)(2,1)} %bitcast.4), calls=%async_computation | async-start | bytes 2097152 | tf_op jit(solution)/shard_map/all_to_all | solution.py:223
  17.6 40.7 %collective-permute-start.3 = (bf16[1344,1024]{1,0:T(8,128)(2,1)}, bf16[1344,1024]{1,0:T(8,128)(2,1)}, u32[]{:S(2)}, u32[]{:S(2)}) collective-permute-start(bf16[1344,1024]{1,0:T(8,128)(2,1)} %pad_maximum_fusion), channel_id=1, source_target_pairs={{0,1},{1,0},{2,3},{3,2},{4,5},{5,4},{6,7},{7,6},{8,9},{9,8},{10,11... | collective-permute-start | bytes 8257544 | tf_op jit(solution)/shard_map/ppermute | solution.py:270
  19.7 19.0 %collective-permute-start = (bf16[8,1152]{1,0:T(8,128)(2,1)S(1)}, bf16[8,1152]{1,0:T(8,128)(2,1)S(1)}, u32[]{:S(2)}, u32[]{:S(2)}) collective-permute-start(bf16[8,1152]{1,0:T(8,128)(2,1)S(1)} %fusion.7.asked_ref.refs_0_), channel_id=1, source_target_pairs={{0,16},{16,0},{32,48},{48,32},{1,17},{17,1},{33,49},{49,33},{2,18}... | collective-permute-start | bytes 55304 | tf_op jit(solution)/shard_map/ppermute | solution.py:206
  28.5 14.4 %collective-permute-start.1 = (bf16[8,1152]{1,0:T(8,128)(2,1)S(1)}, bf16[8,1152]{1,0:T(8,128)(2,1)S(1)}, u32[]{:S(2)}, u32[]{:S(2)}) collective-permute-start(bf16[8,1152]{1,0:T(8,128)(2,1)S(1)} %fusion.7.asked_ref.refs_0_), channel_id=1, source_target_pairs={{0,32},{16,48},{32,0},{48,16},{1,33},{17,49},{33,1},{49,17},{2,34}... | collective-permute-start | bytes 55304 | tf_op jit(solution)/shard_map/ppermute | solution.py:206
  36.7 11.2 %collective-permute-start.2 = (bf16[8,1152]{1,0:T(8,128)(2,1)S(1)}, bf16[8,1152]{1,0:T(8,128)(2,1)S(1)}, u32[]{:S(2)}, u32[]{:S(2)}) collective-permute-start(bf16[8,1152]{1,0:T(8,128)(2,1)S(1)} %fusion.7.asked_ref.refs_0_), channel_id=1, source_target_pairs={{0,48},{16,32},{32,16},{48,0},{1,49},{17,33},{33,17},{49,1},{2,50}... | collective-permute-start | bytes 55304 | tf_op jit(solution)/shard_map/ppermute | solution.py:206
  50.1 26.0 %all-to-all-start.1 = ((bf16[4,4,8,1152]{3,2,1,0:T(8,128)(2,1)}), bf16[4,4,8,1152]{3,2,1,0:T(8,128)(2,1)S(1)}, u32[]{:S(2)}, u32[]{:S(2)}) async-start(bf16[4,4,8,1152]{3,2,1,0:T(8,128)(2,1)} %shard_map.135), calls=%async_computation.1 | async-start | bytes 589824 | tf_op jit(solution)/shard_map/all_to_all | solution.py:252
  59.6 3.0 %copy-start.3 = (bf16[448,1024]{1,0:T(8,128)(2,1)S(1)}, bf16[448,1024]{1,0:T(8,128)(2,1)}, u32[]{:S(2)}) copy-start(bf16[448,1024]{1,0:T(8,128)(2,1)} %param.22) | copy-start | bytes 2752516
  62.6 22.0 %copy-start.8 = (bf16[1024]{0:T(1024)(128)(2,1)S(1)}, bf16[1024]{0:T(1024)(128)(2,1)}, u32[]{:S(2)}) copy-start(bf16[1024]{0:T(1024)(128)(2,1)} %param.19) | copy-start | bytes 6148
  77.3 21.5 %all-to-all-start.2 = ((bf16[8,32,1024]{2,1,0:T(8,128)(2,1)}), bf16[8,32,1024]{2,1,0:T(8,128)(2,1)S(1)}, u32[]{:S(2)}, u32[]{:S(2)}) async-start(bf16[8,32,1024]{2,1,0:T(8,128)(2,1)} %get-tuple-element.28), calls=%async_computation.2 | async-start | bytes 1048576 | tf_op jit(solution)/shard_map/all_to_all | solution.py:298
  99.0 2.5 %copy-start.5 = (bf16[896,1024]{1,0:T(8,128)(2,1)S(1)}, bf16[896,1024]{1,0:T(8,128)(2,1)}, u32[]{:S(2)}) copy-start(bf16[896,1024]{1,0:T(8,128)(2,1)} %slice.43) | copy-start | bytes 5505028
  117.8 11.5 %copy-start.4 = (bf16[896,1024]{1,0:T(8,128)(2,1)S(1)}, bf16[896,1024]{1,0:T(8,128)(2,1)}, u32[]{:S(2)}) copy-start(bf16[896,1024]{1,0:T(8,128)(2,1)} %pad_maximum_fusion.2) | copy-start | bytes 5505028
  152.0 17.9 %all-to-all-start.6 = ((bf16[4,8,1024]{2,1,0:T(8,128)(2,1)}), bf16[4,8,1024]{2,1,0:T(8,128)(2,1)S(1)}, u32[]{:S(2)}, u32[]{:S(2)}) async-start(bf16[4,8,1024]{2,1,0:T(8,128)(2,1)} %bitcast.13), calls=%async_computation.6 | async-start | bytes 131072 | tf_op jit(solution)/shard_map/all_to_all | solution.py:35

commit v7 on v6

--- a/solution.py
+++ b/solution.py
@@ -233,7 +233,7 @@
         out_shape=(square, square, square),
         in_specs=[whole] * 4,
         out_specs=(whole, whole, whole),
-        compiler_params=pltpu.CompilerParams(vmem_limit_bytes=8 << 20),
+        compiler_params=pltpu.CompilerParams(vmem_limit_bytes=4 << 20),
         cost_estimate=pl.CostEstimate(
             flops=6 * queries_here * HD * pages_here * PAGE,
             bytes_accessed=2 * resident.size,
@@ -247,7 +247,7 @@
         out_shape=jax.ShapeDtypeStruct((far_count, far_count, tokens, width + HD), jnp.bfloat16),
         in_specs=[scalar] + [whole] * (far_count + 4),
         out_specs=whole,
-        compiler_params=pltpu.CompilerParams(vmem_limit_bytes=12 << 20),
+        compiler_params=pltpu.CompilerParams(vmem_limit_bytes=6 << 20),
     )(far, *asked, landed, *found)
     parts = lax.all_to_all(parts, "zhi", split_axis=0, concat_axis=0, tiled=True)
     parts, weights = lax.optimization_barrier((parts, weights))

time: 171 us -> 171 us (level)
  no operation moved by 1% of the time
where the time goes in v7:
time: 171 us
  waiting for transfers between devices  49.1 us (29%)
  starting transfers between devices  47.5 us (28%)
  blocking collectives  46.7 us (27%)
  other arithmetic  10.9 us (6%)
  local copies, waits for them, and re-layouts  7.57 us (4%)
  Pallas kernels  3.89 us (2%)
  matrix products  3.81 us (2%)
    all_to_all x2, blocking collectives, collect(): lax.all_to_all(parts, axes, split_axis=0, concat_axis=0, tiled=True)  35.9 us
    ppermute x3, starting transfers between devices, attention(): lax.ppermute(asked, 'zhi', [(i, i ^ flip) for i in range(far_count)])  19 us
    all_to_all x1, waiting for transfers between devices, mlp(): lax.all_to_all(copies, MID, split_axis=0, concat_axis=0, tiled=True)  14 us
    all_to_all x1, waiting for transfers between devices, attention(): lax.all_to_all(parts, 'zhi', split_axis=0, concat_axis=0, tiled=True)  13.1 us
    all_to_all x1, waiting for transfers between devices, collect(): lax.all_to_all(parts, axes, split_axis=0, concat_axis=0, tiled=True)  12.7 us
    all_to_all x1, blocking collectives, spread(): lax.all_to_all(copies, axes, split_axis=0, concat_axis=0, tiled=True)  10.9 us
    ppermute x3, waiting for transfers between devices, attention(): lax.ppermute(asked, 'zhi', [(i, i ^ flip) for i in range(far_count)])  9.23 us
    all_to_all x1, starting transfers between devices, attention(): lax.all_to_all(outgoing, NEAR, split_axis=0, concat_axis=0, tiled=True)  9.08 us
  transfers between devices with their start and end apart: 8, of which 5 were waited for; matrix products, arithmetic and copies ran while one was open for 7% of the time, Pallas kernels for 2%

profile of v7, /device:TPU:32, one launch (start us, length us, event | category | flops | bytes accessed | tf_op | source)
XLA Modules:
  0.0 170.5 jit_solution(10390654933897633369)
XLA Ops:
  0.6 0.9 convert_reduce_fusion.2
  1.6 0.7 fusion.14
  2.2 0.1 select_reduce_fusion.1
  2.4 1.7 gather_fusion
  4.1 9.1 %all-to-all-start = ((bf16[16,8,2,16,128]{4,3,2,1,0:T(8,128)(2,1)}), bf16[16,8,2,16,128]{4,3,2,1,0:T(8,128)(2,1)S(1)}, u32[]{:S(2)}, u32[]{:S(2)}) async-start(bf16[16,8,2,16,128]{4,3,2,1,0:T(8,128)(2,1)} %bitcast.4), calls=%async_computation | async-start | bytes 2097152 | tf_op jit(solution)/shard_map/all_to_all | solution.py:223
  13.3 0.1 clamp_multiply_fusion
  13.3 0.1 select_reduce_fusion
  13.5 0.1 broadcast_in_dim.78
  13.5 0.1 broadcast_in_dim_reshape.3.seen_ref
  13.7 0.1 slice_bitcast_fusion
  13.8 0.6 shard_map.134
  14.3 3.3 %pad_maximum_fusion = bf16[1344,1024]{1,0:T(8,128)(2,1)} fusion(bf16[448,1024]{1,0:T(8,128)(2,1)} %param.22, bf16[448,1024]{1,0:T(8,128)(2,1)S(1)} %bitcast.28, bf16[448,1024]{1,0:T(8,128)(2,1)} %bitcast.30), kind=kLoop, calls=%fused_computation.1 | loop fusion | flops 8257536 | bytes 5505024 | tf_op jit(solution)/shard_map/concatenate | solution.py:270
  17.6 2.0 %collective-permute-start.3 = (bf16[1344,1024]{1,0:T(8,128)(2,1)}, bf16[1344,1024]{1,0:T(8,128)(2,1)}, u32[]{:S(2)}, u32[]{:S(2)}) collective-permute-start(bf16[1344,1024]{1,0:T(8,128)(2,1)} %pad_maximum_fusion), channel_id=1, source_target_pairs={{0,1},{1,0},{2,3},{3,2},{4,5},{5,4},{6,7},{7,6},{8,9},{9,8},{10,11... | collective-permute-start | bytes 8257544 | tf_op jit(solution)/shard_map/ppermute | solution.py:270
  19.7 8.8 %collective-permute-start = (bf16[8,1152]{1,0:T(8,128)(2,1)S(1)}, bf16[8,1152]{1,0:T(8,128)(2,1)S(1)}, u32[]{:S(2)}, u32[]{:S(2)}) collective-permute-start(bf16[8,1152]{1,0:T(8,128)(2,1)S(1)} %fusion.7.asked_ref.refs_0_), channel_id=1, source_target_pairs={{0,16},{16,0},{32,48},{48,32},{1,17},{17,1},{33,49},{49,33},{2,18}... | collective-permute-start | bytes 55304 | tf_op jit(solution)/shard_map/ppermute | solution.py:206
  28.5 8.2 %collective-permute-start.1 = (bf16[8,1152]{1,0:T(8,128)(2,1)S(1)}, bf16[8,1152]{1,0:T(8,128)(2,1)S(1)}, u32[]{:S(2)}, u32[]{:S(2)}) collective-permute-start(bf16[8,1152]{1,0:T(8,128)(2,1)S(1)} %fusion.7.asked_ref.refs_0_), channel_id=1, source_target_pairs={{0,32},{16,48},{32,0},{48,16},{1,33},{17,49},{33,1},{49,17},{2,34}... | collective-permute-start | bytes 55304 | tf_op jit(solution)/shard_map/ppermute | solution.py:206
  36.8 1.9 %collective-permute-start.2 = (bf16[8,1152]{1,0:T(8,128)(2,1)S(1)}, bf16[8,1152]{1,0:T(8,128)(2,1)S(1)}, u32[]{:S(2)}, u32[]{:S(2)}) collective-permute-start(bf16[8,1152]{1,0:T(8,128)(2,1)S(1)} %fusion.7.asked_ref.refs_0_), channel_id=1, source_target_pairs={{0,48},{16,32},{32,16},{48,0},{1,49},{17,33},{33,17},{49,1},{2,50}... | collective-permute-start | bytes 55304 | tf_op jit(solution)/shard_map/ppermute | solution.py:206
  38.7 4.2 %collective-permute-done.1.refs_2_ = bf16[8,1152]{1,0:T(8,128)(2,1)S(1)} collective-permute-done((bf16[8,1152]{1,0:T(8,128)(2,1)S(1)}, bf16[8,1152]{1,0:T(8,128)(2,1)S(1)}, u32[]{:S(2)}, u32[]{:S(2)}) %collective-permute-start.1) | collective-permute-done | bytes 18464 | tf_op jit(solution)/shard_map/ppermute | solution.py:206
  42.9 5.0 %collective-permute-done.2.refs_3_ = bf16[8,1152]{1,0:T(8,128)(2,1)S(1)} collective-permute-done((bf16[8,1152]{1,0:T(8,128)(2,1)S(1)}, bf16[8,1152]{1,0:T(8,128)(2,1)S(1)}, u32[]{:S(2)}, u32[]{:S(2)}) %collective-permute-start.2) | collective-permute-done | bytes 18464 | tf_op jit(solution)/shard_map/ppermute | solution.py:206
  47.9 2.1 %shard_map.135 = bf16[4,4,8,1152]{3,2,1,0:T(8,128)(2,1)} custom-call(s32[1]{0:T(128)} %bitcast.far_ref, bf16[8,1152]{1,0:T(8,128)(2,1)S(1)} %fusion.7.asked_ref.refs_0_, bf16[8,1152]{1,0:T(8,128)(2,1)S(1)} %collective-permute-done.refs_1_, bf16[8,1152]{1,0:T(8,128)(2,1)S(1)} %collective-permute-done.1.refs_2_, ...), custom_call_target="tpu_custom_call" | custom-call | tf_op jit(solution)/shard_map/pallas_call | solution.py:245
  50.1 5.7 %all-to-all-start.1 = ((bf16[4,4,8,1152]{3,2,1,0:T(8,128)(2,1)}), bf16[4,4,8,1152]{3,2,1,0:T(8,128)(2,1)S(1)}, u32[]{:S(2)}, u32[]{:S(2)}) async-start(bf16[4,4,8,1152]{3,2,1,0:T(8,128)(2,1)} %shard_map.135), calls=%async_computation.1 | async-start | bytes 589824 | tf_op jit(solution)/shard_map/all_to_all | solution.py:252
  55.8 2.6 %pad_maximum_fusion.1 = bf16[896,1024]{1,0:T(8,128)(2,1)} fusion(bf16[448,1024]{1,0:T(8,128)(2,1)S(1)} %bitcast.29, bf16[448,1024]{1,0:T(8,128)(2,1)} %bitcast.31), kind=kLoop, calls=%fused_computation.3 | loop fusion | flops 3670016 | bytes 3670016 | tf_op jit(solution)/shard_map/concatenate | solution.py:271
  58.4 1.2 slice.44
  59.6 3.0 %slice.43 = bf16[896,1024]{1,0:T(8,128)(2,1)} slice(bf16[1344,1024]{1,0:T(8,128)(2,1)} %collective-permute-done.3), slice={[0:896], [0:1024]} | slice | bytes 3670016 | tf_op jit(solution)/shard_map/slice | solution.py:273
  62.6 1.4 pad_maximum_fusion.2
  64.0 13.1 %all-to-all-done.1.parts_ref = bf16[4,4,8,1152]{3,2,1,0:T(8,128)(2,1)S(1)} async-done(((bf16[4,4,8,1152]{3,2,1,0:T(8,128)(2,1)}), bf16[4,4,8,1152]{3,2,1,0:T(8,128)(2,1)S(1)}, u32[]{:S(2)}, u32[]{:S(2)}) %all-to-all-start.1) | async-done | bytes 294944 | tf_op jit(solution)/shard_map/all_to_all | solution.py:252
  77.0 1.2 shard_map.136
  78.2 6.4 %all-to-all-start.2 = ((bf16[8,32,1024]{2,1,0:T(8,128)(2,1)}), bf16[8,32,1024]{2,1,0:T(8,128)(2,1)S(1)}, u32[]{:S(2)}, u32[]{:S(2)}) async-start(bf16[8,32,1024]{2,1,0:T(8,128)(2,1)} %get-tuple-element.28), calls=%async_computation.2 | async-start | bytes 1048576 | tf_op jit(solution)/shard_map/all_to_all | solution.py:298
  84.6 14.0 %all-to-all-done.2 = bf16[8,32,1024]{2,1,0:T(8,128)(2,1)S(1)} async-done(((bf16[8,32,1024]{2,1,0:T(8,128)(2,1)}), bf16[8,32,1024]{2,1,0:T(8,128)(2,1)S(1)}, u32[]{:S(2)}, u32[]{:S(2)}) %all-to-all-start.2) | async-done | bytes 524320 | tf_op jit(solution)/shard_map/all_to_all | solution.py:298
  98.6 0.2 multiply_reduce_fusion
  98.8 0.1 reduce_sum.75
  98.9 0.1 fusion
  99.0 2.4 %convolution_convert_fusion.2 = bf16[256,896]{1,0:T(8,128)(2,1)S(1)} fusion(bf16[256,1024]{1,0:T(8,128)(2,1)S(1)} %fusion, bf16[896,1024]{1,0:T(8,128)(2,1)} %pad_maximum_fusion.1), kind=kOutput, calls=%fused_computation.7 | convolution fusion | flops 469991424 | bytes 2818048 | tf_op jit(solution)/shard_map/dot_general | solution.py:282
  101.4 0.7 convolution_convert_fusion.1
  102.2 0.1 select_convert_fusion
  102.3 0.1 pad_maximum_fusion.3
  102.4 15.3 %all_to_all.35 = bf16[8,32,1920]{2,1,0:T(8,128)(2,1)S(1)} all-to-all(bf16[8,32,1920]{2,1,0:T(8,128)(2,1)S(1)} %bitcast.27), channel_id=1, replica_groups=mesh['ylo'=2,'x'=4,'zhi'=4,'zlo'=4,'yhi'=2,'core'=2] {'ylo','x'}, dimensions={0} | all-to-all | bytes 1966080 | tf_op jit(solution)/shard_map/all_to_all | solution.py:35
  117.6 0.1 convert_reduce_fusion
  117.8 0.2 fusion.11
  118.0 0.1 fusion.4
  118.1 0.1 pad_maximum_fusion.4
  118.2 10.9 %all_to_all.36 = bf16[8,32,896]{2,1,0:T(8,128)(2,1)S(1)} all-to-all(bf16[8,32,896]{2,1,0:T(8,128)(2,1)S(1)} %broadcast_in_dim.82), channel_id=1, replica_groups=mesh['ylo'=2,'x'=4,'zhi'=4,'zlo'=4,'yhi'=2,'core'=2] {'ylo','x'}, dimensions={0} | all-to-all | bytes 917504 | tf_op jit(solution)/shard_map/all_to_all | solution.py:30
  129.1 0.7 convolution_convert_fusion
  129.8 20.6 %all_to_all.37 = bf16[8,32,1024]{2,1,0:T(8,128)(2,1)S(1)} all-to-all(bf16[8,32,1024]{2,1,0:T(8,128)(2,1)S(1)} %bitcast.32), channel_id=1, replica_groups=mesh['ylo'=2,'x'=4,'zhi'=4,'zlo'=4,'yhi'=2,'core'=2] {'zlo','yhi'}, dimensions={0} | all-to-all | bytes 1048576 | tf_op jit(solution)/shard_map/all_to_all | solution.py:35
  150.4 0.7 reduce_sum.77
  151.1 5.4 %all-to-all-start.6 = ((bf16[4,8,1024]{2,1,0:T(8,128)(2,1)}), bf16[4,8,1024]{2,1,0:T(8,128)(2,1)S(1)}, u32[]{:S(2)}, u32[]{:S(2)}) async-start(bf16[4,8,1024]{2,1,0:T(8,128)(2,1)} %bitcast.13), calls=%async_computation.6 | async-start | bytes 131072 | tf_op jit(solution)/shard_map/all_to_all | solution.py:35
  156.5 0.6 reshape.136
  157.1 12.7 %all-to-all-done.6 = bf16[4,8,1024]{2,1,0:T(8,128)(2,1)S(1)} async-done(((bf16[4,8,1024]{2,1,0:T(8,128)(2,1)}), bf16[4,8,1024]{2,1,0:T(8,128)(2,1)S(1)}, u32[]{:S(2)}, u32[]{:S(2)}) %all-to-all-start.6) | async-done | bytes 65568 | tf_op jit(solution)/shard_map/all_to_all | solution.py:35
  169.9 0.6 reshape.141
  (43 shorter events, 0.2 us)
Async XLA Ops:
  0.6 1.7 %copy-start = (bf16[64,2,16,128]{3,2,1,0:T(8,128)(2,1)S(1)}, bf16[64,2,16,128]{3,2,1,0:T(8,128)(2,1)}, u32[]{:S(2)}) copy-start(bf16[64,2,16,128]{3,2,1,0:T(8,128)(2,1)} %param.15) | copy-start | bytes 1572868
  2.4 10.8 %copy-start.6 = (bf16[2,4,1024]{2,1,0:T(4,128)(2,1)S(1)}, bf16[2,4,1024]{2,1,0:T(4,128)(2,1)}, u32[]{:S(2)}) copy-start(bf16[2,4,1024]{2,1,0:T(4,128)(2,1)} %param.12) | copy-start | bytes 49156
  2.4 10.9 %copy-start.10 = (s32[2]{0:T(128)S(1)}, s32[2]{0:T(128)}, u32[]{:S(2)}) copy-start(s32[2]{0:T(128)} %param.18) | copy-start | bytes 28
  2.4 10.9 %copy-start.11 = (s32[2]{0:T(128)S(1)}, s32[2]{0:T(128)}, u32[]{:S(2)}) copy-start(s32[2]{0:T(128)} %constant.69) | copy-start | bytes 28
  2.4 10.9 %copy-start.9 = (s32[2,64]{1,0:T(2,128)S(1)}, s32[2,64]{1,0:T(2,128)}, u32[]{:S(2)}) copy-start(s32[2,64]{1,0:T(2,128)} %param.17) | copy-start | bytes 1540
  2.4 11.2 %copy-start.7 = (bf16[2,4,2,128]{3,2,1,0:T(2,128)(2,1)S(1)}, bf16[2,4,2,128]{3,2,1,0:T(2,128)(2,1)}, u32[]{:S(2)}) copy-start(bf16[2,4,2,128]{3,2,1,0:T(2,128)(2,1)} %param.13) | copy-start | bytes 12292
  2.4 11.3 %copy-start.1 = (bf16[64,2,16,128]{3,2,1,0:T(8,128)(2,1)S(1)}, bf16[64,2,16,128]{3,2,1,0:T(8,128)(2,1)}, u32[]{:S(2)}) copy-start(bf16[64,2,16,128]{3,2,1,0:T(8,128)(2,1)} %resident_ref.1) | copy-start | bytes 1572868
  4.1 10.2 %copy-start.2 = (bf16[1024,448]{0,1:T(8,128)(2,1)S(1)}, bf16[1024,448]{0,1:T(8,128)(2,1)}, u32[]{:S(2)}) copy-start(bf16[1024,448]{0,1:T(8,128)(2,1)} %param.21) | copy-start | bytes 2752516
  4.1 43.8 %all-to-all-start = ((bf16[16,8,2,16,128]{4,3,2,1,0:T(8,128)(2,1)}), bf16[16,8,2,16,128]{4,3,2,1,0:T(8,128)(2,1)S(1)}, u32[]{:S(2)}, u32[]{:S(2)}) async-start(bf16[16,8,2,16,128]{4,3,2,1,0:T(8,128)(2,1)} %bitcast.4), calls=%async_computation | async-start | bytes 2097152 | tf_op jit(solution)/shard_map/all_to_all | solution.py:223
  17.6 40.7 %collective-permute-start.3 = (bf16[1344,1024]{1,0:T(8,128)(2,1)}, bf16[1344,1024]{1,0:T(8,128)(2,1)}, u32[]{:S(2)}, u32[]{:S(2)}) collective-permute-start(bf16[1344,1024]{1,0:T(8,128)(2,1)} %pad_maximum_fusion), channel_id=1, source_target_pairs={{0,1},{1,0},{2,3},{3,2},{4,5},{5,4},{6,7},{7,6},{8,9},{9,8},{10,11... | collective-permute-start | bytes 8257544 | tf_op jit(solution)/shard_map/ppermute | solution.py:270
  19.7 19.0 %collective-permute-start = (bf16[8,1152]{1,0:T(8,128)(2,1)S(1)}, bf16[8,1152]{1,0:T(8,128)(2,1)S(1)}, u32[]{:S(2)}, u32[]{:S(2)}) collective-permute-start(bf16[8,1152]{1,0:T(8,128)(2,1)S(1)} %fusion.7.asked_ref.refs_0_), channel_id=1, source_target_pairs={{0,16},{16,0},{32,48},{48,32},{1,17},{17,1},{33,49},{49,33},{2,18}... | collective-permute-start | bytes 55304 | tf_op jit(solution)/shard_map/ppermute | solution.py:206
  28.5 14.4 %collective-permute-start.1 = (bf16[8,1152]{1,0:T(8,128)(2,1)S(1)}, bf16[8,1152]{1,0:T(8,128)(2,1)S(1)}, u32[]{:S(2)}, u32[]{:S(2)}) collective-permute-start(bf16[8,1152]{1,0:T(8,128)(2,1)S(1)} %fusion.7.asked_ref.refs_0_), channel_id=1, source_target_pairs={{0,32},{16,48},{32,0},{48,16},{1,33},{17,49},{33,1},{49,17},{2,34}... | collective-permute-start | bytes 55304 | tf_op jit(solution)/shard_map/ppermute | solution.py:206
  36.8 11.2 %collective-permute-start.2 = (bf16[8,1152]{1,0:T(8,128)(2,1)S(1)}, bf16[8,1152]{1,0:T(8,128)(2,1)S(1)}, u32[]{:S(2)}, u32[]{:S(2)}) collective-permute-start(bf16[8,1152]{1,0:T(8,128)(2,1)S(1)} %fusion.7.asked_ref.refs_0_), channel_id=1, source_target_pairs={{0,48},{16,32},{32,16},{48,0},{1,49},{17,33},{33,17},{49,1},{2,50}... | collective-permute-start | bytes 55304 | tf_op jit(solution)/shard_map/ppermute | solution.py:206
  50.1 27.0 %all-to-all-start.1 = ((bf16[4,4,8,1152]{3,2,1,0:T(8,128)(2,1)}), bf16[4,4,8,1152]{3,2,1,0:T(8,128)(2,1)S(1)}, u32[]{:S(2)}, u32[]{:S(2)}) async-start(bf16[4,4,8,1152]{3,2,1,0:T(8,128)(2,1)} %shard_map.135), calls=%async_computation.1 | async-start | bytes 589824 | tf_op jit(solution)/shard_map/all_to_all | solution.py:252
  59.6 3.0 %copy-start.3 = (bf16[448,1024]{1,0:T(8,128)(2,1)S(1)}, bf16[448,1024]{1,0:T(8,128)(2,1)}, u32[]{:S(2)}) copy-start(bf16[448,1024]{1,0:T(8,128)(2,1)} %param.22) | copy-start | bytes 2752516
  62.6 22.0 %copy-start.8 = (bf16[1024]{0:T(1024)(128)(2,1)S(1)}, bf16[1024]{0:T(1024)(128)(2,1)}, u32[]{:S(2)}) copy-start(bf16[1024]{0:T(1024)(128)(2,1)} %param.19) | copy-start | bytes 6148
  78.2 20.4 %all-to-all-start.2 = ((bf16[8,32,1024]{2,1,0:T(8,128)(2,1)}), bf16[8,32,1024]{2,1,0:T(8,128)(2,1)S(1)}, u32[]{:S(2)}, u32[]{:S(2)}) async-start(bf16[8,32,1024]{2,1,0:T(8,128)(2,1)} %get-tuple-element.28), calls=%async_computation.2 | async-start | bytes 1048576 | tf_op jit(solution)/shard_map/all_to_all | solution.py:298
  98.9 2.5 %copy-start.5 = (bf16[896,1024]{1,0:T(8,128)(2,1)S(1)}, bf16[896,1024]{1,0:T(8,128)(2,1)}, u32[]{:S(2)}) copy-start(bf16[896,1024]{1,0:T(8,128)(2,1)} %slice.43) | copy-start | bytes 5505028
  117.6 11.5 %copy-start.4 = (bf16[896,1024]{1,0:T(8,128)(2,1)S(1)}, bf16[896,1024]{1,0:T(8,128)(2,1)}, u32[]{:S(2)}) copy-start(bf16[896,1024]{1,0:T(8,128)(2,1)} %pad_maximum_fusion.2) | copy-start | bytes 5505028
  151.1 18.7 %all-to-all-start.6 = ((bf16[4,8,1024]{2,1,0:T(8,128)(2,1)}), bf16[4,8,1024]{2,1,0:T(8,128)(2,1)S(1)}, u32[]{:S(2)}, u32[]{:S(2)}) async-start(bf16[4,8,1024]{2,1,0:T(8,128)(2,1)} %bitcast.13), calls=%async_computation.6 | async-start | bytes 131072 | tf_op jit(solution)/shard_map/all_to_all | solution.py:35
